TPU v7x, 32 devices: a whole 2x2x4 slice. The times are simulated.
32 devices in a mesh: row: 8 (over z, y), col: 4 (over x, core).
Axes of the slice: x: 2, y: 2, z: 4, core: 2. Of those that a mesh axis runs over, the one named last changes fastest.
Arguments:
- front: bfloat16 [8192, 8192], P('row', 'col'), may hold values from -0.125 to 0.125
- tile_mask: int32 [32, 32], P('row', 'col'), may hold values 0 or 1
- probes: bfloat16 [8192, 256], P(('col', 'row')), may hold values from -6 to 6
- coupling: float32 [8192, 256], P(('row', 'col')), may hold values from -0.375 to 0.375
Outputs:
- leaf_basis: float32 [8192, 256], P(('row', 'col'))
- upper_transfer: float32 [4, 8192, 256], P(None, ('row', 'col'))
Inputs may be any that keep to these rules, and one draw needn't show every extreme that they name: `tile_mask`: 1 where a tile of the front is present, 0 where it is absent.
All inputs are finite; a program needn't handle non-finite values. No bound on the sum of `tile_mask` on one device may be relied on, other than what follows from the above.
Results may differ from a plain program's by a relative error of at most 0.0003.
Values may be sent and summed in bfloat16 or wider, within the bound.
No kernel may reach another device: no remote copies, remote signals or barrier semaphores. Data moves between devices by JAX's collectives and lax.ppermute only.
A program may use at most 128 MiB of HBM per device.

v0:
```python
import functools

import jax
import jax.numpy as jnp
from jax import lax
from jax.experimental import pallas as pl
from jax.experimental.pallas import tpu as pltpu
from jax.sharding import PartitionSpec as P

F32 = jnp.float32
BF16 = jnp.bfloat16
SUB, LANE = 8, 128
BLOCK = LANE // 2
PANEL = 2


def split(x):
    high = x.astype(BF16)
    return high, (x - high.astype(F32)).astype(BF16)


def dot(left, right, dims):
    return lax.dot_general(
        left, right, (((dims[0],), (dims[1],)), ((), ())), preferred_element_type=F32
    )


def product(left, right, dims):
    total = None
    for i in reversed(range(len(left))):
        for j in reversed(range(len(right))):
            if i + j < 2:
                term = dot(left[i], right[j], dims)
                total = term if total is None else total + term
    return total


def lane_copy(x, lane):
    return jnp.take_along_axis(
        x, jnp.full(x.shape, lane, jnp.int32), axis=1, mode="promise_in_bounds"
    )


def row_copy(x, row):
    return jnp.broadcast_to(x[row : row + 1, :], x.shape)


def tree_sum(terms):
    while len(terms) > 1:
        pairs = [terms[i] + terms[i + 1] for i in range(0, len(terms) - 1, 2)]
        terms = pairs + terms[len(pairs) * 2 :]
    return terms[0]


def factor_block(packed, offset):
    count = BLOCK // SUB
    rows = [packed[SUB * k : SUB * (k + 1), :] for k in range(count)]
    sub = lax.broadcasted_iota(jnp.int32, (SUB, LANE), 0)
    out = []
    for first in range(0, count, PANEL):
        width, start = SUB * PANEL, offset + SUB * first
        held = rows[first : first + PANEL]
        cols = [[lane_copy(held[q], start + t) for q in range(PANEL)] for t in range(width)]
        done, scales = [None] * PANEL, [None] * PANEL
        for s in range(width):
            own, at = divmod(s, SUB)
            if at == 0:
                for t in range(s, width):
                    for q in range(own):
                        cols[t][q] = lane_copy(held[q], start + t)
            here = sub == at
            pivot = row_copy(cols[s][own], at)
            scale = 1.0 / pivot
            root = lax.rsqrt(pivot)
            bare = [jnp.where(here, 0.0, cols[s][q]) if q == own else cols[s][q] for q in range(PANEL)]
            factor = [x * scale for x in bare]
            row = row_copy(held[own], at)
            if at == 0:
                done[own], scales[own] = row * root, scale
            else:
                done[own] = jnp.where(here, row * root, done[own])
                scales[own] = jnp.where(here, scale, scales[own])
            for t in range(s + 1, width):
                across = row_copy(cols[s][t // SUB], t % SUB)
                for q in range(PANEL):
                    if q < t // SUB and own < t // SUB:
                        continue
                    if t == s + 1:
                        cols[t][q] = cols[t][q] - (bare[q] * across) * scale
                    else:
                        cols[t][q] = cols[t][q] - factor[q] * across
            for q in range(PANEL):
                held[q] = held[q] - factor[q] * row
        out += done
        if first + PANEL < count:
            held = [held[q] * scales[q] for q in range(PANEL)]
            solved = [row_copy(held[s // SUB], s % SUB) for s in range(width)]
            for k in range(first + PANEL, count):
                weight = [lane_copy(rows[k], start + s) for s in range(width)]
                rows[k] = rows[k] - tree_sum([weight[s] * solved[s] for s in range(width)])
    return jnp.concatenate(out, axis=0)


def four(x):
    high, low = split(x)
    return jnp.concatenate([high, high, low, low], axis=0)


def two_parts(x):
    high = x.astype(BF16).astype(F32)
    return high, x - high


def factor_all(gram, rights):
    count = gram.shape[0] // BLOCK
    lane = lax.broadcasted_iota(jnp.int32, (BLOCK, LANE), 1)
    sub = lax.broadcasted_iota(jnp.int32, (BLOCK, LANE), 0)
    blocks = [gram[BLOCK * i : BLOCK * (i + 1), :] for i in range(count)]
    rights = [[x[BLOCK * i : BLOCK * (i + 1), :] for i in range(count)] for x in rights]
    upper, solved = [], [[] for _ in rights]
    for i in range(count):
        first, offset = BLOCK * i // LANE * LANE, BLOCK * i % LANE
        other = BLOCK - offset
        mine = (lane >= offset) & (lane < offset + BLOCK)
        tile = slice(first, first + LANE)
        both = factor_block(
            jnp.where(mine, blocks[i][:, tile], jnp.where(lane - other == sub, 1.0, 0.0)), offset
        )
        high, low = two_parts(jnp.where(mine, 0.0, both))
        low_here = pltpu.roll(low, BLOCK, 1)
        left = jnp.concatenate([jnp.where(mine, low_here, high), high], axis=1).astype(BF16)
        right = [dot(left, four(x[i]), (1, 0)) for x in rights]
        for x, y in zip(solved, right):
            x.append(y)
        row = both
        if i + 1 < count:
            high_here = pltpu.roll(high, BLOCK, 1)
            across = jnp.concatenate([high_here, low_here, high_here], axis=1).astype(BF16)
            below = jnp.concatenate([blocks[j][:, tile] for j in range(i + 1, count)], axis=0)
            high, low = split(below)
            column = dot(
                jnp.concatenate([high, high, low], axis=1),
                jnp.concatenate([across, across], axis=0),
                (1, 1),
            )
            row = dot(left, four(blocks[i][:, first:]), (1, 0))
            high, low = two_parts(column)
            near = lax.broadcasted_iota(jnp.int32, column.shape, 1) < BLOCK
            column = jnp.concatenate(
                [jnp.where(near, high, low), jnp.where(near, high, 0.0)], axis=1
            ).astype(BF16)
            change = dot(column, four(row), (1, 0))
            for j in range(i + 1, count):
                at = BLOCK * (j - i - 1)
                new = blocks[j][:, first:] - change[at : at + BLOCK, :]
                if first:
                    new = jnp.concatenate([blocks[j][:, :first], new], axis=1)
                blocks[j] = new
            for x, y in zip(rights, right):
                change = dot(column, four(y), (1, 0))
                for j in range(i + 1, count):
                    at = BLOCK * (j - i - 1)
                    x[j] = x[j] - change[at : at + BLOCK, :]
        head = jnp.where(mine, both, row[:, :LANE])
        head = jnp.where(lane < offset + jnp.where(mine, sub, 0), 0.0, head)
        upper.append(head if row.shape[1] == LANE else jnp.concatenate([head, row[:, LANE:]], axis=1))
    return upper, [jnp.concatenate(x, axis=0) for x in solved]


def merge_math(own, other, level, want_state):
    own_s, own_w, own_p = own
    other_s, other_w, other_p = other
    if level > 1:
        factor = 2.0 ** (-(level - 1) / 2.0)
        own_s = own_s - factor * product(own_p, other_w, (1, 0))
        other_s = other_s - factor * product(other_p, own_w, (1, 0))
    size = own_s.shape[1]
    own_h, other_h = split(own_s), split(other_s)
    gram = product(own_h, own_h, (0, 0)) + product(other_h, other_h, (0, 0))
    trace = jnp.sum(own_s * own_s) + jnp.sum(other_s * other_s)
    shift = 0.001 * (trace / size + 1e-06)
    eye = lax.broadcasted_iota(jnp.int32, (size, size), 0) == lax.broadcasted_iota(
        jnp.int32, (size, size), 1
    )
    rights = [jnp.where(eye, 1.0, 0.0)]
    if want_state:
        rights.append(product(own_h, own_w, (0, 0)) + product(other_h, other_w, (0, 0)))
    upper, solved = factor_all(gram + jnp.where(eye, shift, 0.0), rights)
    q = product(own_h, split(solved[0]), (1, 1))
    return q, upper, solved[1] if want_state else None


def store_state(side, upper, w, state, send):
    half = w.shape[0] // 2
    part = half // 2
    share = half - part // 2
    state[0, :half] = w[:half]
    state[1, :half] = w[half:]
    top = jnp.concatenate(upper[:2], axis=0)
    state[0, half:] = top[:share]
    state[1, half : half + half - share] = top[share:]
    state[1, half + half - share :] = jnp.concatenate(upper[2:], axis=1)
    send[...] = state[side[0]]


def load_state(first, second):
    half = first.shape[1] // 2
    part = half // 2
    share = half - part // 2
    w = jnp.concatenate([first[:half], second[:half]], axis=0)
    split_at = half + half - share
    top = jnp.concatenate([first[half:], second[half:split_at]], axis=0)
    last = second[split_at:]
    corner = jnp.concatenate([last[:, :half], last[:, half:]], axis=0)
    bottom = jnp.concatenate([jnp.zeros((half, half), F32), corner], axis=1)
    return jnp.concatenate([top, bottom], axis=0), w


def first_kernel(
    side, own_a, own_b, other_a, other_b, own_w, other_w, q_out, state, send
):
    q, upper, w = merge_math(
        (own_a[...] + own_b[...], (own_w[...],), None),
        (other_a[...] + other_b[...], (other_w[...],), None),
        1,
        True,
    )
    store_state(side, upper, w, state, send)
    q_out[...] = q


def upper_kernel(level, is_last, has_buffer, side, own, own_p, near, far, other_p, *refs):
    refs = list(refs)
    if has_buffer:
        refs.pop(0)
    q_all = refs.pop(0)
    outs = [] if is_last else [refs.pop(0), refs.pop(0)]
    q_here, done = refs
    is_first = side[0] == 0
    own_s, own_w = load_state(own[0], own[1])
    near, far = near[...], far[...]
    other_s, other_w = load_state(jnp.where(is_first, near, far), jnp.where(is_first, far, near))
    q, upper, w = merge_math(
        (own_s, split(own_w), split(own_p[...])),
        (other_s, split(other_w), split(other_p[...])),
        level,
        not is_last,
    )
    q_here[...] = q
    copy = pltpu.make_async_copy(q_here, q_all.at[level - 2], done)
    copy.start()
    if not is_last:
        store_state(side, upper, w, *outs)
    copy.wait()


VMEM = pl.BlockSpec(memory_space=pltpu.VMEM)
SMEM = pl.BlockSpec(memory_space=pltpu.SMEM)
ANY = pl.BlockSpec(memory_space=pl.ANY)


def state_shapes(size):
    rows = size // 2 + 3 * size // 8
    return [
        jax.ShapeDtypeStruct((2, rows, size), F32),
        jax.ShapeDtypeStruct((rows, size), F32),
    ]


def first_merge(side, arrays):
    rows, size = arrays[0].shape
    return pl.pallas_call(
        first_kernel,
        out_shape=[jax.ShapeDtypeStruct((rows, size), F32)] + state_shapes(size),
        in_specs=[SMEM] + [VMEM] * len(arrays),
        out_specs=[VMEM] * 3,
        name="first_merge",
    )(side, *arrays)


def upper_merge(level, levels, side, arrays, buffer):
    size = arrays[1].shape[1]
    is_last = level == levels
    extra = [] if buffer is None else [buffer]
    out_shape = [jax.ShapeDtypeStruct((levels - 1, size, size), F32)]
    out_shape += [] if is_last else state_shapes(size)
    return pl.pallas_call(
        functools.partial(upper_kernel, level, is_last, bool(extra)),
        out_shape=out_shape,
        in_specs=[SMEM] + [VMEM] * len(arrays) + [ANY] * len(extra),
        out_specs=[ANY] + [VMEM] * (len(out_shape) - 1),
        scratch_shapes=[pltpu.VMEM((size, size), F32), pltpu.SemaphoreType.DMA(())],
        input_output_aliases={1 + len(arrays): 0} if extra else {},
    )(side, *arrays, *extra)


def sample_kernel(keys, place, mask, front, *refs):
    count = len(keys)
    chunks, (keep, send, tiles, arrived) = refs[:count], refs[count:]
    leaf = chunks[0].shape[0]
    slots = 2 * keep.shape[0]
    order = [*range(1, slots, 2), *range(0, slots, 2)]
    present, copies = {}, {}
    for slot in order:
        tile_row = place[1] ^ slot
        for j, key in enumerate(keys):
            chunk = place[0] ^ key
            row_tile = place[0] * slots + tile_row
            col_tile = place[1] * count + chunk
            present[slot, j] = (mask[tile_row, chunk] != 0) & (row_tile // 2 != col_tile // 2)
            copies[slot, j] = pltpu.make_async_copy(
                front.at[
                    pl.ds(pl.multiple_of(tile_row * leaf, leaf), leaf),
                    pl.ds(pl.multiple_of(chunk * leaf, leaf), leaf),
                ],
                tiles.at[slot, j],
                arrived.at[slot, j],
            )

            @pl.when(present[slot, j])
            def _():
                copies[slot, j].start()

    for slot in order:
        for j in range(count):

            @pl.when(present[slot, j])
            def _():
                copies[slot, j].wait()

        total = None
        for j in range(count):
            tile = jnp.where(present[slot, j], tiles[slot, j], jnp.zeros((), BF16))
            term = dot(tile, chunks[j][...], (1, 0))
            total = term if total is None else total + term
        out = send if slot % 2 else keep
        out[slot // 2] = total


def all_samples(front, tile_mask, place, chunks, keys):
    leaf, size = chunks[0].shape
    slots = front.shape[0] // leaf
    return pl.pallas_call(
        functools.partial(sample_kernel, keys),
        out_shape=[jax.ShapeDtypeStruct((slots // 2, leaf, size), F32)] * 2,
        in_specs=[SMEM, SMEM, ANY] + [VMEM] * len(keys),
        out_specs=[VMEM] * 2,
        scratch_shapes=[
            pltpu.VMEM((slots, len(keys), leaf, leaf), BF16),
            pltpu.SemaphoreType.DMA((slots, len(keys))),
        ],
        name="samples",
    )(place, tile_mask, front, *chunks)


def swap(x, axis, bit):
    return lax.ppermute(x, axis, [(i, i ^ (1 << bit)) for i in range(lax.axis_size(axis))])


def step(front, tile_mask, probes, coupling):
    col_count, row_count = lax.axis_size("col"), lax.axis_size("row")
    row_index, col_index = lax.axis_index("row"), lax.axis_index("col")
    col_levels, row_levels = col_count.bit_length() - 1, row_count.bit_length() - 1
    levels = col_levels + row_levels
    place = jnp.stack([row_index, col_index]).astype(jnp.int32)
    side = (col_index & 1).astype(jnp.int32)[None]
    bits = [("col", b) for b in range(col_levels)] + [("row", b) for b in range(row_levels)]

    chunks = {0: probes}
    chunks[1] = swap(probes, "row", 0)
    for bit in range(row_levels - 1, 0, -1):
        for key in list(chunks):
            new = key | 1 << bit
            if key == 1:
                chunks[new] = swap(chunks[new ^ 1], "row", 0)
            else:
                chunks[new] = swap(chunks[key], "row", bit)

    pairs = [
        ((b % row_count) * col_count + b // row_count, b) for b in range(row_count * col_count)
    ]
    own_w = lax.ppermute(probes, ("row", "col"), pairs)
    other_w = swap(own_w, "col", 0)

    own_p, other_p, total_p = {}, {}, coupling
    for level, (axis, bit) in enumerate(bits, start=1):
        own_p[level], other_p[level] = total_p, swap(total_p, axis, bit)
        if level < levels:
            total_p = own_p[level] + other_p[level]

    order = list(chunks)
    keep, send = all_samples(front, tile_mask, place, [chunks[k] for k in order], order)
    got = swap(send, "col", 0)
    slots = {2 * k: (keep[k], got[k]) for k in range(col_count // 2)}
    for bit in range(1, col_levels):
        far = 1 << bit
        left = list(range(0, col_count, 2 * far))
        moved = swap(jnp.stack([slots[k + far][0] + slots[k + far][1] for k in left]), "col", bit)
        slots = {k: (slots[k][0] + slots[k][1], moved[i]) for i, k in enumerate(left)}
    own_a, own_b = slots[0]
    other_a = swap(own_a, "col", 0)
    other_b = swap(own_b, "col", 0)

    leaf_basis, state, send = first_merge(side, (own_a, own_b, other_a, other_b, own_w, other_w))
    buffer = None
    for level, (axis, bit) in list(enumerate(bits, start=1))[1:]:
        near = swap(send, axis, bit)
        far = swap(near, "col", 0)
        buffer, *rest = upper_merge(
            level, levels, side, (state, own_p[level], near, far, other_p[level]), buffer
        )
        if rest:
            state, send = rest
    return (leaf_basis, buffer)


def solution(mesh):
    in_specs = (P("row", "col"), P("row", "col"), P(("col", "row"), None), P(("row", "col"), None))
    out_specs = (P(("row", "col"), None), P(None, ("row", "col"), None))
    return jax.shard_map(step, mesh=mesh, in_specs=in_specs, out_specs=out_specs, check_vma=False)
```

profile of v0, /device:TPU:0, one launch (start us, length us, event | category | flops | bytes accessed | tf_op | source)
XLA Modules:
  0.0 164.3 jit_solution(7522766342725448037)
XLA Ops:
  0.7 4.1 %collective-permute-start.1 = (bf16[256,256]{1,0:T(8,128)(2,1)}, bf16[256,256]{1,0:T(8,128)(2,1)S(1)}, u32[]{:S(2)}, u32[]{:S(2)}) collective-permute-start(bf16[256,256]{1,0:T(8,128)(2,1)} %refs_0_.1), channel_id=1, source_target_pairs={{0,16},{4,20},{8,24},{12,28},{16,0},{20,4},{24,8},{28,12},{1,17},{... | collective-permute-start | bytes 393224 | tf_op jit(solution)/shard_map/ppermute | solution.py:357
  4.8 1.6 collective-permute-start.3
  6.4 5.0 %collective-permute-done.1.refs_2_ = bf16[256,256]{1,0:T(8,128)(2,1)S(1)} collective-permute-done((bf16[256,256]{1,0:T(8,128)(2,1)}, bf16[256,256]{1,0:T(8,128)(2,1)S(1)}, u32[]{:S(2)}, u32[]{:S(2)}) %collective-permute-start.1) | collective-permute-done | bytes 131104 | tf_op jit(solution)/shard_map/ppermute | solution.py:357
  11.4 1.6 collective-permute-start.2
  13.4 0.7 collective-permute-start.5
  14.2 1.5 collective-permute-start.4
  15.7 2.1 %collective-permute-done.2.refs_3_ = bf16[256,256]{1,0:T(8,128)(2,1)S(1)} collective-permute-done((bf16[256,256]{1,0:T(8,128)(2,1)S(1)}, bf16[256,256]{1,0:T(8,128)(2,1)S(1)}, u32[]{:S(2)}, u32[]{:S(2)}) %collective-permute-start.2) | collective-permute-done | bytes 131104 | tf_op jit(solution)/shard_map/ppermute | solution.py:357
  17.8 0.7 collective-permute-start.6
  18.5 0.6 pad_add_fusion.place
  19.1 0.8 collective-permute-done.refs_1_
  19.9 1.4 collective-permute-done.4.refs_5_
  21.3 1.4 collective-permute-done.6.refs_7_
  22.8 0.6 copy-done.29
  23.4 6.1 %samples.1 = (f32[2,256,256]{2,1,0:T(8,128)}, f32[2,256,256]{2,1,0:T(8,128)}) custom-call(s32[2]{0:T(128)} %pad_add_fusion.place, s32[4,8]{1,0:T(4,128)} %mask.1, bf16[1024,2048]{1,0:T(8,128)(2,1)} %front.1, bf16[256,256]{1,0:T(8,128)(2,1)} %refs_0_.1, bf16[256,256]{1,0:T(8,128)(2,1)} %copy-done.25, bf16[256,256]{1,0:T(8,128)(2,1)} %copy-done.22, ...), custom_call_target="tpu_custom_call" | custom-call | tf_op jit(solution)/shard_map/samples/pallas_call | solution.py:343
  29.6 2.1 %collective-permute-done.7 = f32[2,256,256]{2,1,0:T(8,128)S(1)} collective-permute-done((f32[2,256,256]{2,1,0:T(8,128)}, f32[2,256,256]{2,1,0:T(8,128)S(1)}, u32[]{:S(2)}, u32[]{:S(2)}) %collective-permute-start.7) | collective-permute-done | bytes 524320 | tf_op jit(solution)/shard_map/ppermute | solution.py:357
  31.7 1.1 slice_add_fusion
  32.9 0.8 collective-permute-start.8
  33.6 0.8 collective-permute-start.11
  34.5 3.4 %collective-permute-start.9 = (f32[256,256]{1,0:T(8,128)S(1)}, f32[256,256]{1,0:T(8,128)S(1)}, u32[]{:S(2)}, u32[]{:S(2)}) collective-permute-start(f32[256,256]{1,0:T(8,128)S(1)} %get-tuple-element.31.own_a), channel_id=1, source_target_pairs={{0,1},{1,0},{2,3},{3,2},{4,5},{5,4},{6,7},{7,6},{8,9},{9,8},{10,11... | collective-permute-start | bytes 786440 | tf_op jit(solution)/shard_map/ppermute | solution.py:357
  37.9 3.4 %collective-permute-done.8 = f32[1,256,256]{2,1,0:T(8,128)S(1)} collective-permute-done((f32[1,256,256]{2,1,0:T(8,128)S(1)}, f32[1,256,256]{2,1,0:T(8,128)S(1)}, u32[]{:S(2)}, u32[]{:S(2)}) %collective-permute-start.8) | collective-permute-done | bytes 262176 | tf_op jit(solution)/shard_map/ppermute | solution.py:357
  41.3 0.5 collective-permute-start.12
  41.9 1.1 collective-permute-done.12.other_w
  43.0 0.6 copy-done.30
  43.8 9.3 %first_merge.1 = (f32[256,256]{1,0:T(8,128)}, f32[2,224,256]{2,1,0:T(8,128)}, f32[224,256]{1,0:T(8,128)}) custom-call(s32[1]{0:T(128)} %bitcast.side, f32[256,256]{1,0:T(8,128)} %copy-done.3, f32[256,256]{1,0:T(8,128)} %bitcast.7, f32[256,256]{1,0:T(8,128)} %copy-done.10, f32[256,256]{1,0:T(8,128)} %copy-done.11, bf16[256,256]{1,0:T(8,128)(2,1)} %copy-done.28, ...), custom_call_target="tpu_custom_call" | custom-call | tf_op jit(solution)/shard_map/first_merge/pallas_call | solution.py:272
  53.1 2.1 %collective-permute-start.14 = (f32[224,256]{1,0:T(8,128)}, f32[224,256]{1,0:T(8,128)S(1)}, u32[]{:S(2)}, u32[]{:S(2)}) collective-permute-start(f32[224,256]{1,0:T(8,128)} %get-tuple-element.20), channel_id=1, source_target_pairs={{0,2},{1,3},{2,0},{3,1},{4,6},{5,7},{6,4},{7,5},{8,10},{9,11},{10,... | collective-permute-start | bytes 688136 | tf_op jit(solution)/shard_map/ppermute | solution.py:357
  55.4 6.5 %collective-permute-done.14.near = f32[224,256]{1,0:T(8,128)S(1)} collective-permute-done((f32[224,256]{1,0:T(8,128)}, f32[224,256]{1,0:T(8,128)S(1)}, u32[]{:S(2)}, u32[]{:S(2)}) %collective-permute-start.14) | collective-permute-done | bytes 229408 | tf_op jit(solution)/shard_map/ppermute | solution.py:357
  61.9 5.1 %collective-permute-done.16.other_p = f32[256,256]{1,0:T(8,128)S(1)} collective-permute-done((f32[256,256]{1,0:T(8,128)S(1)}, f32[256,256]{1,0:T(8,128)S(1)}, u32[]{:S(2)}, u32[]{:S(2)}) %collective-permute-start.16) | collective-permute-done | bytes 262176 | tf_op jit(solution)/shard_map/ppermute | solution.py:357
  67.0 0.7 copy-done.4
  67.8 10.6 %shard_map.59 = (f32[4,256,256]{2,1,0:T(8,128)}, f32[2,224,256]{2,1,0:T(8,128)}, f32[224,256]{1,0:T(8,128)}) custom-call(s32[1]{0:T(128)} %bitcast.side, f32[2,224,256]{2,1,0:T(8,128)} %get-tuple-element.19.own, f32[256,256]{1,0:T(8,128)} %copy-done, f32[224,256]{1,0:T(8,128)} %copy-done.13, f32[224,256]{1,0:T(8,128)} %copy-done.20, f32[256,256]{1,0:T(8,128)} %copy-done.4), custom_call_target="tpu_custom_call" | custom-call | tf_op jit(solution)/shard_map/pallas_call | solution.py:287
  78.5 5.9 %collective-permute-start.17 = (f32[224,256]{1,0:T(8,128)}, f32[224,256]{1,0:T(8,128)S(1)}, u32[]{:S(2)}, u32[]{:S(2)}) collective-permute-start(f32[224,256]{1,0:T(8,128)} %get-tuple-element.22), channel_id=1, source_target_pairs={{0,4},{4,0},{8,12},{12,8},{16,20},{20,16},{24,28},{28,24},{1,5},{5... | collective-permute-start | bytes 688136 | tf_op jit(solution)/shard_map/ppermute | solution.py:357
  84.4 1.1 add.25.own_p
  85.5 5.5 %collective-permute-done.17.near = f32[224,256]{1,0:T(8,128)S(1)} collective-permute-done((f32[224,256]{1,0:T(8,128)}, f32[224,256]{1,0:T(8,128)S(1)}, u32[]{:S(2)}, u32[]{:S(2)}) %collective-permute-start.17) | collective-permute-done | bytes 229408 | tf_op jit(solution)/shard_map/ppermute | solution.py:357
  91.1 4.2 %collective-permute-done.19.other_p = f32[256,256]{1,0:T(8,128)S(1)} collective-permute-done((f32[256,256]{1,0:T(8,128)S(1)}, f32[256,256]{1,0:T(8,128)S(1)}, u32[]{:S(2)}, u32[]{:S(2)}) %collective-permute-start.19) | collective-permute-done | bytes 262176 | tf_op jit(solution)/shard_map/ppermute | solution.py:357
  95.3 0.7 copy-done.5
  96.1 10.9 %shard_map.60 = (f32[4,256,256]{2,1,0:T(8,128)}, f32[2,224,256]{2,1,0:T(8,128)}, f32[224,256]{1,0:T(8,128)}) custom-call(s32[1]{0:T(128)} %bitcast.side, f32[2,224,256]{2,1,0:T(8,128)} %get-tuple-element.21.own, f32[256,256]{1,0:T(8,128)} %copy-done.1, f32[224,256]{1,0:T(8,128)} %copy-done.14, ...), custom_call_target="tpu_custom_call", output_to_operand_aliasing={{0}: (6, {})} | custom-call | tf_op jit(solution)/shard_map/pallas_call | solution.py:287
  107.1 1.1 add.26.own_p
  108.1 2.1 %collective-permute-start.22 = (f32[256,256]{1,0:T(8,128)S(1)}, f32[256,256]{1,0:T(8,128)S(1)}, u32[]{:S(2)}, u32[]{:S(2)}) collective-permute-start(f32[256,256]{1,0:T(8,128)S(1)} %add.26.own_p), channel_id=1, source_target_pairs={{0,8},{4,12},{8,0},{12,4},{16,24},{20,28},{24,16},{28,20},{1,9},{5... | collective-permute-start | bytes 786440 | tf_op jit(solution)/shard_map/ppermute | solution.py:357
  110.2 5.5 %collective-permute-done.20.near = f32[224,256]{1,0:T(8,128)S(1)} collective-permute-done((f32[224,256]{1,0:T(8,128)}, f32[224,256]{1,0:T(8,128)S(1)}, u32[]{:S(2)}, u32[]{:S(2)}) %collective-permute-start.20) | collective-permute-done | bytes 229408 | tf_op jit(solution)/shard_map/ppermute | solution.py:357
  115.7 3.4 %collective-permute-done.22.other_p = f32[256,256]{1,0:T(8,128)S(1)} collective-permute-done((f32[256,256]{1,0:T(8,128)S(1)}, f32[256,256]{1,0:T(8,128)S(1)}, u32[]{:S(2)}, u32[]{:S(2)}) %collective-permute-start.22) | collective-permute-done | bytes 262176 | tf_op jit(solution)/shard_map/ppermute | solution.py:357
  119.1 0.7 copy-done.6
  119.9 10.6 %shard_map.61 = (f32[4,256,256]{2,1,0:T(8,128)}, f32[2,224,256]{2,1,0:T(8,128)}, f32[224,256]{1,0:T(8,128)}) custom-call(s32[1]{0:T(128)} %bitcast.side, f32[2,224,256]{2,1,0:T(8,128)} %get-tuple-element.24.own, f32[256,256]{1,0:T(8,128)} %copy-done.2, f32[224,256]{1,0:T(8,128)} %copy-done.15, ...), custom_call_target="tpu_custom_call", output_to_operand_aliasing={{0}: (6, {})} | custom-call | tf_op jit(solution)/shard_map/pallas_call | solution.py:287
  130.6 1.2 collective-permute-start.23
  131.8 1.1 add.27.own_p
  132.9 1.9 %collective-permute-start.25 = (f32[256,256]{1,0:T(8,128)S(1)}, f32[256,256]{1,0:T(8,128)S(1)}, u32[]{:S(2)}, u32[]{:S(2)}) collective-permute-start(f32[256,256]{1,0:T(8,128)S(1)} %add.27.own_p), channel_id=1, source_target_pairs={{0,16},{4,20},{8,24},{12,28},{16,0},{20,4},{24,8},{28,12},{1,17},{... | collective-permute-start | bytes 786440 | tf_op jit(solution)/shard_map/ppermute | solution.py:357
  134.7 13.3 %collective-permute-done.23.near = f32[224,256]{1,0:T(8,128)S(1)} collective-permute-done((f32[224,256]{1,0:T(8,128)}, f32[224,256]{1,0:T(8,128)S(1)}, u32[]{:S(2)}, u32[]{:S(2)}) %collective-permute-start.23) | collective-permute-done | bytes 229408 | tf_op jit(solution)/shard_map/ppermute | solution.py:357
  148.0 5.2 %collective-permute-done.25.other_p = f32[256,256]{1,0:T(8,128)S(1)} collective-permute-done((f32[256,256]{1,0:T(8,128)S(1)}, f32[256,256]{1,0:T(8,128)S(1)}, u32[]{:S(2)}, u32[]{:S(2)}) %collective-permute-start.25) | collective-permute-done | bytes 262176 | tf_op jit(solution)/shard_map/ppermute | solution.py:357
  153.3 0.7 copy-done.12
  154.1 10.1 %shard_map.62 = f32[4,256,256]{2,1,0:T(8,128)} custom-call(s32[1]{0:T(128)} %bitcast.side, f32[2,224,256]{2,1,0:T(8,128)} %get-tuple-element.27.own, f32[256,256]{1,0:T(8,128)} %copy-done.7, f32[224,256]{1,0:T(8,128)} %copy-done.16, f32[224,256]{1,0:T(8,128)} %copy-done.19, f32[256,256]{1,0:T(8,128)} %copy-done.12, ...), custom_call_target="tpu_custom_call", output_to_operand_aliasing={{}: (6, {})} | custom-call | tf_op jit(solution)/shard_map/pallas_call | solution.py:287
  (78 shorter events, 1.7 us)
Async XLA Ops:
  0.6 33.0 %copy-start.21 = (bf16[256,256]{1,0:T(8,128)(2,1)S(1)}, bf16[256,256]{1,0:T(8,128)(2,1)}, u32[]{:S(2)}) copy-start(bf16[256,256]{1,0:T(8,128)(2,1)} %refs_0_.1) | copy-start | bytes 393220
  0.6 41.1 %copy-start.8 = (f32[256,256]{1,0:T(8,128)S(1)}, f32[256,256]{1,0:T(8,128)}, u32[]{:S(2)}) copy-start(f32[256,256]{1,0:T(8,128)} %param.7) | copy-start | bytes 786436
  0.7 10.8 %collective-permute-start.1 = (bf16[256,256]{1,0:T(8,128)(2,1)}, bf16[256,256]{1,0:T(8,128)(2,1)S(1)}, u32[]{:S(2)}, u32[]{:S(2)}) collective-permute-start(bf16[256,256]{1,0:T(8,128)(2,1)} %refs_0_.1), channel_id=1, source_target_pairs={{0,16},{4,20},{8,24},{12,28},{16,0},{20,4},{24,8},{28,12},{1,17},{... | collective-permute-start | bytes 393224 | tf_op jit(solution)/shard_map/ppermute | solution.py:357
  4.8 9.4 %collective-permute-start.3 = (bf16[256,256]{1,0:T(8,128)(2,1)}, bf16[256,256]{1,0:T(8,128)(2,1)S(1)}, u32[]{:S(2)}, u32[]{:S(2)}) collective-permute-start(bf16[256,256]{1,0:T(8,128)(2,1)} %refs_0_.1), channel_id=1, source_target_pairs={{0,8},{4,12},{8,0},{12,4},{16,24},{20,28},{24,16},{28,20},{1,9},{5... | collective-permute-start | bytes 393224 | tf_op jit(solution)/shard_map/ppermute | solution.py:357
  11.4 11.3 %copy-start.22 = (bf16[256,256]{1,0:T(8,128)(2,1)}, bf16[256,256]{1,0:T(8,128)(2,1)S(1)}, u32[]{:S(2)}) copy-start(bf16[256,256]{1,0:T(8,128)(2,1)S(1)} %collective-permute-done.1.refs_2_) | copy-start | bytes 393220
  11.4 6.4 %collective-permute-start.2 = (bf16[256,256]{1,0:T(8,128)(2,1)S(1)}, bf16[256,256]{1,0:T(8,128)(2,1)S(1)}, u32[]{:S(2)}, u32[]{:S(2)}) collective-permute-start(bf16[256,256]{1,0:T(8,128)(2,1)S(1)} %collective-permute-done.1.refs_2_), channel_id=1, source_target_pairs={{0,4},{4,0},{8,12},{12,8},{16,20},{20,16},{24,28},{28,24},{1,5},{5... | collective-permute-start | bytes 393224 | tf_op jit(solution)/shard_map/ppermute | solution.py:357
  13.0 7.0 %collective-permute-start = (bf16[256,256]{1,0:T(8,128)(2,1)}, bf16[256,256]{1,0:T(8,128)(2,1)S(1)}, u32[]{:S(2)}, u32[]{:S(2)}) collective-permute-start(bf16[256,256]{1,0:T(8,128)(2,1)} %refs_0_.1), channel_id=1, source_target_pairs={{0,4},{4,0},{8,12},{12,8},{16,20},{20,16},{24,28},{28,24},{1,5},{5... | collective-permute-start | bytes 393224 | tf_op jit(solution)/shard_map/ppermute | solution.py:357
  13.4 7.9 %collective-permute-start.5 = (bf16[256,256]{1,0:T(8,128)(2,1)S(1)}, bf16[256,256]{1,0:T(8,128)(2,1)S(1)}, u32[]{:S(2)}, u32[]{:S(2)}) collective-permute-start(bf16[256,256]{1,0:T(8,128)(2,1)S(1)} %collective-permute-done.1.refs_2_), channel_id=1, source_target_pairs={{0,8},{4,12},{8,0},{12,4},{16,24},{20,28},{24,16},{28,20},{1,9},{5... | collective-permute-start | bytes 393224 | tf_op jit(solution)/shard_map/ppermute | solution.py:357
  14.2 8.6 %copy-start.23 = (bf16[256,256]{1,0:T(8,128)(2,1)}, bf16[256,256]{1,0:T(8,128)(2,1)S(1)}, u32[]{:S(2)}) copy-start(bf16[256,256]{1,0:T(8,128)(2,1)S(1)} %collective-permute-done.3.refs_4_) | copy-start | bytes 393220
  14.2 7.2 %collective-permute-start.4 = (bf16[256,256]{1,0:T(8,128)(2,1)S(1)}, bf16[256,256]{1,0:T(8,128)(2,1)S(1)}, u32[]{:S(2)}, u32[]{:S(2)}) collective-permute-start(bf16[256,256]{1,0:T(8,128)(2,1)S(1)} %collective-permute-done.3.refs_4_), channel_id=1, source_target_pairs={{0,4},{4,0},{8,12},{12,8},{16,20},{20,16},{24,28},{28,24},{1,5},{5... | collective-permute-start | bytes 393224 | tf_op jit(solution)/shard_map/ppermute | solution.py:357
  17.8 5.0 %copy-start.24 = (bf16[256,256]{1,0:T(8,128)(2,1)}, bf16[256,256]{1,0:T(8,128)(2,1)S(1)}, u32[]{:S(2)}) copy-start(bf16[256,256]{1,0:T(8,128)(2,1)S(1)} %collective-permute-done.2.refs_3_) | copy-start | bytes 393220
  17.8 5.0 %collective-permute-start.6 = (bf16[256,256]{1,0:T(8,128)(2,1)S(1)}, bf16[256,256]{1,0:T(8,128)(2,1)S(1)}, u32[]{:S(2)}, u32[]{:S(2)}) collective-permute-start(bf16[256,256]{1,0:T(8,128)(2,1)S(1)} %collective-permute-done.2.refs_3_), channel_id=1, source_target_pairs={{0,8},{4,12},{8,0},{12,4},{16,24},{20,28},{24,16},{28,20},{1,9},{5... | collective-permute-start | bytes 393224 | tf_op jit(solution)/shard_map/ppermute | solution.py:357
  19.9 2.8 %copy-start.25 = (bf16[256,256]{1,0:T(8,128)(2,1)}, bf16[256,256]{1,0:T(8,128)(2,1)S(1)}, u32[]{:S(2)}) copy-start(bf16[256,256]{1,0:T(8,128)(2,1)S(1)} %collective-permute-done.refs_1_) | copy-start | bytes 393220
  21.3 1.4 copy-start.27
  21.3 1.4 copy-start.26
  29.6 2.2 %collective-permute-start.7 = (f32[2,256,256]{2,1,0:T(8,128)}, f32[2,256,256]{2,1,0:T(8,128)S(1)}, u32[]{:S(2)}, u32[]{:S(2)}) collective-permute-start(f32[2,256,256]{2,1,0:T(8,128)} %get-tuple-element.17), channel_id=1, source_target_pairs={{0,1},{1,0},{2,3},{3,2},{4,5},{5,4},{6,7},{7,6},{8,9},{9,8},{10,11... | collective-permute-start | bytes 1572872 | tf_op jit(solution)/shard_map/ppermute | solution.py:357
  32.8 10.2 %copy-start.3 = (f32[256,256]{1,0:T(8,128)}, f32[256,256]{1,0:T(8,128)S(1)}, u32[]{:S(2)}) copy-start(f32[256,256]{1,0:T(8,128)S(1)} %get-tuple-element.31.own_a) | copy-start | bytes 786436
  32.9 8.4 %collective-permute-start.8 = (f32[1,256,256]{2,1,0:T(8,128)S(1)}, f32[1,256,256]{2,1,0:T(8,128)S(1)}, u32[]{:S(2)}, u32[]{:S(2)}) collective-permute-start(f32[1,256,256]{2,1,0:T(8,128)S(1)} %get-tuple-element.30), channel_id=1, source_target_pairs={{0,2},{1,3},{2,0},{3,1},{4,6},{5,7},{6,4},{7,5},{8,10},{9,11},{10,... | collective-permute-start | bytes 786440 | tf_op jit(solution)/shard_map/ppermute | solution.py:357
  33.6 7.6 %collective-permute-start.11 = (bf16[256,256]{1,0:T(8,128)(2,1)S(1)}, bf16[256,256]{1,0:T(8,128)(2,1)S(1)}, u32[]{:S(2)}, u32[]{:S(2)}) collective-permute-start(bf16[256,256]{1,0:T(8,128)(2,1)S(1)} %copy-done.21), channel_id=1, source_target_pairs={{0,0},{4,1},{8,2},{12,3},{16,4},{20,5},{24,6},{28,7},{1,8},{5,9},{... | collective-permute-start | bytes 393224 | tf_op jit(solution)/shard_map/ppermute | solution.py:382
  34.5 8.5 %collective-permute-start.9 = (f32[256,256]{1,0:T(8,128)S(1)}, f32[256,256]{1,0:T(8,128)S(1)}, u32[]{:S(2)}, u32[]{:S(2)}) collective-permute-start(f32[256,256]{1,0:T(8,128)S(1)} %get-tuple-element.31.own_a), channel_id=1, source_target_pairs={{0,1},{1,0},{2,3},{3,2},{4,5},{5,4},{6,7},{7,6},{8,9},{9,8},{10,11... | collective-permute-start | bytes 786440 | tf_op jit(solution)/shard_map/ppermute | solution.py:357
  41.3 1.8 %copy-start.9 = (f32[1,256,256]{2,1,0:T(8,128)}, f32[1,256,256]{2,1,0:T(8,128)S(1)}, u32[]{:S(2)}) copy-start(f32[1,256,256]{2,1,0:T(8,128)S(1)} %collective-permute-done.8) | copy-start | bytes 786436
  41.3 1.7 %collective-permute-start.10 = (f32[256,256]{1,0:T(8,128)S(1)}, f32[256,256]{1,0:T(8,128)S(1)}, u32[]{:S(2)}, u32[]{:S(2)}) collective-permute-start(f32[256,256]{1,0:T(8,128)S(1)} %bitcast.6), channel_id=1, source_target_pairs={{0,1},{1,0},{2,3},{3,2},{4,5},{5,4},{6,7},{7,6},{8,9},{9,8},{10,11... | collective-permute-start | bytes 786440 | tf_op jit(solution)/shard_map/ppermute | solution.py:357
  41.3 1.8 %copy-start.28 = (bf16[256,256]{1,0:T(8,128)(2,1)}, bf16[256,256]{1,0:T(8,128)(2,1)S(1)}, u32[]{:S(2)}) copy-start(bf16[256,256]{1,0:T(8,128)(2,1)S(1)} %collective-permute-done.11.own_w) | copy-start | bytes 393220
  41.3 1.7 %collective-permute-start.12 = (bf16[256,256]{1,0:T(8,128)(2,1)S(1)}, bf16[256,256]{1,0:T(8,128)(2,1)S(1)}, u32[]{:S(2)}, u32[]{:S(2)}) collective-permute-start(bf16[256,256]{1,0:T(8,128)(2,1)S(1)} %collective-permute-done.11.own_w), channel_id=1, source_target_pairs={{0,1},{1,0},{2,3},{3,2},{4,5},{5,4},{6,7},{7,6},{8,9},{9,8},{10,11... | collective-permute-start | bytes 393224 | tf_op jit(solution)/shard_map/ppermute | solution.py:357
  41.8 13.5 %collective-permute-start.13 = (f32[256,256]{1,0:T(8,128)S(1)}, f32[256,256]{1,0:T(8,128)S(1)}, u32[]{:S(2)}, u32[]{:S(2)}) collective-permute-start(f32[256,256]{1,0:T(8,128)S(1)} %copy-done.8), channel_id=1, source_target_pairs={{0,1},{1,0},{2,3},{3,2},{4,5},{5,4},{6,7},{7,6},{8,9},{9,8},{10,11... | collective-permute-start | bytes 786440 | tf_op jit(solution)/shard_map/ppermute | solution.py:357
  43.0 0.8 copy-start.11
  53.1 8.8 %collective-permute-start.14 = (f32[224,256]{1,0:T(8,128)}, f32[224,256]{1,0:T(8,128)S(1)}, u32[]{:S(2)}, u32[]{:S(2)}) collective-permute-start(f32[224,256]{1,0:T(8,128)} %get-tuple-element.20), channel_id=1, source_target_pairs={{0,2},{1,3},{2,0},{3,1},{4,6},{5,7},{6,4},{7,5},{8,10},{9,11},{10,... | collective-permute-start | bytes 688136 | tf_op jit(solution)/shard_map/ppermute | solution.py:357
  55.3 11.7 %copy-start = (f32[256,256]{1,0:T(8,128)}, f32[256,256]{1,0:T(8,128)S(1)}, u32[]{:S(2)}) copy-start(f32[256,256]{1,0:T(8,128)S(1)} %add.24.own_p) | copy-start | bytes 786436
  55.3 11.7 %collective-permute-start.16 = (f32[256,256]{1,0:T(8,128)S(1)}, f32[256,256]{1,0:T(8,128)S(1)}, u32[]{:S(2)}, u32[]{:S(2)}) collective-permute-start(f32[256,256]{1,0:T(8,128)S(1)} %add.24.own_p), channel_id=1, source_target_pairs={{0,2},{1,3},{2,0},{3,1},{4,6},{5,7},{6,4},{7,5},{8,10},{9,11},{10,... | collective-permute-start | bytes 786440 | tf_op jit(solution)/shard_map/ppermute | solution.py:357
  61.9 5.1 %copy-start.13 = (f32[224,256]{1,0:T(8,128)}, f32[224,256]{1,0:T(8,128)S(1)}, u32[]{:S(2)}) copy-start(f32[224,256]{1,0:T(8,128)S(1)} %collective-permute-done.14.near) | copy-start | bytes 688132
  61.9 5.1 %collective-permute-start.15 = (f32[224,256]{1,0:T(8,128)S(1)}, f32[224,256]{1,0:T(8,128)S(1)}, u32[]{:S(2)}, u32[]{:S(2)}) collective-permute-start(f32[224,256]{1,0:T(8,128)S(1)} %collective-permute-done.14.near), channel_id=1, source_target_pairs={{0,1},{1,0},{2,3},{3,2},{4,5},{5,4},{6,7},{7,6},{8,9},{9,8},{10,11... | collective-permute-start | bytes 688136 | tf_op jit(solution)/shard_map/ppermute | solution.py:357
  67.0 0.8 copy-start.20
  78.5 12.6 %collective-permute-start.17 = (f32[224,256]{1,0:T(8,128)}, f32[224,256]{1,0:T(8,128)S(1)}, u32[]{:S(2)}, u32[]{:S(2)}) collective-permute-start(f32[224,256]{1,0:T(8,128)} %get-tuple-element.22), channel_id=1, source_target_pairs={{0,4},{4,0},{8,12},{12,8},{16,20},{20,16},{24,28},{28,24},{1,5},{5... | collective-permute-start | bytes 688136 | tf_op jit(solution)/shard_map/ppermute | solution.py:357
  85.4 9.8 %copy-start.1 = (f32[256,256]{1,0:T(8,128)}, f32[256,256]{1,0:T(8,128)S(1)}, u32[]{:S(2)}) copy-start(f32[256,256]{1,0:T(8,128)S(1)} %add.25.own_p) | copy-start | bytes 786436
  85.5 9.8 %collective-permute-start.19 = (f32[256,256]{1,0:T(8,128)S(1)}, f32[256,256]{1,0:T(8,128)S(1)}, u32[]{:S(2)}, u32[]{:S(2)}) collective-permute-start(f32[256,256]{1,0:T(8,128)S(1)} %add.25.own_p), channel_id=1, source_target_pairs={{0,4},{4,0},{8,12},{12,8},{16,20},{20,16},{24,28},{28,24},{1,5},{5... | collective-permute-start | bytes 786440 | tf_op jit(solution)/shard_map/ppermute | solution.py:357
  91.0 4.2 %copy-start.14 = (f32[224,256]{1,0:T(8,128)}, f32[224,256]{1,0:T(8,128)S(1)}, u32[]{:S(2)}) copy-start(f32[224,256]{1,0:T(8,128)S(1)} %collective-permute-done.17.near) | copy-start | bytes 688132
  91.1 4.2 %collective-permute-start.18 = (f32[224,256]{1,0:T(8,128)S(1)}, f32[224,256]{1,0:T(8,128)S(1)}, u32[]{:S(2)}, u32[]{:S(2)}) collective-permute-start(f32[224,256]{1,0:T(8,128)S(1)} %collective-permute-done.17.near), channel_id=1, source_target_pairs={{0,1},{1,0},{2,3},{3,2},{4,5},{5,4},{6,7},{7,6},{8,9},{9,8},{10,11... | collective-permute-start | bytes 688136 | tf_op jit(solution)/shard_map/ppermute | solution.py:357
  95.3 0.8 copy-start.17
  107.0 8.7 %collective-permute-start.20 = (f32[224,256]{1,0:T(8,128)}, f32[224,256]{1,0:T(8,128)S(1)}, u32[]{:S(2)}, u32[]{:S(2)}) collective-permute-start(f32[224,256]{1,0:T(8,128)} %get-tuple-element.25), channel_id=1, source_target_pairs={{0,8},{4,12},{8,0},{12,4},{16,24},{20,28},{24,16},{28,20},{1,9},{5... | collective-permute-start | bytes 688136 | tf_op jit(solution)/shard_map/ppermute | solution.py:357
  108.1 11.0 %copy-start.2 = (f32[256,256]{1,0:T(8,128)}, f32[256,256]{1,0:T(8,128)S(1)}, u32[]{:S(2)}) copy-start(f32[256,256]{1,0:T(8,128)S(1)} %add.26.own_p) | copy-start | bytes 786436
  108.1 11.0 %collective-permute-start.22 = (f32[256,256]{1,0:T(8,128)S(1)}, f32[256,256]{1,0:T(8,128)S(1)}, u32[]{:S(2)}, u32[]{:S(2)}) collective-permute-start(f32[256,256]{1,0:T(8,128)S(1)} %add.26.own_p), channel_id=1, source_target_pairs={{0,8},{4,12},{8,0},{12,4},{16,24},{20,28},{24,16},{28,20},{1,9},{5... | collective-permute-start | bytes 786440 | tf_op jit(solution)/shard_map/ppermute | solution.py:357
  115.7 3.4 %copy-start.15 = (f32[224,256]{1,0:T(8,128)}, f32[224,256]{1,0:T(8,128)S(1)}, u32[]{:S(2)}) copy-start(f32[224,256]{1,0:T(8,128)S(1)} %collective-permute-done.20.near) | copy-start | bytes 688132
  115.7 3.4 %collective-permute-start.21 = (f32[224,256]{1,0:T(8,128)S(1)}, f32[224,256]{1,0:T(8,128)S(1)}, u32[]{:S(2)}, u32[]{:S(2)}) collective-permute-start(f32[224,256]{1,0:T(8,128)S(1)} %collective-permute-done.20.near), channel_id=1, source_target_pairs={{0,1},{1,0},{2,3},{3,2},{4,5},{5,4},{6,7},{7,6},{8,9},{9,8},{10,11... | collective-permute-start | bytes 688136 | tf_op jit(solution)/shard_map/ppermute | solution.py:357
  130.6 17.5 %collective-permute-start.23 = (f32[224,256]{1,0:T(8,128)}, f32[224,256]{1,0:T(8,128)S(1)}, u32[]{:S(2)}, u32[]{:S(2)}) collective-permute-start(f32[224,256]{1,0:T(8,128)} %get-tuple-element.28), channel_id=1, source_target_pairs={{0,16},{4,20},{8,24},{12,28},{16,0},{20,4},{24,8},{28,12},{1,17},{... | collective-permute-start | bytes 688136 | tf_op jit(solution)/shard_map/ppermute | solution.py:357
  132.8 20.4 %copy-start.7 = (f32[256,256]{1,0:T(8,128)}, f32[256,256]{1,0:T(8,128)S(1)}, u32[]{:S(2)}) copy-start(f32[256,256]{1,0:T(8,128)S(1)} %add.27.own_p) | copy-start | bytes 786436
  132.9 20.4 %collective-permute-start.25 = (f32[256,256]{1,0:T(8,128)S(1)}, f32[256,256]{1,0:T(8,128)S(1)}, u32[]{:S(2)}, u32[]{:S(2)}) collective-permute-start(f32[256,256]{1,0:T(8,128)S(1)} %add.27.own_p), channel_id=1, source_target_pairs={{0,16},{4,20},{8,24},{12,28},{16,0},{20,4},{24,8},{28,12},{1,17},{... | collective-permute-start | bytes 786440 | tf_op jit(solution)/shard_map/ppermute | solution.py:357
  148.0 5.3 %copy-start.16 = (f32[224,256]{1,0:T(8,128)}, f32[224,256]{1,0:T(8,128)S(1)}, u32[]{:S(2)}) copy-start(f32[224,256]{1,0:T(8,128)S(1)} %collective-permute-done.23.near) | copy-start | bytes 688132
  148.0 5.2 %collective-permute-start.24 = (f32[224,256]{1,0:T(8,128)S(1)}, f32[224,256]{1,0:T(8,128)S(1)}, u32[]{:S(2)}, u32[]{:S(2)}) collective-permute-start(f32[224,256]{1,0:T(8,128)S(1)} %collective-permute-done.23.near), channel_id=1, source_target_pairs={{0,1},{1,0},{2,3},{3,2},{4,5},{5,4},{6,7},{7,6},{8,9},{9,8},{10,11... | collective-permute-start | bytes 688136 | tf_op jit(solution)/shard_map/ppermute | solution.py:357
  (9 other events, 6.4 us)
where the time goes:
time: 165 us; the launch traced here: 164 us
  waiting for transfers between devices  66.2 us (40%)
  Pallas kernels  57.6 us (35%)
  starting transfers between devices  29.8 us (18%)
  other arithmetic  4.93 us (3%)
  local copies, waits for them, and re-layouts  4.68 us (3%)
    ppermute x25, waiting for transfers between devices, swap(): lax.ppermute(x, axis, [(i, i ^ 1 << bit) for i in range(lax.axis_size(axi...  66.2 us
    pallas_call x4, Pallas kernels, upper_merge(): pl.pallas_call(functools.partial(upper_kernel, level, is_last, bool(extra...  42.2 us
    ppermute x25, starting transfers between devices, swap(): lax.ppermute(x, axis, [(i, i ^ 1 << bit) for i in range(lax.axis_size(axi...  28.9 us
    pallas_call x1, Pallas kernels, first_merge(): pl.pallas_call(first_kernel, out_shape=[jax.ShapeDtypeStruct((rows, size)...  9.27 us
    pallas_call x1, Pallas kernels, all_samples(): pl.pallas_call(functools.partial(sample_kernel, keys), out_shape=[jax.Sha...  6.11 us
    unnamed x62, local copies, waits for them, and re-layouts  4.68 us
  transfers between devices with their start and end apart: 26, of which 16 were waited for; matrix products, arithmetic and copies ran while one was open for 2% of the time, Pallas kernels for 6%

commit v1 on v0

--- a/solution.py
+++ b/solution.py
@@ -259,12 +259,13 @@
 ANY = pl.BlockSpec(memory_space=pl.ANY)
 
 
+def near_core(arrays):
+    return [pltpu.with_memory_space_constraint(x, pltpu.VMEM) for x in arrays]
+
+
 def state_shapes(size):
     rows = size // 2 + 3 * size // 8
-    return [
-        jax.ShapeDtypeStruct((2, rows, size), F32),
-        jax.ShapeDtypeStruct((rows, size), F32),
-    ]
+    return [pltpu.VMEM((2, rows, size), F32), pltpu.VMEM((rows, size), F32)]
 
 
 def first_merge(side, arrays):
@@ -275,7 +276,7 @@
         in_specs=[SMEM] + [VMEM] * len(arrays),
         out_specs=[VMEM] * 3,
         name="first_merge",
-    )(side, *arrays)
+    )(side, *near_core(arrays))
 
 
 def upper_merge(level, levels, side, arrays, buffer):
@@ -291,7 +292,7 @@
         out_specs=[ANY] + [VMEM] * (len(out_shape) - 1),
         scratch_shapes=[pltpu.VMEM((size, size), F32), pltpu.SemaphoreType.DMA(())],
         input_output_aliases={1 + len(arrays): 0} if extra else {},
-    )(side, *arrays, *extra)
+    )(side, *near_core(arrays), *extra)
 
 
 def sample_kernel(keys, place, mask, front, *refs):
@@ -321,6 +322,7 @@
             def _():
                 copies[slot, j].start()
 
+    probes = jnp.concatenate([x[...] for x in chunks], axis=0)
     for slot in order:
         for j in range(count):
 
@@ -328,21 +330,20 @@
             def _():
                 copies[slot, j].wait()
 
-        total = None
-        for j in range(count):
-            tile = jnp.where(present[slot, j], tiles[slot, j], jnp.zeros((), BF16))
-            term = dot(tile, chunks[j][...], (1, 0))
-            total = term if total is None else total + term
+        row = [
+            jnp.where(present[slot, j], tiles[slot, j], jnp.zeros((), BF16)) for j in range(count)
+        ]
         out = send if slot % 2 else keep
-        out[slot // 2] = total
+        out[slot // 2] = dot(jnp.concatenate(row, axis=1), probes, (1, 0))
 
 
 def all_samples(front, tile_mask, place, chunks, keys):
     leaf, size = chunks[0].shape
     slots = front.shape[0] // leaf
+    small = len(keys) * leaf * size < 2**20
     return pl.pallas_call(
         functools.partial(sample_kernel, keys),
-        out_shape=[jax.ShapeDtypeStruct((slots // 2, leaf, size), F32)] * 2,
+        out_shape=[(pltpu.VMEM if small else jax.ShapeDtypeStruct)((slots // 2, leaf, size), F32)] * 2,
         in_specs=[SMEM, SMEM, ANY] + [VMEM] * len(keys),
         out_specs=[VMEM] * 2,
         scratch_shapes=[
@@ -350,7 +351,7 @@
             pltpu.SemaphoreType.DMA((slots, len(keys))),
         ],
         name="samples",
-    )(place, tile_mask, front, *chunks)
+    )(place, tile_mask, front, *(near_core(chunks) if small else chunks))
 
 
 def swap(x, axis, bit):
@@ -401,7 +402,9 @@
     other_a = swap(own_a, "col", 0)
     other_b = swap(own_b, "col", 0)
 
-    leaf_basis, state, send = first_merge(side, (own_a, own_b, other_a, other_b, own_w, other_w))
+    leaf_basis, state, send = first_merge(
+        side, (own_a, own_b, other_a, other_b, own_w, other_w)
+    )
     buffer = None
     for level, (axis, bit) in list(enumerate(bits, start=1))[1:]:
         near = swap(send, axis, bit)

time: 165 us -> 148 us (0.90)
  Pallas kernels: 57.6 us -> 47.2 us
  other arithmetic: 4.93 us -> 0.82 us
  local copies, waits for them, and re-layouts: 4.68 us -> 0.91 us
  waiting for transfers between devices: 66.2 us -> 68.7 us
    pallas_call x4, Pallas kernels: 42.2 us -> 34.3 us  [upper_merge(): pl.pallas_call(functools.partial(upper_kernel, level, is_last, bool(extra...]
    unnamed x62 -> x6, local copies, waits for them, and re-layouts: 4.68 us -> 0.91 us
    add x4, other arithmetic: 3.22 us -> 0.14 us  [step(): total_p = own_p[level] + other_p[level]]
    ppermute x25, waiting for transfers between devices: 66.2 us -> 68.6 us  [swap(): lax.ppermute(x, axis, [(i, i ^ 1 << bit) for i in range(lax.axis_size(axi...]
  transfers between devices with their start and end apart: 26 -> 26, of which waited for: 16 -> 16; matrix products, arithmetic and copies ran while one was open for 2% -> 1% of each run, Pallas kernels for 6% -> 5%
where the time goes in v1:
time: 148 us
  waiting for transfers between devices  68.7 us (46%)
  Pallas kernels  47.2 us (32%)
  starting transfers between devices  29 us (20%)
    ppermute x25, waiting for transfers between devices, swap(): lax.ppermute(x, axis, [(i, i ^ 1 << bit) for i in range(lax.axis_size(axi...  68.6 us
    pallas_call x4, Pallas kernels, upper_merge(): pl.pallas_call(functools.partial(upper_kernel, level, is_last, bool(extra...  34.3 us
    ppermute x25, starting transfers between devices, swap(): lax.ppermute(x, axis, [(i, i ^ 1 << bit) for i in range(lax.axis_size(axi...  28.2 us
    pallas_call x1, Pallas kernels, first_merge(): pl.pallas_call(first_kernel, out_shape=[jax.ShapeDtypeStruct((rows, size)...  8.01 us
    pallas_call x1, Pallas kernels, all_samples(): pl.pallas_call(functools.partial(sample_kernel, keys), out_shape=[(pltpu....  4.85 us
  transfers between devices with their start and end apart: 26, of which 16 were waited for; matrix products, arithmetic and copies ran while one was open for 1% of the time, Pallas kernels for 5%

profile of v1, /device:TPU:0, one launch (start us, length us, event | category | flops | bytes accessed | tf_op | source)
XLA Modules:
  0.0 147.6 jit_solution(4526948540883761649)
XLA Ops:
  0.6 4.1 %collective-permute-start.1 = (bf16[256,256]{1,0:T(8,128)(2,1)}, bf16[256,256]{1,0:T(8,128)(2,1)S(1)}, u32[]{:S(2)}, u32[]{:S(2)}) collective-permute-start(bf16[256,256]{1,0:T(8,128)(2,1)} %refs_0_.1), channel_id=1, source_target_pairs={{0,16},{4,20},{8,24},{12,28},{16,0},{20,4},{24,8},{28,12},{1,17},{... | collective-permute-start | bytes 393224 | tf_op jit(solution)/shard_map/ppermute | solution.py:358
  4.8 1.6 %collective-permute-start.3 = (bf16[256,256]{1,0:T(8,128)(2,1)}, bf16[256,256]{1,0:T(8,128)(2,1)S(1)}, u32[]{:S(2)}, u32[]{:S(2)}) collective-permute-start(bf16[256,256]{1,0:T(8,128)(2,1)} %refs_0_.1), channel_id=1, source_target_pairs={{0,8},{4,12},{8,0},{12,4},{16,24},{20,28},{24,16},{28,20},{1,9},{5... | collective-permute-start | bytes 393224 | tf_op jit(solution)/shard_map/ppermute | solution.py:358
  6.3 5.0 %collective-permute-done.1.refs_2_ = bf16[256,256]{1,0:T(8,128)(2,1)S(1)} collective-permute-done((bf16[256,256]{1,0:T(8,128)(2,1)}, bf16[256,256]{1,0:T(8,128)(2,1)S(1)}, u32[]{:S(2)}, u32[]{:S(2)}) %collective-permute-start.1) | collective-permute-done | bytes 131104 | tf_op jit(solution)/shard_map/ppermute | solution.py:358
  11.4 1.6 %collective-permute-start.2 = (bf16[256,256]{1,0:T(8,128)(2,1)S(1)}, bf16[256,256]{1,0:T(8,128)(2,1)S(1)}, u32[]{:S(2)}, u32[]{:S(2)}) collective-permute-start(bf16[256,256]{1,0:T(8,128)(2,1)S(1)} %collective-permute-done.1.refs_2_), channel_id=1, source_target_pairs={{0,4},{4,0},{8,12},{12,8},{16,20},{20,16},{24,28},{28,24},{1,5},{5... | collective-permute-start | bytes 393224 | tf_op jit(solution)/shard_map/ppermute | solution.py:358
  12.9 0.5 collective-permute-start
  13.4 0.7 collective-permute-start.5
  14.1 1.5 %collective-permute-start.4 = (bf16[256,256]{1,0:T(8,128)(2,1)S(1)}, bf16[256,256]{1,0:T(8,128)(2,1)S(1)}, u32[]{:S(2)}, u32[]{:S(2)}) collective-permute-start(bf16[256,256]{1,0:T(8,128)(2,1)S(1)} %collective-permute-done.3.refs_4_), channel_id=1, source_target_pairs={{0,4},{4,0},{8,12},{12,8},{16,20},{20,16},{24,28},{28,24},{1,5},{5... | collective-permute-start | bytes 393224 | tf_op jit(solution)/shard_map/ppermute | solution.py:358
  15.7 2.1 %collective-permute-done.2.refs_3_ = bf16[256,256]{1,0:T(8,128)(2,1)S(1)} collective-permute-done((bf16[256,256]{1,0:T(8,128)(2,1)S(1)}, bf16[256,256]{1,0:T(8,128)(2,1)S(1)}, u32[]{:S(2)}, u32[]{:S(2)}) %collective-permute-start.2) | collective-permute-done | bytes 131104 | tf_op jit(solution)/shard_map/ppermute | solution.py:358
  17.8 0.7 collective-permute-start.6
  18.5 0.6 pad_add_fusion.place
  19.1 0.8 collective-permute-done.refs_1_
  19.9 1.4 collective-permute-done.4.refs_5_
  21.3 0.0 collective-permute-done.5.refs_6_
  21.3 1.4 collective-permute-done.6.refs_7_
  22.7 0.9 copy-done
  23.6 4.8 %samples.1 = (f32[2,256,256]{2,1,0:T(8,128)S(1)}, f32[2,256,256]{2,1,0:T(8,128)S(1)}) custom-call(s32[2]{0:T(128)} %pad_add_fusion.place, s32[4,8]{1,0:T(4,128)} %mask.1, bf16[1024,2048]{1,0:T(8,128)(2,1)} %front.1, bf16[256,256]{1,0:T(8,128)(2,1)S(1)} %copy-done, bf16[256,256]{1,0:T(8,128)(2,1)S(1)} %collective-permute-done.refs_1_, ...), custom_call_target="tpu_custom_call" | custom-call | tf_op jit(solution)/shard_map/samples/pallas_call | solution.py:344
  28.5 0.1 collective-permute-start.7
  28.6 1.9 %collective-permute-done.7 = f32[2,256,256]{2,1,0:T(8,128)S(1)} collective-permute-done((f32[2,256,256]{2,1,0:T(8,128)S(1)}, f32[2,256,256]{2,1,0:T(8,128)S(1)}, u32[]{:S(2)}, u32[]{:S(2)}) %collective-permute-start.7) | collective-permute-done | bytes 524320 | tf_op jit(solution)/shard_map/ppermute | solution.py:358
  30.5 0.1 slice_add_fusion
  30.5 0.8 collective-permute-start.8
  31.3 0.8 collective-permute-start.11
  32.2 3.0 %collective-permute-start.9 = (f32[256,256]{1,0:T(8,128)S(1)}, f32[256,256]{1,0:T(8,128)S(1)}, u32[]{:S(2)}, u32[]{:S(2)}) collective-permute-start(f32[256,256]{1,0:T(8,128)S(1)} %get-tuple-element.31.own_a), channel_id=1, source_target_pairs={{0,1},{1,0},{2,3},{3,2},{4,5},{5,4},{6,7},{7,6},{8,9},{9,8},{10,11... | collective-permute-start | bytes 786440 | tf_op jit(solution)/shard_map/ppermute | solution.py:358
  35.2 3.8 %collective-permute-done.8 = f32[1,256,256]{2,1,0:T(8,128)S(1)} collective-permute-done((f32[1,256,256]{2,1,0:T(8,128)S(1)}, f32[1,256,256]{2,1,0:T(8,128)S(1)}, u32[]{:S(2)}, u32[]{:S(2)}) %collective-permute-start.8) | collective-permute-done | bytes 262176 | tf_op jit(solution)/shard_map/ppermute | solution.py:358
  38.9 0.0 collective-permute-start.10
  39.0 0.5 collective-permute-start.12
  39.5 0.1 collective-permute-start.13
  39.5 1.1 collective-permute-done.12.other_w
  40.7 8.0 %first_merge.1 = (f32[256,256]{1,0:T(8,128)}, f32[2,224,256]{2,1,0:T(8,128)S(1)}, f32[224,256]{1,0:T(8,128)S(1)}) custom-call(s32[1]{0:T(128)} %bitcast.side, f32[256,256]{1,0:T(8,128)S(1)} %get-tuple-element.31.own_a, f32[256,256]{1,0:T(8,128)S(1)} %bitcast.7, f32[256,256]{1,0:T(8,128)S(1)} %collective-permute-done.9.other_a, ...), custom_call_target="tpu_custom_call" | custom-call | tf_op jit(solution)/shard_map/first_merge/pallas_call | solution.py:273
  48.7 2.2 %collective-permute-start.14 = (f32[224,256]{1,0:T(8,128)S(1)}, f32[224,256]{1,0:T(8,128)S(1)}, u32[]{:S(2)}, u32[]{:S(2)}) collective-permute-start(f32[224,256]{1,0:T(8,128)S(1)} %get-tuple-element.20), channel_id=1, source_target_pairs={{0,2},{1,3},{2,0},{3,1},{4,6},{5,7},{6,4},{7,5},{8,10},{9,11},{10,... | collective-permute-start | bytes 688136 | tf_op jit(solution)/shard_map/ppermute | solution.py:358
  50.9 0.1 collective-permute-start.16
  51.0 6.3 %collective-permute-done.14.near = f32[224,256]{1,0:T(8,128)S(1)} collective-permute-done((f32[224,256]{1,0:T(8,128)S(1)}, f32[224,256]{1,0:T(8,128)S(1)}, u32[]{:S(2)}, u32[]{:S(2)}) %collective-permute-start.14) | collective-permute-done | bytes 229408 | tf_op jit(solution)/shard_map/ppermute | solution.py:358
  57.4 5.1 %collective-permute-done.16.other_p = f32[256,256]{1,0:T(8,128)S(1)} collective-permute-done((f32[256,256]{1,0:T(8,128)S(1)}, f32[256,256]{1,0:T(8,128)S(1)}, u32[]{:S(2)}, u32[]{:S(2)}) %collective-permute-start.16) | collective-permute-done | bytes 262176 | tf_op jit(solution)/shard_map/ppermute | solution.py:358
  62.4 8.5 %shard_map.59 = (f32[4,256,256]{2,1,0:T(8,128)}, f32[2,224,256]{2,1,0:T(8,128)S(1)}, f32[224,256]{1,0:T(8,128)S(1)}) custom-call(s32[1]{0:T(128)} %bitcast.side, f32[2,224,256]{2,1,0:T(8,128)S(1)} %get-tuple-element.19.own, f32[256,256]{1,0:T(8,128)S(1)} %add.24.own_p, f32[224,256]{1,0:T(8,128)S(1)} %collective-permute-done.14.near, ...), custom_call_target="tpu_custom_call" | custom-call | tf_op jit(solution)/shard_map/pallas_call | solution.py:288
  70.9 5.5 %collective-permute-start.17 = (f32[224,256]{1,0:T(8,128)S(1)}, f32[224,256]{1,0:T(8,128)S(1)}, u32[]{:S(2)}, u32[]{:S(2)}) collective-permute-start(f32[224,256]{1,0:T(8,128)S(1)} %get-tuple-element.22), channel_id=1, source_target_pairs={{0,4},{4,0},{8,12},{12,8},{16,20},{20,16},{24,28},{28,24},{1,5},{5... | collective-permute-start | bytes 688136 | tf_op jit(solution)/shard_map/ppermute | solution.py:358
  76.4 0.1 collective-permute-start.19
  76.5 6.3 %collective-permute-done.17.near = f32[224,256]{1,0:T(8,128)S(1)} collective-permute-done((f32[224,256]{1,0:T(8,128)S(1)}, f32[224,256]{1,0:T(8,128)S(1)}, u32[]{:S(2)}, u32[]{:S(2)}) %collective-permute-start.17) | collective-permute-done | bytes 229408 | tf_op jit(solution)/shard_map/ppermute | solution.py:358
  82.8 4.2 %collective-permute-done.19.other_p = f32[256,256]{1,0:T(8,128)S(1)} collective-permute-done((f32[256,256]{1,0:T(8,128)S(1)}, f32[256,256]{1,0:T(8,128)S(1)}, u32[]{:S(2)}, u32[]{:S(2)}) %collective-permute-start.19) | collective-permute-done | bytes 262176 | tf_op jit(solution)/shard_map/ppermute | solution.py:358
  87.1 8.7 %shard_map.60 = (f32[4,256,256]{2,1,0:T(8,128)}, f32[2,224,256]{2,1,0:T(8,128)S(1)}, f32[224,256]{1,0:T(8,128)S(1)}) custom-call(s32[1]{0:T(128)} %bitcast.side, f32[2,224,256]{2,1,0:T(8,128)S(1)} %get-tuple-element.21.own, f32[256,256]{1,0:T(8,128)S(1)} %add.25.own_p, f32[224,256]{1,0:T(8,128)S(1)} %collective-permute-done.17.near, ...), custom_call_target="tpu_custom_call", output_to_operand_aliasing={{0}: (6, {})} | custom-call | tf_op jit(solution)/shard_map/pallas_call | solution.py:288
  95.8 0.1 collective-permute-start.20
  95.9 2.1 %collective-permute-start.22 = (f32[256,256]{1,0:T(8,128)S(1)}, f32[256,256]{1,0:T(8,128)S(1)}, u32[]{:S(2)}, u32[]{:S(2)}) collective-permute-start(f32[256,256]{1,0:T(8,128)S(1)} %add.26.own_p), channel_id=1, source_target_pairs={{0,8},{4,12},{8,0},{12,4},{16,24},{20,28},{24,16},{28,20},{1,9},{5... | collective-permute-start | bytes 786440 | tf_op jit(solution)/shard_map/ppermute | solution.py:358
  97.9 6.3 %collective-permute-done.20.near = f32[224,256]{1,0:T(8,128)S(1)} collective-permute-done((f32[224,256]{1,0:T(8,128)S(1)}, f32[224,256]{1,0:T(8,128)S(1)}, u32[]{:S(2)}, u32[]{:S(2)}) %collective-permute-start.20) | collective-permute-done | bytes 229408 | tf_op jit(solution)/shard_map/ppermute | solution.py:358
  104.3 3.4 %collective-permute-done.22.other_p = f32[256,256]{1,0:T(8,128)S(1)} collective-permute-done((f32[256,256]{1,0:T(8,128)S(1)}, f32[256,256]{1,0:T(8,128)S(1)}, u32[]{:S(2)}, u32[]{:S(2)}) %collective-permute-start.22) | collective-permute-done | bytes 262176 | tf_op jit(solution)/shard_map/ppermute | solution.py:358
  107.7 8.5 %shard_map.61 = (f32[4,256,256]{2,1,0:T(8,128)}, f32[2,224,256]{2,1,0:T(8,128)S(1)}, f32[224,256]{1,0:T(8,128)S(1)}) custom-call(s32[1]{0:T(128)} %bitcast.side, f32[2,224,256]{2,1,0:T(8,128)S(1)} %get-tuple-element.24.own, f32[256,256]{1,0:T(8,128)S(1)} %add.26.own_p, f32[224,256]{1,0:T(8,128)S(1)} %collective-permute-done.20.near, ...), custom_call_target="tpu_custom_call", output_to_operand_aliasing={{0}: (6, {})} | custom-call | tf_op jit(solution)/shard_map/pallas_call | solution.py:288
  116.1 0.8 collective-permute-start.23
  117.0 2.3 %collective-permute-start.25 = (f32[256,256]{1,0:T(8,128)S(1)}, f32[256,256]{1,0:T(8,128)S(1)}, u32[]{:S(2)}, u32[]{:S(2)}) collective-permute-start(f32[256,256]{1,0:T(8,128)S(1)} %add.27.own_p), channel_id=1, source_target_pairs={{0,16},{4,20},{8,24},{12,28},{16,0},{20,4},{24,8},{28,12},{1,17},{... | collective-permute-start | bytes 786440 | tf_op jit(solution)/shard_map/ppermute | solution.py:358
  119.2 13.9 %collective-permute-done.23.near = f32[224,256]{1,0:T(8,128)S(1)} collective-permute-done((f32[224,256]{1,0:T(8,128)S(1)}, f32[224,256]{1,0:T(8,128)S(1)}, u32[]{:S(2)}, u32[]{:S(2)}) %collective-permute-start.23) | collective-permute-done | bytes 229408 | tf_op jit(solution)/shard_map/ppermute | solution.py:358
  133.1 5.5 %collective-permute-done.25.other_p = f32[256,256]{1,0:T(8,128)S(1)} collective-permute-done((f32[256,256]{1,0:T(8,128)S(1)}, f32[256,256]{1,0:T(8,128)S(1)}, u32[]{:S(2)}, u32[]{:S(2)}) %collective-permute-start.25) | collective-permute-done | bytes 262176 | tf_op jit(solution)/shard_map/ppermute | solution.py:358
  138.6 8.7 %shard_map.62 = f32[4,256,256]{2,1,0:T(8,128)} custom-call(s32[1]{0:T(128)} %bitcast.side, f32[2,224,256]{2,1,0:T(8,128)S(1)} %get-tuple-element.27.own, f32[256,256]{1,0:T(8,128)S(1)} %add.27.own_p, f32[224,256]{1,0:T(8,128)S(1)} %collective-permute-done.23.near, f32[224,256]{1,0:T(8,128)S(1)} %collective-permute-done.24.far, ...), custom_call_target="tpu_custom_call", output_to_operand_aliasing={{}: (6, {})} | custom-call | tf_op jit(solution)/shard_map/pallas_call | solution.py:288
  (22 shorter events, 0.2 us)
Async XLA Ops:
  0.6 10.8 %collective-permute-start.1 = (bf16[256,256]{1,0:T(8,128)(2,1)}, bf16[256,256]{1,0:T(8,128)(2,1)S(1)}, u32[]{:S(2)}, u32[]{:S(2)}) collective-permute-start(bf16[256,256]{1,0:T(8,128)(2,1)} %refs_0_.1), channel_id=1, source_target_pairs={{0,16},{4,20},{8,24},{12,28},{16,0},{20,4},{24,8},{28,12},{1,17},{... | collective-permute-start | bytes 393224 | tf_op jit(solution)/shard_map/ppermute | solution.py:358
  4.8 9.4 %collective-permute-start.3 = (bf16[256,256]{1,0:T(8,128)(2,1)}, bf16[256,256]{1,0:T(8,128)(2,1)S(1)}, u32[]{:S(2)}, u32[]{:S(2)}) collective-permute-start(bf16[256,256]{1,0:T(8,128)(2,1)} %refs_0_.1), channel_id=1, source_target_pairs={{0,8},{4,12},{8,0},{12,4},{16,24},{20,28},{24,16},{28,20},{1,9},{5... | collective-permute-start | bytes 393224 | tf_op jit(solution)/shard_map/ppermute | solution.py:358
  11.4 6.4 %collective-permute-start.2 = (bf16[256,256]{1,0:T(8,128)(2,1)S(1)}, bf16[256,256]{1,0:T(8,128)(2,1)S(1)}, u32[]{:S(2)}, u32[]{:S(2)}) collective-permute-start(bf16[256,256]{1,0:T(8,128)(2,1)S(1)} %collective-permute-done.1.refs_2_), channel_id=1, source_target_pairs={{0,4},{4,0},{8,12},{12,8},{16,20},{20,16},{24,28},{28,24},{1,5},{5... | collective-permute-start | bytes 393224 | tf_op jit(solution)/shard_map/ppermute | solution.py:358
  12.9 7.0 %collective-permute-start = (bf16[256,256]{1,0:T(8,128)(2,1)}, bf16[256,256]{1,0:T(8,128)(2,1)S(1)}, u32[]{:S(2)}, u32[]{:S(2)}) collective-permute-start(bf16[256,256]{1,0:T(8,128)(2,1)} %refs_0_.1), channel_id=1, source_target_pairs={{0,4},{4,0},{8,12},{12,8},{16,20},{20,16},{24,28},{28,24},{1,5},{5... | collective-permute-start | bytes 393224 | tf_op jit(solution)/shard_map/ppermute | solution.py:358
  13.4 7.9 %collective-permute-start.5 = (bf16[256,256]{1,0:T(8,128)(2,1)S(1)}, bf16[256,256]{1,0:T(8,128)(2,1)S(1)}, u32[]{:S(2)}, u32[]{:S(2)}) collective-permute-start(bf16[256,256]{1,0:T(8,128)(2,1)S(1)} %collective-permute-done.1.refs_2_), channel_id=1, source_target_pairs={{0,8},{4,12},{8,0},{12,4},{16,24},{20,28},{24,16},{28,20},{1,9},{5... | collective-permute-start | bytes 393224 | tf_op jit(solution)/shard_map/ppermute | solution.py:358
  14.1 7.2 %collective-permute-start.4 = (bf16[256,256]{1,0:T(8,128)(2,1)S(1)}, bf16[256,256]{1,0:T(8,128)(2,1)S(1)}, u32[]{:S(2)}, u32[]{:S(2)}) collective-permute-start(bf16[256,256]{1,0:T(8,128)(2,1)S(1)} %collective-permute-done.3.refs_4_), channel_id=1, source_target_pairs={{0,4},{4,0},{8,12},{12,8},{16,20},{20,16},{24,28},{28,24},{1,5},{5... | collective-permute-start | bytes 393224 | tf_op jit(solution)/shard_map/ppermute | solution.py:358
  17.8 5.0 %collective-permute-start.6 = (bf16[256,256]{1,0:T(8,128)(2,1)S(1)}, bf16[256,256]{1,0:T(8,128)(2,1)S(1)}, u32[]{:S(2)}, u32[]{:S(2)}) collective-permute-start(bf16[256,256]{1,0:T(8,128)(2,1)S(1)} %collective-permute-done.2.refs_3_), channel_id=1, source_target_pairs={{0,8},{4,12},{8,0},{12,4},{16,24},{20,28},{24,16},{28,20},{1,9},{5... | collective-permute-start | bytes 393224 | tf_op jit(solution)/shard_map/ppermute | solution.py:358
  22.7 0.9 copy-start
  23.6 7.7 %copy-start.1 = (bf16[256,256]{1,0:T(8,128)(2,1)S(1)}, bf16[256,256]{1,0:T(8,128)(2,1)}, u32[]{:S(2)}) copy-start(bf16[256,256]{1,0:T(8,128)(2,1)} %refs_0_.1) | copy-start | bytes 393220
  23.6 15.8 %copy-start.2 = (f32[256,256]{1,0:T(8,128)S(1)}, f32[256,256]{1,0:T(8,128)}, u32[]{:S(2)}) copy-start(f32[256,256]{1,0:T(8,128)} %param.7) | copy-start | bytes 786436
  28.5 2.0 %collective-permute-start.7 = (f32[2,256,256]{2,1,0:T(8,128)S(1)}, f32[2,256,256]{2,1,0:T(8,128)S(1)}, u32[]{:S(2)}, u32[]{:S(2)}) collective-permute-start(f32[2,256,256]{2,1,0:T(8,128)S(1)} %get-tuple-element.17), channel_id=1, source_target_pairs={{0,1},{1,0},{2,3},{3,2},{4,5},{5,4},{6,7},{7,6},{8,9},{9,8},{10,11... | collective-permute-start | bytes 1572872 | tf_op jit(solution)/shard_map/ppermute | solution.py:358
  30.5 8.4 %collective-permute-start.8 = (f32[1,256,256]{2,1,0:T(8,128)S(1)}, f32[1,256,256]{2,1,0:T(8,128)S(1)}, u32[]{:S(2)}, u32[]{:S(2)}) collective-permute-start(f32[1,256,256]{2,1,0:T(8,128)S(1)} %get-tuple-element.30), channel_id=1, source_target_pairs={{0,2},{1,3},{2,0},{3,1},{4,6},{5,7},{6,4},{7,5},{8,10},{9,11},{10,... | collective-permute-start | bytes 786440 | tf_op jit(solution)/shard_map/ppermute | solution.py:358
  31.3 7.6 %collective-permute-start.11 = (bf16[256,256]{1,0:T(8,128)(2,1)S(1)}, bf16[256,256]{1,0:T(8,128)(2,1)S(1)}, u32[]{:S(2)}, u32[]{:S(2)}) collective-permute-start(bf16[256,256]{1,0:T(8,128)(2,1)S(1)} %copy-done.1), channel_id=1, source_target_pairs={{0,0},{4,1},{8,2},{12,3},{16,4},{20,5},{24,6},{28,7},{1,8},{5,9},{... | collective-permute-start | bytes 393224 | tf_op jit(solution)/shard_map/ppermute | solution.py:383
  32.2 8.5 %collective-permute-start.9 = (f32[256,256]{1,0:T(8,128)S(1)}, f32[256,256]{1,0:T(8,128)S(1)}, u32[]{:S(2)}, u32[]{:S(2)}) collective-permute-start(f32[256,256]{1,0:T(8,128)S(1)} %get-tuple-element.31.own_a), channel_id=1, source_target_pairs={{0,1},{1,0},{2,3},{3,2},{4,5},{5,4},{6,7},{7,6},{8,9},{9,8},{10,11... | collective-permute-start | bytes 786440 | tf_op jit(solution)/shard_map/ppermute | solution.py:358
  38.9 1.7 %collective-permute-start.10 = (f32[256,256]{1,0:T(8,128)S(1)}, f32[256,256]{1,0:T(8,128)S(1)}, u32[]{:S(2)}, u32[]{:S(2)}) collective-permute-start(f32[256,256]{1,0:T(8,128)S(1)} %bitcast.6), channel_id=1, source_target_pairs={{0,1},{1,0},{2,3},{3,2},{4,5},{5,4},{6,7},{7,6},{8,9},{9,8},{10,11... | collective-permute-start | bytes 786440 | tf_op jit(solution)/shard_map/ppermute | solution.py:358
  39.0 1.7 %collective-permute-start.12 = (bf16[256,256]{1,0:T(8,128)(2,1)S(1)}, bf16[256,256]{1,0:T(8,128)(2,1)S(1)}, u32[]{:S(2)}, u32[]{:S(2)}) collective-permute-start(bf16[256,256]{1,0:T(8,128)(2,1)S(1)} %collective-permute-done.11.own_w), channel_id=1, source_target_pairs={{0,1},{1,0},{2,3},{3,2},{4,5},{5,4},{6,7},{7,6},{8,9},{9,8},{10,11... | collective-permute-start | bytes 393224 | tf_op jit(solution)/shard_map/ppermute | solution.py:358
  39.5 11.4 %collective-permute-start.13 = (f32[256,256]{1,0:T(8,128)S(1)}, f32[256,256]{1,0:T(8,128)S(1)}, u32[]{:S(2)}, u32[]{:S(2)}) collective-permute-start(f32[256,256]{1,0:T(8,128)S(1)} %copy-done.2), channel_id=1, source_target_pairs={{0,1},{1,0},{2,3},{3,2},{4,5},{5,4},{6,7},{7,6},{8,9},{9,8},{10,11... | collective-permute-start | bytes 786440 | tf_op jit(solution)/shard_map/ppermute | solution.py:358
  48.7 8.7 %collective-permute-start.14 = (f32[224,256]{1,0:T(8,128)S(1)}, f32[224,256]{1,0:T(8,128)S(1)}, u32[]{:S(2)}, u32[]{:S(2)}) collective-permute-start(f32[224,256]{1,0:T(8,128)S(1)} %get-tuple-element.20), channel_id=1, source_target_pairs={{0,2},{1,3},{2,0},{3,1},{4,6},{5,7},{6,4},{7,5},{8,10},{9,11},{10,... | collective-permute-start | bytes 688136 | tf_op jit(solution)/shard_map/ppermute | solution.py:358
  50.9 11.5 %collective-permute-start.16 = (f32[256,256]{1,0:T(8,128)S(1)}, f32[256,256]{1,0:T(8,128)S(1)}, u32[]{:S(2)}, u32[]{:S(2)}) collective-permute-start(f32[256,256]{1,0:T(8,128)S(1)} %add.24.own_p), channel_id=1, source_target_pairs={{0,2},{1,3},{2,0},{3,1},{4,6},{5,7},{6,4},{7,5},{8,10},{9,11},{10,... | collective-permute-start | bytes 786440 | tf_op jit(solution)/shard_map/ppermute | solution.py:358
  57.4 5.1 %collective-permute-start.15 = (f32[224,256]{1,0:T(8,128)S(1)}, f32[224,256]{1,0:T(8,128)S(1)}, u32[]{:S(2)}, u32[]{:S(2)}) collective-permute-start(f32[224,256]{1,0:T(8,128)S(1)} %collective-permute-done.14.near), channel_id=1, source_target_pairs={{0,1},{1,0},{2,3},{3,2},{4,5},{5,4},{6,7},{7,6},{8,9},{9,8},{10,11... | collective-permute-start | bytes 688136 | tf_op jit(solution)/shard_map/ppermute | solution.py:358
  70.9 11.9 %collective-permute-start.17 = (f32[224,256]{1,0:T(8,128)S(1)}, f32[224,256]{1,0:T(8,128)S(1)}, u32[]{:S(2)}, u32[]{:S(2)}) collective-permute-start(f32[224,256]{1,0:T(8,128)S(1)} %get-tuple-element.22), channel_id=1, source_target_pairs={{0,4},{4,0},{8,12},{12,8},{16,20},{20,16},{24,28},{28,24},{1,5},{5... | collective-permute-start | bytes 688136 | tf_op jit(solution)/shard_map/ppermute | solution.py:358
  76.4 10.6 %collective-permute-start.19 = (f32[256,256]{1,0:T(8,128)S(1)}, f32[256,256]{1,0:T(8,128)S(1)}, u32[]{:S(2)}, u32[]{:S(2)}) collective-permute-start(f32[256,256]{1,0:T(8,128)S(1)} %add.25.own_p), channel_id=1, source_target_pairs={{0,4},{4,0},{8,12},{12,8},{16,20},{20,16},{24,28},{28,24},{1,5},{5... | collective-permute-start | bytes 786440 | tf_op jit(solution)/shard_map/ppermute | solution.py:358
  82.8 4.2 %collective-permute-start.18 = (f32[224,256]{1,0:T(8,128)S(1)}, f32[224,256]{1,0:T(8,128)S(1)}, u32[]{:S(2)}, u32[]{:S(2)}) collective-permute-start(f32[224,256]{1,0:T(8,128)S(1)} %collective-permute-done.17.near), channel_id=1, source_target_pairs={{0,1},{1,0},{2,3},{3,2},{4,5},{5,4},{6,7},{7,6},{8,9},{9,8},{10,11... | collective-permute-start | bytes 688136 | tf_op jit(solution)/shard_map/ppermute | solution.py:358
  95.8 8.5 %collective-permute-start.20 = (f32[224,256]{1,0:T(8,128)S(1)}, f32[224,256]{1,0:T(8,128)S(1)}, u32[]{:S(2)}, u32[]{:S(2)}) collective-permute-start(f32[224,256]{1,0:T(8,128)S(1)} %get-tuple-element.25), channel_id=1, source_target_pairs={{0,8},{4,12},{8,0},{12,4},{16,24},{20,28},{24,16},{28,20},{1,9},{5... | collective-permute-start | bytes 688136 | tf_op jit(solution)/shard_map/ppermute | solution.py:358
  95.9 11.8 %collective-permute-start.22 = (f32[256,256]{1,0:T(8,128)S(1)}, f32[256,256]{1,0:T(8,128)S(1)}, u32[]{:S(2)}, u32[]{:S(2)}) collective-permute-start(f32[256,256]{1,0:T(8,128)S(1)} %add.26.own_p), channel_id=1, source_target_pairs={{0,8},{4,12},{8,0},{12,4},{16,24},{20,28},{24,16},{28,20},{1,9},{5... | collective-permute-start | bytes 786440 | tf_op jit(solution)/shard_map/ppermute | solution.py:358
  104.3 3.4 %collective-permute-start.21 = (f32[224,256]{1,0:T(8,128)S(1)}, f32[224,256]{1,0:T(8,128)S(1)}, u32[]{:S(2)}, u32[]{:S(2)}) collective-permute-start(f32[224,256]{1,0:T(8,128)S(1)} %collective-permute-done.20.near), channel_id=1, source_target_pairs={{0,1},{1,0},{2,3},{3,2},{4,5},{5,4},{6,7},{7,6},{8,9},{9,8},{10,11... | collective-permute-start | bytes 688136 | tf_op jit(solution)/shard_map/ppermute | solution.py:358
  116.1 17.0 %collective-permute-start.23 = (f32[224,256]{1,0:T(8,128)S(1)}, f32[224,256]{1,0:T(8,128)S(1)}, u32[]{:S(2)}, u32[]{:S(2)}) collective-permute-start(f32[224,256]{1,0:T(8,128)S(1)} %get-tuple-element.28), channel_id=1, source_target_pairs={{0,16},{4,20},{8,24},{12,28},{16,0},{20,4},{24,8},{28,12},{1,17},{... | collective-permute-start | bytes 688136 | tf_op jit(solution)/shard_map/ppermute | solution.py:358
  117.0 21.6 %collective-permute-start.25 = (f32[256,256]{1,0:T(8,128)S(1)}, f32[256,256]{1,0:T(8,128)S(1)}, u32[]{:S(2)}, u32[]{:S(2)}) collective-permute-start(f32[256,256]{1,0:T(8,128)S(1)} %add.27.own_p), channel_id=1, source_target_pairs={{0,16},{4,20},{8,24},{12,28},{16,0},{20,4},{24,8},{28,12},{1,17},{... | collective-permute-start | bytes 786440 | tf_op jit(solution)/shard_map/ppermute | solution.py:358
  133.1 5.5 %collective-permute-start.24 = (f32[224,256]{1,0:T(8,128)S(1)}, f32[224,256]{1,0:T(8,128)S(1)}, u32[]{:S(2)}, u32[]{:S(2)}) collective-permute-start(f32[224,256]{1,0:T(8,128)S(1)} %collective-permute-done.23.near), channel_id=1, source_target_pairs={{0,1},{1,0},{2,3},{3,2},{4,5},{5,4},{6,7},{7,6},{8,9},{9,8},{10,11... | collective-permute-start | bytes 688136 | tf_op jit(solution)/shard_map/ppermute | solution.py:358

commit v2 on v1

--- a/solution.py
+++ b/solution.py
@@ -12,6 +12,7 @@
 SUB, LANE = 8, 128
 BLOCK = LANE // 2
 PANEL = 2
+SCRATCH_BYTES = 16 * 2**20
 
 
 def split(x):
@@ -275,6 +276,7 @@
         out_shape=[jax.ShapeDtypeStruct((rows, size), F32)] + state_shapes(size),
         in_specs=[SMEM] + [VMEM] * len(arrays),
         out_specs=[VMEM] * 3,
+        compiler_params=pltpu.CompilerParams(vmem_limit_bytes=SCRATCH_BYTES),
         name="first_merge",
     )(side, *near_core(arrays))
 
@@ -292,66 +294,93 @@
         out_specs=[ANY] + [VMEM] * (len(out_shape) - 1),
         scratch_shapes=[pltpu.VMEM((size, size), F32), pltpu.SemaphoreType.DMA(())],
         input_output_aliases={1 + len(arrays): 0} if extra else {},
+        compiler_params=pltpu.CompilerParams(vmem_limit_bytes=SCRATCH_BYTES),
     )(side, *near_core(arrays), *extra)
 
 
-def sample_kernel(keys, place, mask, front, *refs):
-    count = len(keys)
-    chunks, (keep, send, tiles, arrived) = refs[:count], refs[count:]
-    leaf = chunks[0].shape[0]
-    slots = 2 * keep.shape[0]
-    order = [*range(1, slots, 2), *range(0, slots, 2)]
-    present, copies = {}, {}
-    for slot in order:
-        tile_row = place[1] ^ slot
+def load_kernel(keys, place, mask, front, own, rows, own_here, arrived):
+    slots, leaf = rows.shape[:2]
+    own_copy = pltpu.make_async_copy(own, own_here, arrived.at[slots, 0])
+    own_copy.start()
+    tiles = []
+    for slot in range(slots):
         for j, key in enumerate(keys):
-            chunk = place[0] ^ key
+            tile_row, chunk = place[1] ^ slot, place[0] ^ key
             row_tile = place[0] * slots + tile_row
-            col_tile = place[1] * count + chunk
-            present[slot, j] = (mask[tile_row, chunk] != 0) & (row_tile // 2 != col_tile // 2)
-            copies[slot, j] = pltpu.make_async_copy(
+            col_tile = place[1] * len(keys) + chunk
+            present = (mask[tile_row, chunk] != 0) & (row_tile // 2 != col_tile // 2)
+            here = rows.at[slot, :, pl.ds(j * leaf, leaf)]
+            copy = pltpu.make_async_copy(
                 front.at[
                     pl.ds(pl.multiple_of(tile_row * leaf, leaf), leaf),
                     pl.ds(pl.multiple_of(chunk * leaf, leaf), leaf),
                 ],
-                tiles.at[slot, j],
+                here,
                 arrived.at[slot, j],
             )
-
-            @pl.when(present[slot, j])
+            tiles.append((present, copy))
+
+            @pl.when(present)
             def _():
-                copies[slot, j].start()
-
+                copy.start()
+
+            @pl.when(jnp.logical_not(present))
+            def _():
+                here[...] = jnp.zeros(here.shape, BF16)
+
+    for present, copy in tiles:
+
+        @pl.when(present)
+        def _():
+            copy.wait()
+
+    own_copy.wait()
+
+
+def load_front(front, tile_mask, place, own, keys):
+    leaf, size = own.shape
+    slots, width = front.shape[0] // leaf, front.shape[1]
+    small = width * size < 2**20
+    form = pltpu.VMEM if small else jax.ShapeDtypeStruct
+    return pl.pallas_call(
+        functools.partial(load_kernel, keys),
+        out_shape=[form((slots, leaf, width), BF16), form((leaf, size), BF16)],
+        in_specs=[SMEM, SMEM, ANY, ANY],
+        out_specs=[VMEM] * 2,
+        scratch_shapes=[pltpu.SemaphoreType.DMA((slots + 1, len(keys)))],
+        compiler_params=pltpu.CompilerParams(vmem_limit_bytes=SCRATCH_BYTES * (1 if small else 3)),
+        name="load_front",
+    )(
+        place,
+        tile_mask,
+        pltpu.with_memory_space_constraint(front, pltpu.HBM),
+        pltpu.with_memory_space_constraint(own, pltpu.HBM),
+    )
+
+
+def sample_kernel(rows, *refs):
+    chunks, (keep, send) = refs[:-2], refs[-2:]
+    slots = rows.shape[0]
     probes = jnp.concatenate([x[...] for x in chunks], axis=0)
-    for slot in order:
-        for j in range(count):
-
-            @pl.when(present[slot, j])
-            def _():
-                copies[slot, j].wait()
-
-        row = [
-            jnp.where(present[slot, j], tiles[slot, j], jnp.zeros((), BF16)) for j in range(count)
-        ]
+    for slot in [*range(1, slots, 2), *range(0, slots, 2)]:
         out = send if slot % 2 else keep
-        out[slot // 2] = dot(jnp.concatenate(row, axis=1), probes, (1, 0))
-
-
-def all_samples(front, tile_mask, place, chunks, keys):
-    leaf, size = chunks[0].shape
-    slots = front.shape[0] // leaf
-    small = len(keys) * leaf * size < 2**20
+        out[slot // 2] = dot(rows[slot], probes, (1, 0))
+
+
+def all_samples(rows, chunks):
+    slots, leaf, width = rows.shape
+    size = chunks[0].shape[1]
+    small = width * size < 2**20
+    form = pltpu.VMEM if small else jax.ShapeDtypeStruct
+    arrays = [rows, *chunks]
     return pl.pallas_call(
-        functools.partial(sample_kernel, keys),
-        out_shape=[(pltpu.VMEM if small else jax.ShapeDtypeStruct)((slots // 2, leaf, size), F32)] * 2,
-        in_specs=[SMEM, SMEM, ANY] + [VMEM] * len(keys),
+        sample_kernel,
+        out_shape=[form((slots // 2, leaf, size), F32)] * 2,
+        in_specs=[VMEM] * len(arrays),
         out_specs=[VMEM] * 2,
-        scratch_shapes=[
-            pltpu.VMEM((slots, len(keys), leaf, leaf), BF16),
-            pltpu.SemaphoreType.DMA((slots, len(keys))),
-        ],
+        compiler_params=pltpu.CompilerParams(vmem_limit_bytes=SCRATCH_BYTES * (1 if small else 3)),
         name="samples",
-    )(place, tile_mask, front, *(near_core(chunks) if small else chunks))
+    )(*(near_core(arrays) if small else arrays))
 
 
 def swap(x, axis, bit):
@@ -390,7 +419,8 @@
             total_p = own_p[level] + other_p[level]
 
     order = list(chunks)
-    keep, send = all_samples(front, tile_mask, place, [chunks[k] for k in order], order)
+    rows, own_chunk = load_front(front, tile_mask, place, probes, order)
+    keep, send = all_samples(rows, [own_chunk] + [chunks[k] for k in order[1:]])
     got = swap(send, "col", 0)
     slots = {2 * k: (keep[k], got[k]) for k in range(col_count // 2)}
     for bit in range(1, col_levels):

time: 148 us -> 143 us (0.966)
  waiting for transfers between devices: 68.7 us -> 66.2 us
    ppermute x25, waiting for transfers between devices: 68.6 us -> 66.2 us  [swap(): lax.ppermute(x, axis, [(i, i ^ 1 << bit) for i in range(lax.axis_size(axi...]
    pallas_call x1 -> x2, Pallas kernels: 4.85 us -> 4 us  [the longest x1 2.76 us: load_front(): pl.pallas_call(functools.partial(load_kernel, keys), out_shape=[form((slo...]
  transfers between devices with their start and end apart: 26 -> 26, of which waited for: 16 -> 14; matrix products, arithmetic and copies ran while one was open for 1% -> 0% of each run, Pallas kernels for 5% -> 8%
where the time goes in v2:
time: 143 us
  waiting for transfers between devices  66.2 us (46%)
  Pallas kernels  46.4 us (32%)
  starting transfers between devices  28.6 us (20%)
    ppermute x25, waiting for transfers between devices, swap(): lax.ppermute(x, axis, [(i, i ^ 1 << bit) for i in range(lax.axis_size(axi...  66.2 us
    pallas_call x4, Pallas kernels, upper_merge(): pl.pallas_call(functools.partial(upper_kernel, level, is_last, bool(extra...  34.4 us
    ppermute x25, starting transfers between devices, swap(): lax.ppermute(x, axis, [(i, i ^ 1 << bit) for i in range(lax.axis_size(axi...  27.8 us
    pallas_call x1, Pallas kernels, first_merge(): pl.pallas_call(first_kernel, out_shape=[jax.ShapeDtypeStruct((rows, size)...  8.01 us
  transfers between devices with their start and end apart: 26, of which 14 were waited for; matrix products, arithmetic and copies ran while one was open for 0% of the time, Pallas kernels for 8%

profile of v2, /device:TPU:0, one launch (start us, length us, event | category | flops | bytes accessed | tf_op | source)
XLA Modules:
  0.0 143.2 jit_solution(17029618149275443489)
XLA Ops:
  0.6 4.1 %collective-permute-start.1 = (bf16[256,256]{1,0:T(8,128)(2,1)}, bf16[256,256]{1,0:T(8,128)(2,1)S(1)}, u32[]{:S(2)}, u32[]{:S(2)}) collective-permute-start(bf16[256,256]{1,0:T(8,128)(2,1)} %own.1), channel_id=1, source_target_pairs={{0,16},{4,20},{8,24},{12,28},{16,0},{20,4},{24,8},{28,12},{1,17},{... | collective-permute-start | bytes 393224 | tf_op jit(solution)/shard_map/ppermute | solution.py:387
  4.8 1.6 %collective-permute-start.3 = (bf16[256,256]{1,0:T(8,128)(2,1)}, bf16[256,256]{1,0:T(8,128)(2,1)S(1)}, u32[]{:S(2)}, u32[]{:S(2)}) collective-permute-start(bf16[256,256]{1,0:T(8,128)(2,1)} %own.1), channel_id=1, source_target_pairs={{0,8},{4,12},{8,0},{12,4},{16,24},{20,28},{24,16},{28,20},{1,9},{5... | collective-permute-start | bytes 393224 | tf_op jit(solution)/shard_map/ppermute | solution.py:387
  6.3 5.0 %collective-permute-done.1.refs_2_ = bf16[256,256]{1,0:T(8,128)(2,1)S(1)} collective-permute-done((bf16[256,256]{1,0:T(8,128)(2,1)}, bf16[256,256]{1,0:T(8,128)(2,1)S(1)}, u32[]{:S(2)}, u32[]{:S(2)}) %collective-permute-start.1) | collective-permute-done | bytes 131104 | tf_op jit(solution)/shard_map/ppermute | solution.py:387
  11.4 1.6 %collective-permute-start.2 = (bf16[256,256]{1,0:T(8,128)(2,1)S(1)}, bf16[256,256]{1,0:T(8,128)(2,1)S(1)}, u32[]{:S(2)}, u32[]{:S(2)}) collective-permute-start(bf16[256,256]{1,0:T(8,128)(2,1)S(1)} %collective-permute-done.1.refs_2_), channel_id=1, source_target_pairs={{0,4},{4,0},{8,12},{12,8},{16,20},{20,16},{24,28},{28,24},{1,5},{5... | collective-permute-start | bytes 393224 | tf_op jit(solution)/shard_map/ppermute | solution.py:387
  12.9 0.5 collective-permute-start
  13.4 0.7 collective-permute-start.5
  14.1 1.5 %collective-permute-start.4 = (bf16[256,256]{1,0:T(8,128)(2,1)S(1)}, bf16[256,256]{1,0:T(8,128)(2,1)S(1)}, u32[]{:S(2)}, u32[]{:S(2)}) collective-permute-start(bf16[256,256]{1,0:T(8,128)(2,1)S(1)} %collective-permute-done.3.refs_4_), channel_id=1, source_target_pairs={{0,4},{4,0},{8,12},{12,8},{16,20},{20,16},{24,28},{28,24},{1,5},{5... | collective-permute-start | bytes 393224 | tf_op jit(solution)/shard_map/ppermute | solution.py:387
  15.7 2.1 %collective-permute-done.2.refs_3_ = bf16[256,256]{1,0:T(8,128)(2,1)S(1)} collective-permute-done((bf16[256,256]{1,0:T(8,128)(2,1)S(1)}, bf16[256,256]{1,0:T(8,128)(2,1)S(1)}, u32[]{:S(2)}, u32[]{:S(2)}) %collective-permute-start.2) | collective-permute-done | bytes 131104 | tf_op jit(solution)/shard_map/ppermute | solution.py:387
  17.8 0.7 collective-permute-start.6
  18.5 0.1 pad_add_fusion.place
  18.5 0.7 copy-done
  19.2 2.8 %load_front.1 = (bf16[4,256,2048]{2,1,0:T(8,128)(2,1)S(1)}, bf16[256,256]{1,0:T(8,128)(2,1)S(1)}) custom-call(s32[2]{0:T(128)S(1)} %pad_add_fusion.place, s32[4,8]{1,0:T(4,128)S(1)} %copy-done, bf16[1024,2048]{1,0:T(8,128)(2,1)} %front.1, bf16[256,256]{1,0:T(8,128)(2,1)} %own.1), custom_call_target="tpu_custom_call" | custom-call | tf_op jit(solution)/shard_map/load_front/pallas_call | solution.py:345
  22.0 0.0 copy-start.2
  22.0 0.0 copy-start.1
  22.0 0.0 collective-permute-done.refs_1_
  22.1 0.7 collective-permute-done.6.refs_7_
  22.7 1.2 samples.1
  24.0 0.1 collective-permute-start.7
  24.0 1.9 %collective-permute-done.7 = f32[2,256,256]{2,1,0:T(8,128)S(1)} collective-permute-done((f32[2,256,256]{2,1,0:T(8,128)S(1)}, f32[2,256,256]{2,1,0:T(8,128)S(1)}, u32[]{:S(2)}, u32[]{:S(2)}) %collective-permute-start.7) | collective-permute-done | bytes 524320 | tf_op jit(solution)/shard_map/ppermute | solution.py:387
  25.9 0.1 slice_add_fusion
  26.0 1.3 collective-permute-start.8
  27.4 0.8 collective-permute-start.11
  28.2 2.3 %collective-permute-start.9 = (f32[256,256]{1,0:T(8,128)S(1)}, f32[256,256]{1,0:T(8,128)S(1)}, u32[]{:S(2)}, u32[]{:S(2)}) collective-permute-start(f32[256,256]{1,0:T(8,128)S(1)} %get-tuple-element.35.own_a), channel_id=1, source_target_pairs={{0,1},{1,0},{2,3},{3,2},{4,5},{5,4},{6,7},{7,6},{8,9},{9,8},{10,11... | collective-permute-start | bytes 786440 | tf_op jit(solution)/shard_map/ppermute | solution.py:387
  30.6 4.1 %collective-permute-done.8 = f32[1,256,256]{2,1,0:T(8,128)S(1)} collective-permute-done((f32[1,256,256]{2,1,0:T(8,128)S(1)}, f32[1,256,256]{2,1,0:T(8,128)S(1)}, u32[]{:S(2)}, u32[]{:S(2)}) %collective-permute-start.8) | collective-permute-done | bytes 262176 | tf_op jit(solution)/shard_map/ppermute | solution.py:387
  34.7 0.5 collective-permute-start.12
  35.2 0.1 collective-permute-start.13
  35.3 1.1 collective-permute-done.12.other_w
  36.4 8.0 %first_merge.1 = (f32[256,256]{1,0:T(8,128)}, f32[2,224,256]{2,1,0:T(8,128)S(1)}, f32[224,256]{1,0:T(8,128)S(1)}) custom-call(s32[1]{0:T(128)} %bitcast.side, f32[256,256]{1,0:T(8,128)S(1)} %get-tuple-element.35.own_a, f32[256,256]{1,0:T(8,128)S(1)} %bitcast.7, f32[256,256]{1,0:T(8,128)S(1)} %collective-permute-done.9.other_a, ...), custom_call_target="tpu_custom_call" | custom-call | tf_op jit(solution)/shard_map/first_merge/pallas_call | solution.py:274
  44.4 2.6 %collective-permute-start.14 = (f32[224,256]{1,0:T(8,128)S(1)}, f32[224,256]{1,0:T(8,128)S(1)}, u32[]{:S(2)}, u32[]{:S(2)}) collective-permute-start(f32[224,256]{1,0:T(8,128)S(1)} %get-tuple-element.24), channel_id=1, source_target_pairs={{0,2},{1,3},{2,0},{3,1},{4,6},{5,7},{6,4},{7,5},{8,10},{9,11},{10,... | collective-permute-start | bytes 688136 | tf_op jit(solution)/shard_map/ppermute | solution.py:387
  47.0 0.1 collective-permute-start.16
  47.1 6.3 %collective-permute-done.14.near = f32[224,256]{1,0:T(8,128)S(1)} collective-permute-done((f32[224,256]{1,0:T(8,128)S(1)}, f32[224,256]{1,0:T(8,128)S(1)}, u32[]{:S(2)}, u32[]{:S(2)}) %collective-permute-start.14) | collective-permute-done | bytes 229408 | tf_op jit(solution)/shard_map/ppermute | solution.py:387
  53.5 5.1 %collective-permute-done.16.other_p = f32[256,256]{1,0:T(8,128)S(1)} collective-permute-done((f32[256,256]{1,0:T(8,128)S(1)}, f32[256,256]{1,0:T(8,128)S(1)}, u32[]{:S(2)}, u32[]{:S(2)}) %collective-permute-start.16) | collective-permute-done | bytes 262176 | tf_op jit(solution)/shard_map/ppermute | solution.py:387
  58.5 8.5 %shard_map.59 = (f32[4,256,256]{2,1,0:T(8,128)}, f32[2,224,256]{2,1,0:T(8,128)S(1)}, f32[224,256]{1,0:T(8,128)S(1)}) custom-call(s32[1]{0:T(128)} %bitcast.side, f32[2,224,256]{2,1,0:T(8,128)S(1)} %get-tuple-element.23.own, f32[256,256]{1,0:T(8,128)S(1)} %add.24.own_p, f32[224,256]{1,0:T(8,128)S(1)} %collective-permute-done.14.near, ...), custom_call_target="tpu_custom_call" | custom-call | tf_op jit(solution)/shard_map/pallas_call | solution.py:290
  67.0 4.8 %collective-permute-start.17 = (f32[224,256]{1,0:T(8,128)S(1)}, f32[224,256]{1,0:T(8,128)S(1)}, u32[]{:S(2)}, u32[]{:S(2)}) collective-permute-start(f32[224,256]{1,0:T(8,128)S(1)} %get-tuple-element.26), channel_id=1, source_target_pairs={{0,4},{4,0},{8,12},{12,8},{16,20},{20,16},{24,28},{28,24},{1,5},{5... | collective-permute-start | bytes 688136 | tf_op jit(solution)/shard_map/ppermute | solution.py:387
  71.9 0.1 collective-permute-start.19
  72.0 6.3 %collective-permute-done.17.near = f32[224,256]{1,0:T(8,128)S(1)} collective-permute-done((f32[224,256]{1,0:T(8,128)S(1)}, f32[224,256]{1,0:T(8,128)S(1)}, u32[]{:S(2)}, u32[]{:S(2)}) %collective-permute-start.17) | collective-permute-done | bytes 229408 | tf_op jit(solution)/shard_map/ppermute | solution.py:387
  78.3 4.2 %collective-permute-done.19.other_p = f32[256,256]{1,0:T(8,128)S(1)} collective-permute-done((f32[256,256]{1,0:T(8,128)S(1)}, f32[256,256]{1,0:T(8,128)S(1)}, u32[]{:S(2)}, u32[]{:S(2)}) %collective-permute-start.19) | collective-permute-done | bytes 262176 | tf_op jit(solution)/shard_map/ppermute | solution.py:387
  82.5 8.7 %shard_map.60 = (f32[4,256,256]{2,1,0:T(8,128)}, f32[2,224,256]{2,1,0:T(8,128)S(1)}, f32[224,256]{1,0:T(8,128)S(1)}) custom-call(s32[1]{0:T(128)} %bitcast.side, f32[2,224,256]{2,1,0:T(8,128)S(1)} %get-tuple-element.25.own, f32[256,256]{1,0:T(8,128)S(1)} %add.25.own_p, f32[224,256]{1,0:T(8,128)S(1)} %collective-permute-done.17.near, ...), custom_call_target="tpu_custom_call", output_to_operand_aliasing={{0}: (6, {})} | custom-call | tf_op jit(solution)/shard_map/pallas_call | solution.py:290
  91.2 0.1 collective-permute-start.20
  91.3 2.1 %collective-permute-start.22 = (f32[256,256]{1,0:T(8,128)S(1)}, f32[256,256]{1,0:T(8,128)S(1)}, u32[]{:S(2)}, u32[]{:S(2)}) collective-permute-start(f32[256,256]{1,0:T(8,128)S(1)} %add.26.own_p), channel_id=1, source_target_pairs={{0,8},{4,12},{8,0},{12,4},{16,24},{20,28},{24,16},{28,20},{1,9},{5... | collective-permute-start | bytes 786440 | tf_op jit(solution)/shard_map/ppermute | solution.py:387
  93.4 6.3 %collective-permute-done.20.near = f32[224,256]{1,0:T(8,128)S(1)} collective-permute-done((f32[224,256]{1,0:T(8,128)S(1)}, f32[224,256]{1,0:T(8,128)S(1)}, u32[]{:S(2)}, u32[]{:S(2)}) %collective-permute-start.20) | collective-permute-done | bytes 229408 | tf_op jit(solution)/shard_map/ppermute | solution.py:387
  99.8 3.4 %collective-permute-done.22.other_p = f32[256,256]{1,0:T(8,128)S(1)} collective-permute-done((f32[256,256]{1,0:T(8,128)S(1)}, f32[256,256]{1,0:T(8,128)S(1)}, u32[]{:S(2)}, u32[]{:S(2)}) %collective-permute-start.22) | collective-permute-done | bytes 262176 | tf_op jit(solution)/shard_map/ppermute | solution.py:387
  103.1 8.5 %shard_map.61 = (f32[4,256,256]{2,1,0:T(8,128)}, f32[2,224,256]{2,1,0:T(8,128)S(1)}, f32[224,256]{1,0:T(8,128)S(1)}) custom-call(s32[1]{0:T(128)} %bitcast.side, f32[2,224,256]{2,1,0:T(8,128)S(1)} %get-tuple-element.28.own, f32[256,256]{1,0:T(8,128)S(1)} %add.26.own_p, f32[224,256]{1,0:T(8,128)S(1)} %collective-permute-done.20.near, ...), custom_call_target="tpu_custom_call", output_to_operand_aliasing={{0}: (6, {})} | custom-call | tf_op jit(solution)/shard_map/pallas_call | solution.py:290
  111.6 1.0 collective-permute-start.23
  112.7 2.0 %collective-permute-start.25 = (f32[256,256]{1,0:T(8,128)S(1)}, f32[256,256]{1,0:T(8,128)S(1)}, u32[]{:S(2)}, u32[]{:S(2)}) collective-permute-start(f32[256,256]{1,0:T(8,128)S(1)} %add.27.own_p), channel_id=1, source_target_pairs={{0,16},{4,20},{8,24},{12,28},{16,0},{20,4},{24,8},{28,12},{1,17},{... | collective-permute-start | bytes 786440 | tf_op jit(solution)/shard_map/ppermute | solution.py:387
  114.7 14.0 %collective-permute-done.23.near = f32[224,256]{1,0:T(8,128)S(1)} collective-permute-done((f32[224,256]{1,0:T(8,128)S(1)}, f32[224,256]{1,0:T(8,128)S(1)}, u32[]{:S(2)}, u32[]{:S(2)}) %collective-permute-start.23) | collective-permute-done | bytes 229408 | tf_op jit(solution)/shard_map/ppermute | solution.py:387
  128.7 5.5 %collective-permute-done.25.other_p = f32[256,256]{1,0:T(8,128)S(1)} collective-permute-done((f32[256,256]{1,0:T(8,128)S(1)}, f32[256,256]{1,0:T(8,128)S(1)}, u32[]{:S(2)}, u32[]{:S(2)}) %collective-permute-start.25) | collective-permute-done | bytes 262176 | tf_op jit(solution)/shard_map/ppermute | solution.py:387
  134.2 8.7 %shard_map.62 = f32[4,256,256]{2,1,0:T(8,128)} custom-call(s32[1]{0:T(128)} %bitcast.side, f32[2,224,256]{2,1,0:T(8,128)S(1)} %get-tuple-element.31.own, f32[256,256]{1,0:T(8,128)S(1)} %add.27.own_p, f32[224,256]{1,0:T(8,128)S(1)} %collective-permute-done.23.near, f32[224,256]{1,0:T(8,128)S(1)} %collective-permute-done.24.far, ...), custom_call_target="tpu_custom_call", output_to_operand_aliasing={{}: (6, {})} | custom-call | tf_op jit(solution)/shard_map/pallas_call | solution.py:290
  (23 shorter events, 0.2 us)
Async XLA Ops:
  0.6 10.8 %collective-permute-start.1 = (bf16[256,256]{1,0:T(8,128)(2,1)}, bf16[256,256]{1,0:T(8,128)(2,1)S(1)}, u32[]{:S(2)}, u32[]{:S(2)}) collective-permute-start(bf16[256,256]{1,0:T(8,128)(2,1)} %own.1), channel_id=1, source_target_pairs={{0,16},{4,20},{8,24},{12,28},{16,0},{20,4},{24,8},{28,12},{1,17},{... | collective-permute-start | bytes 393224 | tf_op jit(solution)/shard_map/ppermute | solution.py:387
  4.8 9.4 %collective-permute-start.3 = (bf16[256,256]{1,0:T(8,128)(2,1)}, bf16[256,256]{1,0:T(8,128)(2,1)S(1)}, u32[]{:S(2)}, u32[]{:S(2)}) collective-permute-start(bf16[256,256]{1,0:T(8,128)(2,1)} %own.1), channel_id=1, source_target_pairs={{0,8},{4,12},{8,0},{12,4},{16,24},{20,28},{24,16},{28,20},{1,9},{5... | collective-permute-start | bytes 393224 | tf_op jit(solution)/shard_map/ppermute | solution.py:387
  11.4 6.4 %collective-permute-start.2 = (bf16[256,256]{1,0:T(8,128)(2,1)S(1)}, bf16[256,256]{1,0:T(8,128)(2,1)S(1)}, u32[]{:S(2)}, u32[]{:S(2)}) collective-permute-start(bf16[256,256]{1,0:T(8,128)(2,1)S(1)} %collective-permute-done.1.refs_2_), channel_id=1, source_target_pairs={{0,4},{4,0},{8,12},{12,8},{16,20},{20,16},{24,28},{28,24},{1,5},{5... | collective-permute-start | bytes 393224 | tf_op jit(solution)/shard_map/ppermute | solution.py:387
  12.9 9.1 %collective-permute-start = (bf16[256,256]{1,0:T(8,128)(2,1)}, bf16[256,256]{1,0:T(8,128)(2,1)S(1)}, u32[]{:S(2)}, u32[]{:S(2)}) collective-permute-start(bf16[256,256]{1,0:T(8,128)(2,1)} %own.1), channel_id=1, source_target_pairs={{0,4},{4,0},{8,12},{12,8},{16,20},{20,16},{24,28},{28,24},{1,5},{5... | collective-permute-start | bytes 393224 | tf_op jit(solution)/shard_map/ppermute | solution.py:387
  13.4 8.6 %collective-permute-start.5 = (bf16[256,256]{1,0:T(8,128)(2,1)S(1)}, bf16[256,256]{1,0:T(8,128)(2,1)S(1)}, u32[]{:S(2)}, u32[]{:S(2)}) collective-permute-start(bf16[256,256]{1,0:T(8,128)(2,1)S(1)} %collective-permute-done.1.refs_2_), channel_id=1, source_target_pairs={{0,8},{4,12},{8,0},{12,4},{16,24},{20,28},{24,16},{28,20},{1,9},{5... | collective-permute-start | bytes 393224 | tf_op jit(solution)/shard_map/ppermute | solution.py:387
  14.1 7.9 %collective-permute-start.4 = (bf16[256,256]{1,0:T(8,128)(2,1)S(1)}, bf16[256,256]{1,0:T(8,128)(2,1)S(1)}, u32[]{:S(2)}, u32[]{:S(2)}) collective-permute-start(bf16[256,256]{1,0:T(8,128)(2,1)S(1)} %collective-permute-done.3.refs_4_), channel_id=1, source_target_pairs={{0,4},{4,0},{8,12},{12,8},{16,20},{20,16},{24,28},{28,24},{1,5},{5... | collective-permute-start | bytes 393224 | tf_op jit(solution)/shard_map/ppermute | solution.py:387
  17.8 5.0 %collective-permute-start.6 = (bf16[256,256]{1,0:T(8,128)(2,1)S(1)}, bf16[256,256]{1,0:T(8,128)(2,1)S(1)}, u32[]{:S(2)}, u32[]{:S(2)}) collective-permute-start(bf16[256,256]{1,0:T(8,128)(2,1)S(1)} %collective-permute-done.2.refs_3_), channel_id=1, source_target_pairs={{0,8},{4,12},{8,0},{12,4},{16,24},{20,28},{24,16},{28,20},{1,9},{5... | collective-permute-start | bytes 393224 | tf_op jit(solution)/shard_map/ppermute | solution.py:387
  18.5 0.7 copy-start
  22.0 5.4 %copy-start.2 = (bf16[256,256]{1,0:T(8,128)(2,1)S(1)}, bf16[256,256]{1,0:T(8,128)(2,1)}, u32[]{:S(2)}) copy-start(bf16[256,256]{1,0:T(8,128)(2,1)} %own.1) | copy-start | bytes 393220
  22.0 13.2 %copy-start.1 = (f32[256,256]{1,0:T(8,128)S(1)}, f32[256,256]{1,0:T(8,128)}, u32[]{:S(2)}) copy-start(f32[256,256]{1,0:T(8,128)} %param.7) | copy-start | bytes 786436
  24.0 2.0 %collective-permute-start.7 = (f32[2,256,256]{2,1,0:T(8,128)S(1)}, f32[2,256,256]{2,1,0:T(8,128)S(1)}, u32[]{:S(2)}, u32[]{:S(2)}) collective-permute-start(f32[2,256,256]{2,1,0:T(8,128)S(1)} %get-tuple-element.21), channel_id=1, source_target_pairs={{0,1},{1,0},{2,3},{3,2},{4,5},{5,4},{6,7},{7,6},{8,9},{9,8},{10,11... | collective-permute-start | bytes 1572872 | tf_op jit(solution)/shard_map/ppermute | solution.py:387
  26.0 8.7 %collective-permute-start.8 = (f32[1,256,256]{2,1,0:T(8,128)S(1)}, f32[1,256,256]{2,1,0:T(8,128)S(1)}, u32[]{:S(2)}, u32[]{:S(2)}) collective-permute-start(f32[1,256,256]{2,1,0:T(8,128)S(1)} %get-tuple-element.34), channel_id=1, source_target_pairs={{0,2},{1,3},{2,0},{3,1},{4,6},{5,7},{6,4},{7,5},{8,10},{9,11},{10,... | collective-permute-start | bytes 786440 | tf_op jit(solution)/shard_map/ppermute | solution.py:387
  27.4 7.3 %collective-permute-start.11 = (bf16[256,256]{1,0:T(8,128)(2,1)S(1)}, bf16[256,256]{1,0:T(8,128)(2,1)S(1)}, u32[]{:S(2)}, u32[]{:S(2)}) collective-permute-start(bf16[256,256]{1,0:T(8,128)(2,1)S(1)} %copy-done.2), channel_id=1, source_target_pairs={{0,0},{4,1},{8,2},{12,3},{16,4},{20,5},{24,6},{28,7},{1,8},{5,9},{... | collective-permute-start | bytes 393224 | tf_op jit(solution)/shard_map/ppermute | solution.py:412
  28.2 8.2 %collective-permute-start.9 = (f32[256,256]{1,0:T(8,128)S(1)}, f32[256,256]{1,0:T(8,128)S(1)}, u32[]{:S(2)}, u32[]{:S(2)}) collective-permute-start(f32[256,256]{1,0:T(8,128)S(1)} %get-tuple-element.35.own_a), channel_id=1, source_target_pairs={{0,1},{1,0},{2,3},{3,2},{4,5},{5,4},{6,7},{7,6},{8,9},{9,8},{10,11... | collective-permute-start | bytes 786440 | tf_op jit(solution)/shard_map/ppermute | solution.py:387
  34.7 1.7 %collective-permute-start.10 = (f32[256,256]{1,0:T(8,128)S(1)}, f32[256,256]{1,0:T(8,128)S(1)}, u32[]{:S(2)}, u32[]{:S(2)}) collective-permute-start(f32[256,256]{1,0:T(8,128)S(1)} %bitcast.6), channel_id=1, source_target_pairs={{0,1},{1,0},{2,3},{3,2},{4,5},{5,4},{6,7},{7,6},{8,9},{9,8},{10,11... | collective-permute-start | bytes 786440 | tf_op jit(solution)/shard_map/ppermute | solution.py:387
  34.7 1.7 %collective-permute-start.12 = (bf16[256,256]{1,0:T(8,128)(2,1)S(1)}, bf16[256,256]{1,0:T(8,128)(2,1)S(1)}, u32[]{:S(2)}, u32[]{:S(2)}) collective-permute-start(bf16[256,256]{1,0:T(8,128)(2,1)S(1)} %collective-permute-done.11.own_w), channel_id=1, source_target_pairs={{0,1},{1,0},{2,3},{3,2},{4,5},{5,4},{6,7},{7,6},{8,9},{9,8},{10,11... | collective-permute-start | bytes 393224 | tf_op jit(solution)/shard_map/ppermute | solution.py:387
  35.2 11.8 %collective-permute-start.13 = (f32[256,256]{1,0:T(8,128)S(1)}, f32[256,256]{1,0:T(8,128)S(1)}, u32[]{:S(2)}, u32[]{:S(2)}) collective-permute-start(f32[256,256]{1,0:T(8,128)S(1)} %copy-done.1), channel_id=1, source_target_pairs={{0,1},{1,0},{2,3},{3,2},{4,5},{5,4},{6,7},{7,6},{8,9},{9,8},{10,11... | collective-permute-start | bytes 786440 | tf_op jit(solution)/shard_map/ppermute | solution.py:387
  44.4 9.0 %collective-permute-start.14 = (f32[224,256]{1,0:T(8,128)S(1)}, f32[224,256]{1,0:T(8,128)S(1)}, u32[]{:S(2)}, u32[]{:S(2)}) collective-permute-start(f32[224,256]{1,0:T(8,128)S(1)} %get-tuple-element.24), channel_id=1, source_target_pairs={{0,2},{1,3},{2,0},{3,1},{4,6},{5,7},{6,4},{7,5},{8,10},{9,11},{10,... | collective-permute-start | bytes 688136 | tf_op jit(solution)/shard_map/ppermute | solution.py:387
  47.0 11.5 %collective-permute-start.16 = (f32[256,256]{1,0:T(8,128)S(1)}, f32[256,256]{1,0:T(8,128)S(1)}, u32[]{:S(2)}, u32[]{:S(2)}) collective-permute-start(f32[256,256]{1,0:T(8,128)S(1)} %add.24.own_p), channel_id=1, source_target_pairs={{0,2},{1,3},{2,0},{3,1},{4,6},{5,7},{6,4},{7,5},{8,10},{9,11},{10,... | collective-permute-start | bytes 786440 | tf_op jit(solution)/shard_map/ppermute | solution.py:387
  53.5 5.1 %collective-permute-start.15 = (f32[224,256]{1,0:T(8,128)S(1)}, f32[224,256]{1,0:T(8,128)S(1)}, u32[]{:S(2)}, u32[]{:S(2)}) collective-permute-start(f32[224,256]{1,0:T(8,128)S(1)} %collective-permute-done.14.near), channel_id=1, source_target_pairs={{0,1},{1,0},{2,3},{3,2},{4,5},{5,4},{6,7},{7,6},{8,9},{9,8},{10,11... | collective-permute-start | bytes 688136 | tf_op jit(solution)/shard_map/ppermute | solution.py:387
  67.0 11.3 %collective-permute-start.17 = (f32[224,256]{1,0:T(8,128)S(1)}, f32[224,256]{1,0:T(8,128)S(1)}, u32[]{:S(2)}, u32[]{:S(2)}) collective-permute-start(f32[224,256]{1,0:T(8,128)S(1)} %get-tuple-element.26), channel_id=1, source_target_pairs={{0,4},{4,0},{8,12},{12,8},{16,20},{20,16},{24,28},{28,24},{1,5},{5... | collective-permute-start | bytes 688136 | tf_op jit(solution)/shard_map/ppermute | solution.py:387
  71.9 10.6 %collective-permute-start.19 = (f32[256,256]{1,0:T(8,128)S(1)}, f32[256,256]{1,0:T(8,128)S(1)}, u32[]{:S(2)}, u32[]{:S(2)}) collective-permute-start(f32[256,256]{1,0:T(8,128)S(1)} %add.25.own_p), channel_id=1, source_target_pairs={{0,4},{4,0},{8,12},{12,8},{16,20},{20,16},{24,28},{28,24},{1,5},{5... | collective-permute-start | bytes 786440 | tf_op jit(solution)/shard_map/ppermute | solution.py:387
  78.3 4.2 %collective-permute-start.18 = (f32[224,256]{1,0:T(8,128)S(1)}, f32[224,256]{1,0:T(8,128)S(1)}, u32[]{:S(2)}, u32[]{:S(2)}) collective-permute-start(f32[224,256]{1,0:T(8,128)S(1)} %collective-permute-done.17.near), channel_id=1, source_target_pairs={{0,1},{1,0},{2,3},{3,2},{4,5},{5,4},{6,7},{7,6},{8,9},{9,8},{10,11... | collective-permute-start | bytes 688136 | tf_op jit(solution)/shard_map/ppermute | solution.py:387
  91.2 8.5 %collective-permute-start.20 = (f32[224,256]{1,0:T(8,128)S(1)}, f32[224,256]{1,0:T(8,128)S(1)}, u32[]{:S(2)}, u32[]{:S(2)}) collective-permute-start(f32[224,256]{1,0:T(8,128)S(1)} %get-tuple-element.29), channel_id=1, source_target_pairs={{0,8},{4,12},{8,0},{12,4},{16,24},{20,28},{24,16},{28,20},{1,9},{5... | collective-permute-start | bytes 688136 | tf_op jit(solution)/shard_map/ppermute | solution.py:387
  91.3 11.8 %collective-permute-start.22 = (f32[256,256]{1,0:T(8,128)S(1)}, f32[256,256]{1,0:T(8,128)S(1)}, u32[]{:S(2)}, u32[]{:S(2)}) collective-permute-start(f32[256,256]{1,0:T(8,128)S(1)} %add.26.own_p), channel_id=1, source_target_pairs={{0,8},{4,12},{8,0},{12,4},{16,24},{20,28},{24,16},{28,20},{1,9},{5... | collective-permute-start | bytes 786440 | tf_op jit(solution)/shard_map/ppermute | solution.py:387
  99.8 3.4 %collective-permute-start.21 = (f32[224,256]{1,0:T(8,128)S(1)}, f32[224,256]{1,0:T(8,128)S(1)}, u32[]{:S(2)}, u32[]{:S(2)}) collective-permute-start(f32[224,256]{1,0:T(8,128)S(1)} %collective-permute-done.20.near), channel_id=1, source_target_pairs={{0,1},{1,0},{2,3},{3,2},{4,5},{5,4},{6,7},{7,6},{8,9},{9,8},{10,11... | collective-permute-start | bytes 688136 | tf_op jit(solution)/shard_map/ppermute | solution.py:387
  111.6 17.1 %collective-permute-start.23 = (f32[224,256]{1,0:T(8,128)S(1)}, f32[224,256]{1,0:T(8,128)S(1)}, u32[]{:S(2)}, u32[]{:S(2)}) collective-permute-start(f32[224,256]{1,0:T(8,128)S(1)} %get-tuple-element.32), channel_id=1, source_target_pairs={{0,16},{4,20},{8,24},{12,28},{16,0},{20,4},{24,8},{28,12},{1,17},{... | collective-permute-start | bytes 688136 | tf_op jit(solution)/shard_map/ppermute | solution.py:387
  112.7 21.5 %collective-permute-start.25 = (f32[256,256]{1,0:T(8,128)S(1)}, f32[256,256]{1,0:T(8,128)S(1)}, u32[]{:S(2)}, u32[]{:S(2)}) collective-permute-start(f32[256,256]{1,0:T(8,128)S(1)} %add.27.own_p), channel_id=1, source_target_pairs={{0,16},{4,20},{8,24},{12,28},{16,0},{20,4},{24,8},{28,12},{1,17},{... | collective-permute-start | bytes 786440 | tf_op jit(solution)/shard_map/ppermute | solution.py:387
  128.7 5.5 %collective-permute-start.24 = (f32[224,256]{1,0:T(8,128)S(1)}, f32[224,256]{1,0:T(8,128)S(1)}, u32[]{:S(2)}, u32[]{:S(2)}) collective-permute-start(f32[224,256]{1,0:T(8,128)S(1)} %collective-permute-done.23.near), channel_id=1, source_target_pairs={{0,1},{1,0},{2,3},{3,2},{4,5},{5,4},{6,7},{7,6},{8,9},{9,8},{10,11... | collective-permute-start | bytes 688136 | tf_op jit(solution)/shard_map/ppermute | solution.py:387

commit v3 on v2

--- a/solution.py
+++ b/solution.py
@@ -406,11 +406,9 @@
             else:
                 chunks[new] = swap(chunks[key], "row", bit)
 
-    pairs = [
-        ((b % row_count) * col_count + b // row_count, b) for b in range(row_count * col_count)
-    ]
-    own_w = lax.ppermute(probes, ("row", "col"), pairs)
-    other_w = swap(own_w, "col", 0)
+    home = [((b % row_count) * col_count + b // row_count, b) for b in range(row_count * col_count)]
+    own_w = lax.ppermute(probes, ("row", "col"), home)
+    other_w = lax.ppermute(probes, ("row", "col"), [(at, b ^ 1) for at, b in home])
 
     own_p, other_p, total_p = {}, {}, coupling
     for level, (axis, bit) in enumerate(bits, start=1):

time: 143 us -> 154 us (1.077)
  waiting for transfers between devices: 66.2 us -> 72.3 us
  starting transfers between devices: 28.6 us -> 33.6 us
    ppermute x1 -> x2, waiting for transfers between devices: 0.01 us -> 4.17 us  [the longest x1 4.17 us: step(): lax.ppermute(probes, ('row', 'col'), [(at, b ^ 1) for at, b in home])]
    ppermute x25 -> x24, starting transfers between devices: 27.8 us -> 30.6 us  [swap(): lax.ppermute(x, axis, [(i, i ^ 1 << bit) for i in range(lax.axis_size(axi...]
    ppermute x1 -> x2, starting transfers between devices: 0.84 us -> 2.97 us  [the longest x1 2.31 us: step(): lax.ppermute(probes, ('row', 'col'), [(at, b ^ 1) for at, b in home])]
    ppermute x25 -> x24, waiting for transfers between devices: 66.2 us -> 68.1 us  [swap(): lax.ppermute(x, axis, [(i, i ^ 1 << bit) for i in range(lax.axis_size(axi...]
  transfers between devices with their start and end apart: 26 -> 26, of which waited for: 14 -> 14; matrix products, arithmetic and copies ran while one was open for 0% -> 0% of each run, Pallas kernels for 8% -> 7%
where the time goes in v3:
time: 154 us
  waiting for transfers between devices  72.3 us (47%)
  Pallas kernels  46.4 us (30%)
  starting transfers between devices  33.6 us (22%)
    ppermute x24, waiting for transfers between devices, swap(): lax.ppermute(x, axis, [(i, i ^ 1 << bit) for i in range(lax.axis_size(axi...  68.1 us
    pallas_call x4, Pallas kernels, upper_merge(): pl.pallas_call(functools.partial(upper_kernel, level, is_last, bool(extra...  34.4 us
    ppermute x24, starting transfers between devices, swap(): lax.ppermute(x, axis, [(i, i ^ 1 << bit) for i in range(lax.axis_size(axi...  30.6 us
    pallas_call x1, Pallas kernels, first_merge(): pl.pallas_call(first_kernel, out_shape=[jax.ShapeDtypeStruct((rows, size)...  8.01 us
    ppermute x1, waiting for transfers between devices, step(): lax.ppermute(probes, ('row', 'col'), [(at, b ^ 1) for at, b in home])  4.17 us
  transfers between devices with their start and end apart: 26, of which 14 were waited for; matrix products, arithmetic and copies ran while one was open for 0% of the time, Pallas kernels for 7%

profile of v3, /device:TPU:0, one launch (start us, length us, event | category | flops | bytes accessed | tf_op | source)
XLA Modules:
  0.0 154.2 jit_solution(10891791161773965574)
XLA Ops:
  0.6 4.1 %collective-permute-start.1 = (bf16[256,256]{1,0:T(8,128)(2,1)}, bf16[256,256]{1,0:T(8,128)(2,1)S(1)}, u32[]{:S(2)}, u32[]{:S(2)}) collective-permute-start(bf16[256,256]{1,0:T(8,128)(2,1)} %own.1), channel_id=1, source_target_pairs={{0,16},{4,20},{8,24},{12,28},{16,0},{20,4},{24,8},{28,12},{1,17},{... | collective-permute-start | bytes 393224 | tf_op jit(solution)/shard_map/ppermute | solution.py:387
  4.8 1.6 %collective-permute-start.3 = (bf16[256,256]{1,0:T(8,128)(2,1)}, bf16[256,256]{1,0:T(8,128)(2,1)S(1)}, u32[]{:S(2)}, u32[]{:S(2)}) collective-permute-start(bf16[256,256]{1,0:T(8,128)(2,1)} %own.1), channel_id=1, source_target_pairs={{0,8},{4,12},{8,0},{12,4},{16,24},{20,28},{24,16},{28,20},{1,9},{5... | collective-permute-start | bytes 393224 | tf_op jit(solution)/shard_map/ppermute | solution.py:387
  6.3 5.0 %collective-permute-done.1.refs_2_ = bf16[256,256]{1,0:T(8,128)(2,1)S(1)} collective-permute-done((bf16[256,256]{1,0:T(8,128)(2,1)}, bf16[256,256]{1,0:T(8,128)(2,1)S(1)}, u32[]{:S(2)}, u32[]{:S(2)}) %collective-permute-start.1) | collective-permute-done | bytes 131104 | tf_op jit(solution)/shard_map/ppermute | solution.py:387
  11.4 1.6 %collective-permute-start.2 = (bf16[256,256]{1,0:T(8,128)(2,1)S(1)}, bf16[256,256]{1,0:T(8,128)(2,1)S(1)}, u32[]{:S(2)}, u32[]{:S(2)}) collective-permute-start(bf16[256,256]{1,0:T(8,128)(2,1)S(1)} %collective-permute-done.1.refs_2_), channel_id=1, source_target_pairs={{0,4},{4,0},{8,12},{12,8},{16,20},{20,16},{24,28},{28,24},{1,5},{5... | collective-permute-start | bytes 393224 | tf_op jit(solution)/shard_map/ppermute | solution.py:387
  12.9 0.5 collective-permute-start
  13.4 0.7 collective-permute-start.5
  14.1 1.5 collective-permute-start.4
  15.7 2.1 %collective-permute-done.2.refs_3_ = bf16[256,256]{1,0:T(8,128)(2,1)S(1)} collective-permute-done((bf16[256,256]{1,0:T(8,128)(2,1)S(1)}, bf16[256,256]{1,0:T(8,128)(2,1)S(1)}, u32[]{:S(2)}, u32[]{:S(2)}) %collective-permute-start.2) | collective-permute-done | bytes 131104 | tf_op jit(solution)/shard_map/ppermute | solution.py:387
  17.8 0.7 collective-permute-start.6
  18.5 0.1 pad_add_fusion.place
  18.5 0.7 copy-done
  19.2 2.8 %load_front.1 = (bf16[4,256,2048]{2,1,0:T(8,128)(2,1)S(1)}, bf16[256,256]{1,0:T(8,128)(2,1)S(1)}) custom-call(s32[2]{0:T(128)S(1)} %pad_add_fusion.place, s32[4,8]{1,0:T(4,128)S(1)} %copy-done, bf16[1024,2048]{1,0:T(8,128)(2,1)} %front.1, bf16[256,256]{1,0:T(8,128)(2,1)} %own.1), custom_call_target="tpu_custom_call" | custom-call | tf_op jit(solution)/shard_map/load_front/pallas_call | solution.py:345
  22.0 0.0 copy-start.2
  22.0 0.0 copy-start.1
  22.0 0.0 collective-permute-done.refs_1_
  22.0 0.0 collective-permute-done.5.refs_6_
  22.1 0.7 collective-permute-done.6.refs_7_
  22.7 1.2 samples.1
  24.0 0.1 collective-permute-start.7
  24.0 1.9 %collective-permute-done.7 = f32[2,256,256]{2,1,0:T(8,128)S(1)} collective-permute-done((f32[2,256,256]{2,1,0:T(8,128)S(1)}, f32[2,256,256]{2,1,0:T(8,128)S(1)}, u32[]{:S(2)}, u32[]{:S(2)}) %collective-permute-start.7) | collective-permute-done | bytes 524320 | tf_op jit(solution)/shard_map/ppermute | solution.py:387
  25.9 0.1 slice_add_fusion
  26.0 1.3 collective-permute-start.8
  27.4 7.1 %collective-permute-done.8 = f32[1,256,256]{2,1,0:T(8,128)S(1)} collective-permute-done((f32[1,256,256]{2,1,0:T(8,128)S(1)}, f32[1,256,256]{2,1,0:T(8,128)S(1)}, u32[]{:S(2)}, u32[]{:S(2)}) %collective-permute-start.8) | collective-permute-done | bytes 262176 | tf_op jit(solution)/shard_map/ppermute | solution.py:387
  34.4 0.7 collective-permute-start.11
  35.1 2.3 %collective-permute-start.12 = (bf16[256,256]{1,0:T(8,128)(2,1)S(1)}, bf16[256,256]{1,0:T(8,128)(2,1)S(1)}, u32[]{:S(2)}, u32[]{:S(2)}) collective-permute-start(bf16[256,256]{1,0:T(8,128)(2,1)S(1)} %copy-done.2), channel_id=1, source_target_pairs={{0,1},{4,0},{8,3},{12,2},{16,5},{20,4},{24,7},{28,6},{1,9},{5,8},{... | collective-permute-start | bytes 393224 | tf_op jit(solution)/shard_map/ppermute | solution.py:411
  37.4 1.2 collective-permute-start.13
  38.6 4.2 %collective-permute-done.12.other_w = bf16[256,256]{1,0:T(8,128)(2,1)S(1)} collective-permute-done((bf16[256,256]{1,0:T(8,128)(2,1)S(1)}, bf16[256,256]{1,0:T(8,128)(2,1)S(1)}, u32[]{:S(2)}, u32[]{:S(2)}) %collective-permute-start.12) | collective-permute-done | bytes 131104 | tf_op jit(solution)/shard_map/ppermute | solution.py:411
  42.8 8.0 %first_merge.1 = (f32[256,256]{1,0:T(8,128)}, f32[2,224,256]{2,1,0:T(8,128)S(1)}, f32[224,256]{1,0:T(8,128)S(1)}) custom-call(s32[1]{0:T(128)} %bitcast.side, f32[256,256]{1,0:T(8,128)S(1)} %get-tuple-element.35.own_a, f32[256,256]{1,0:T(8,128)S(1)} %bitcast.7, f32[256,256]{1,0:T(8,128)S(1)} %collective-permute-done.9.other_a, ...), custom_call_target="tpu_custom_call" | custom-call | tf_op jit(solution)/shard_map/first_merge/pallas_call | solution.py:274
  50.8 5.5 %collective-permute-start.14 = (f32[224,256]{1,0:T(8,128)S(1)}, f32[224,256]{1,0:T(8,128)S(1)}, u32[]{:S(2)}, u32[]{:S(2)}) collective-permute-start(f32[224,256]{1,0:T(8,128)S(1)} %get-tuple-element.24), channel_id=1, source_target_pairs={{0,2},{1,3},{2,0},{3,1},{4,6},{5,7},{6,4},{7,5},{8,10},{9,11},{10,... | collective-permute-start | bytes 688136 | tf_op jit(solution)/shard_map/ppermute | solution.py:387
  56.4 0.1 collective-permute-start.16
  56.4 6.3 %collective-permute-done.14.near = f32[224,256]{1,0:T(8,128)S(1)} collective-permute-done((f32[224,256]{1,0:T(8,128)S(1)}, f32[224,256]{1,0:T(8,128)S(1)}, u32[]{:S(2)}, u32[]{:S(2)}) %collective-permute-start.14) | collective-permute-done | bytes 229408 | tf_op jit(solution)/shard_map/ppermute | solution.py:387
  62.8 5.0 %collective-permute-done.16.other_p = f32[256,256]{1,0:T(8,128)S(1)} collective-permute-done((f32[256,256]{1,0:T(8,128)S(1)}, f32[256,256]{1,0:T(8,128)S(1)}, u32[]{:S(2)}, u32[]{:S(2)}) %collective-permute-start.16) | collective-permute-done | bytes 262176 | tf_op jit(solution)/shard_map/ppermute | solution.py:387
  67.8 8.5 %shard_map.59 = (f32[4,256,256]{2,1,0:T(8,128)}, f32[2,224,256]{2,1,0:T(8,128)S(1)}, f32[224,256]{1,0:T(8,128)S(1)}) custom-call(s32[1]{0:T(128)} %bitcast.side, f32[2,224,256]{2,1,0:T(8,128)S(1)} %get-tuple-element.23.own, f32[256,256]{1,0:T(8,128)S(1)} %add.24.own_p, f32[224,256]{1,0:T(8,128)S(1)} %collective-permute-done.14.near, ...), custom_call_target="tpu_custom_call" | custom-call | tf_op jit(solution)/shard_map/pallas_call | solution.py:290
  76.2 6.4 %collective-permute-start.17 = (f32[224,256]{1,0:T(8,128)S(1)}, f32[224,256]{1,0:T(8,128)S(1)}, u32[]{:S(2)}, u32[]{:S(2)}) collective-permute-start(f32[224,256]{1,0:T(8,128)S(1)} %get-tuple-element.26), channel_id=1, source_target_pairs={{0,4},{4,0},{8,12},{12,8},{16,20},{20,16},{24,28},{28,24},{1,5},{5... | collective-permute-start | bytes 688136 | tf_op jit(solution)/shard_map/ppermute | solution.py:387
  82.7 0.1 collective-permute-start.19
  82.8 6.3 %collective-permute-done.17.near = f32[224,256]{1,0:T(8,128)S(1)} collective-permute-done((f32[224,256]{1,0:T(8,128)S(1)}, f32[224,256]{1,0:T(8,128)S(1)}, u32[]{:S(2)}, u32[]{:S(2)}) %collective-permute-start.17) | collective-permute-done | bytes 229408 | tf_op jit(solution)/shard_map/ppermute | solution.py:387
  89.1 4.2 %collective-permute-done.19.other_p = f32[256,256]{1,0:T(8,128)S(1)} collective-permute-done((f32[256,256]{1,0:T(8,128)S(1)}, f32[256,256]{1,0:T(8,128)S(1)}, u32[]{:S(2)}, u32[]{:S(2)}) %collective-permute-start.19) | collective-permute-done | bytes 262176 | tf_op jit(solution)/shard_map/ppermute | solution.py:387
  93.3 8.7 %shard_map.60 = (f32[4,256,256]{2,1,0:T(8,128)}, f32[2,224,256]{2,1,0:T(8,128)S(1)}, f32[224,256]{1,0:T(8,128)S(1)}) custom-call(s32[1]{0:T(128)} %bitcast.side, f32[2,224,256]{2,1,0:T(8,128)S(1)} %get-tuple-element.25.own, f32[256,256]{1,0:T(8,128)S(1)} %add.25.own_p, f32[224,256]{1,0:T(8,128)S(1)} %collective-permute-done.17.near, ...), custom_call_target="tpu_custom_call", output_to_operand_aliasing={{0}: (6, {})} | custom-call | tf_op jit(solution)/shard_map/pallas_call | solution.py:290
  102.0 1.1 collective-permute-start.20
  103.1 1.1 collective-permute-start.22
  104.2 6.3 %collective-permute-done.20.near = f32[224,256]{1,0:T(8,128)S(1)} collective-permute-done((f32[224,256]{1,0:T(8,128)S(1)}, f32[224,256]{1,0:T(8,128)S(1)}, u32[]{:S(2)}, u32[]{:S(2)}) %collective-permute-start.20) | collective-permute-done | bytes 229408 | tf_op jit(solution)/shard_map/ppermute | solution.py:387
  110.5 3.3 %collective-permute-done.22.other_p = f32[256,256]{1,0:T(8,128)S(1)} collective-permute-done((f32[256,256]{1,0:T(8,128)S(1)}, f32[256,256]{1,0:T(8,128)S(1)}, u32[]{:S(2)}, u32[]{:S(2)}) %collective-permute-start.22) | collective-permute-done | bytes 262176 | tf_op jit(solution)/shard_map/ppermute | solution.py:387
  113.8 8.5 %shard_map.61 = (f32[4,256,256]{2,1,0:T(8,128)}, f32[2,224,256]{2,1,0:T(8,128)S(1)}, f32[224,256]{1,0:T(8,128)S(1)}) custom-call(s32[1]{0:T(128)} %bitcast.side, f32[2,224,256]{2,1,0:T(8,128)S(1)} %get-tuple-element.28.own, f32[256,256]{1,0:T(8,128)S(1)} %add.26.own_p, f32[224,256]{1,0:T(8,128)S(1)} %collective-permute-done.20.near, ...), custom_call_target="tpu_custom_call", output_to_operand_aliasing={{0}: (6, {})} | custom-call | tf_op jit(solution)/shard_map/pallas_call | solution.py:290
  122.3 1.2 collective-permute-start.23
  123.6 1.8 %collective-permute-start.25 = (f32[256,256]{1,0:T(8,128)S(1)}, f32[256,256]{1,0:T(8,128)S(1)}, u32[]{:S(2)}, u32[]{:S(2)}) collective-permute-start(f32[256,256]{1,0:T(8,128)S(1)} %add.27.own_p), channel_id=1, source_target_pairs={{0,16},{4,20},{8,24},{12,28},{16,0},{20,4},{24,8},{28,12},{1,17},{... | collective-permute-start | bytes 786440 | tf_op jit(solution)/shard_map/ppermute | solution.py:387
  125.4 14.8 %collective-permute-done.23.near = f32[224,256]{1,0:T(8,128)S(1)} collective-permute-done((f32[224,256]{1,0:T(8,128)S(1)}, f32[224,256]{1,0:T(8,128)S(1)}, u32[]{:S(2)}, u32[]{:S(2)}) %collective-permute-start.23) | collective-permute-done | bytes 229408 | tf_op jit(solution)/shard_map/ppermute | solution.py:387
  140.2 5.0 %collective-permute-done.25.other_p = f32[256,256]{1,0:T(8,128)S(1)} collective-permute-done((f32[256,256]{1,0:T(8,128)S(1)}, f32[256,256]{1,0:T(8,128)S(1)}, u32[]{:S(2)}, u32[]{:S(2)}) %collective-permute-start.25) | collective-permute-done | bytes 262176 | tf_op jit(solution)/shard_map/ppermute | solution.py:387
  145.2 8.7 %shard_map.62 = f32[4,256,256]{2,1,0:T(8,128)} custom-call(s32[1]{0:T(128)} %bitcast.side, f32[2,224,256]{2,1,0:T(8,128)S(1)} %get-tuple-element.31.own, f32[256,256]{1,0:T(8,128)S(1)} %add.27.own_p, f32[224,256]{1,0:T(8,128)S(1)} %collective-permute-done.23.near, f32[224,256]{1,0:T(8,128)S(1)} %collective-permute-done.24.far, ...), custom_call_target="tpu_custom_call", output_to_operand_aliasing={{}: (6, {})} | custom-call | tf_op jit(solution)/shard_map/pallas_call | solution.py:290
  (23 shorter events, 0.2 us)
Async XLA Ops:
  0.6 10.8 %collective-permute-start.1 = (bf16[256,256]{1,0:T(8,128)(2,1)}, bf16[256,256]{1,0:T(8,128)(2,1)S(1)}, u32[]{:S(2)}, u32[]{:S(2)}) collective-permute-start(bf16[256,256]{1,0:T(8,128)(2,1)} %own.1), channel_id=1, source_target_pairs={{0,16},{4,20},{8,24},{12,28},{16,0},{20,4},{24,8},{28,12},{1,17},{... | collective-permute-start | bytes 393224 | tf_op jit(solution)/shard_map/ppermute | solution.py:387
  4.8 9.4 %collective-permute-start.3 = (bf16[256,256]{1,0:T(8,128)(2,1)}, bf16[256,256]{1,0:T(8,128)(2,1)S(1)}, u32[]{:S(2)}, u32[]{:S(2)}) collective-permute-start(bf16[256,256]{1,0:T(8,128)(2,1)} %own.1), channel_id=1, source_target_pairs={{0,8},{4,12},{8,0},{12,4},{16,24},{20,28},{24,16},{28,20},{1,9},{5... | collective-permute-start | bytes 393224 | tf_op jit(solution)/shard_map/ppermute | solution.py:387
  11.4 6.4 %collective-permute-start.2 = (bf16[256,256]{1,0:T(8,128)(2,1)S(1)}, bf16[256,256]{1,0:T(8,128)(2,1)S(1)}, u32[]{:S(2)}, u32[]{:S(2)}) collective-permute-start(bf16[256,256]{1,0:T(8,128)(2,1)S(1)} %collective-permute-done.1.refs_2_), channel_id=1, source_target_pairs={{0,4},{4,0},{8,12},{12,8},{16,20},{20,16},{24,28},{28,24},{1,5},{5... | collective-permute-start | bytes 393224 | tf_op jit(solution)/shard_map/ppermute | solution.py:387
  12.9 9.1 %collective-permute-start = (bf16[256,256]{1,0:T(8,128)(2,1)}, bf16[256,256]{1,0:T(8,128)(2,1)S(1)}, u32[]{:S(2)}, u32[]{:S(2)}) collective-permute-start(bf16[256,256]{1,0:T(8,128)(2,1)} %own.1), channel_id=1, source_target_pairs={{0,4},{4,0},{8,12},{12,8},{16,20},{20,16},{24,28},{28,24},{1,5},{5... | collective-permute-start | bytes 393224 | tf_op jit(solution)/shard_map/ppermute | solution.py:387
  13.4 8.6 %collective-permute-start.5 = (bf16[256,256]{1,0:T(8,128)(2,1)S(1)}, bf16[256,256]{1,0:T(8,128)(2,1)S(1)}, u32[]{:S(2)}, u32[]{:S(2)}) collective-permute-start(bf16[256,256]{1,0:T(8,128)(2,1)S(1)} %collective-permute-done.1.refs_2_), channel_id=1, source_target_pairs={{0,8},{4,12},{8,0},{12,4},{16,24},{20,28},{24,16},{28,20},{1,9},{5... | collective-permute-start | bytes 393224 | tf_op jit(solution)/shard_map/ppermute | solution.py:387
  14.1 7.9 %collective-permute-start.4 = (bf16[256,256]{1,0:T(8,128)(2,1)S(1)}, bf16[256,256]{1,0:T(8,128)(2,1)S(1)}, u32[]{:S(2)}, u32[]{:S(2)}) collective-permute-start(bf16[256,256]{1,0:T(8,128)(2,1)S(1)} %collective-permute-done.3.refs_4_), channel_id=1, source_target_pairs={{0,4},{4,0},{8,12},{12,8},{16,20},{20,16},{24,28},{28,24},{1,5},{5... | collective-permute-start | bytes 393224 | tf_op jit(solution)/shard_map/ppermute | solution.py:387
  17.8 5.0 %collective-permute-start.6 = (bf16[256,256]{1,0:T(8,128)(2,1)S(1)}, bf16[256,256]{1,0:T(8,128)(2,1)S(1)}, u32[]{:S(2)}, u32[]{:S(2)}) collective-permute-start(bf16[256,256]{1,0:T(8,128)(2,1)S(1)} %collective-permute-done.2.refs_3_), channel_id=1, source_target_pairs={{0,8},{4,12},{8,0},{12,4},{16,24},{20,28},{24,16},{28,20},{1,9},{5... | collective-permute-start | bytes 393224 | tf_op jit(solution)/shard_map/ppermute | solution.py:387
  18.5 0.7 copy-start
  22.0 12.4 %copy-start.2 = (bf16[256,256]{1,0:T(8,128)(2,1)S(1)}, bf16[256,256]{1,0:T(8,128)(2,1)}, u32[]{:S(2)}) copy-start(bf16[256,256]{1,0:T(8,128)(2,1)} %own.1) | copy-start | bytes 393220
  22.0 15.4 %copy-start.1 = (f32[256,256]{1,0:T(8,128)S(1)}, f32[256,256]{1,0:T(8,128)}, u32[]{:S(2)}) copy-start(f32[256,256]{1,0:T(8,128)} %param.7) | copy-start | bytes 786436
  24.0 2.0 %collective-permute-start.7 = (f32[2,256,256]{2,1,0:T(8,128)S(1)}, f32[2,256,256]{2,1,0:T(8,128)S(1)}, u32[]{:S(2)}, u32[]{:S(2)}) collective-permute-start(f32[2,256,256]{2,1,0:T(8,128)S(1)} %get-tuple-element.21), channel_id=1, source_target_pairs={{0,1},{1,0},{2,3},{3,2},{4,5},{5,4},{6,7},{7,6},{8,9},{9,8},{10,11... | collective-permute-start | bytes 1572872 | tf_op jit(solution)/shard_map/ppermute | solution.py:387
  26.0 8.4 %collective-permute-start.8 = (f32[1,256,256]{2,1,0:T(8,128)S(1)}, f32[1,256,256]{2,1,0:T(8,128)S(1)}, u32[]{:S(2)}, u32[]{:S(2)}) collective-permute-start(f32[1,256,256]{2,1,0:T(8,128)S(1)} %get-tuple-element.34), channel_id=1, source_target_pairs={{0,2},{1,3},{2,0},{3,1},{4,6},{5,7},{6,4},{7,5},{8,10},{9,11},{10,... | collective-permute-start | bytes 786440 | tf_op jit(solution)/shard_map/ppermute | solution.py:387
  27.4 15.4 %collective-permute-start.9 = (f32[256,256]{1,0:T(8,128)S(1)}, f32[256,256]{1,0:T(8,128)S(1)}, u32[]{:S(2)}, u32[]{:S(2)}) collective-permute-start(f32[256,256]{1,0:T(8,128)S(1)} %get-tuple-element.35.own_a), channel_id=1, source_target_pairs={{0,1},{1,0},{2,3},{3,2},{4,5},{5,4},{6,7},{7,6},{8,9},{9,8},{10,11... | collective-permute-start | bytes 786440 | tf_op jit(solution)/shard_map/ppermute | solution.py:387
  34.4 8.4 %collective-permute-start.10 = (f32[256,256]{1,0:T(8,128)S(1)}, f32[256,256]{1,0:T(8,128)S(1)}, u32[]{:S(2)}, u32[]{:S(2)}) collective-permute-start(f32[256,256]{1,0:T(8,128)S(1)} %bitcast.6), channel_id=1, source_target_pairs={{0,1},{1,0},{2,3},{3,2},{4,5},{5,4},{6,7},{7,6},{8,9},{9,8},{10,11... | collective-permute-start | bytes 786440 | tf_op jit(solution)/shard_map/ppermute | solution.py:387
  34.4 4.2 %collective-permute-start.11 = (bf16[256,256]{1,0:T(8,128)(2,1)S(1)}, bf16[256,256]{1,0:T(8,128)(2,1)S(1)}, u32[]{:S(2)}, u32[]{:S(2)}) collective-permute-start(bf16[256,256]{1,0:T(8,128)(2,1)S(1)} %copy-done.2), channel_id=1, source_target_pairs={{0,0},{4,1},{8,2},{12,3},{16,4},{20,5},{24,6},{28,7},{1,8},{5,9},{... | collective-permute-start | bytes 393224 | tf_op jit(solution)/shard_map/ppermute | solution.py:410
  35.1 7.7 %collective-permute-start.12 = (bf16[256,256]{1,0:T(8,128)(2,1)S(1)}, bf16[256,256]{1,0:T(8,128)(2,1)S(1)}, u32[]{:S(2)}, u32[]{:S(2)}) collective-permute-start(bf16[256,256]{1,0:T(8,128)(2,1)S(1)} %copy-done.2), channel_id=1, source_target_pairs={{0,1},{4,0},{8,3},{12,2},{16,5},{20,4},{24,7},{28,6},{1,9},{5,8},{... | collective-permute-start | bytes 393224 | tf_op jit(solution)/shard_map/ppermute | solution.py:411
  37.4 18.9 %collective-permute-start.13 = (f32[256,256]{1,0:T(8,128)S(1)}, f32[256,256]{1,0:T(8,128)S(1)}, u32[]{:S(2)}, u32[]{:S(2)}) collective-permute-start(f32[256,256]{1,0:T(8,128)S(1)} %copy-done.1), channel_id=1, source_target_pairs={{0,1},{1,0},{2,3},{3,2},{4,5},{5,4},{6,7},{7,6},{8,9},{9,8},{10,11... | collective-permute-start | bytes 786440 | tf_op jit(solution)/shard_map/ppermute | solution.py:387
  50.8 11.9 %collective-permute-start.14 = (f32[224,256]{1,0:T(8,128)S(1)}, f32[224,256]{1,0:T(8,128)S(1)}, u32[]{:S(2)}, u32[]{:S(2)}) collective-permute-start(f32[224,256]{1,0:T(8,128)S(1)} %get-tuple-element.24), channel_id=1, source_target_pairs={{0,2},{1,3},{2,0},{3,1},{4,6},{5,7},{6,4},{7,5},{8,10},{9,11},{10,... | collective-permute-start | bytes 688136 | tf_op jit(solution)/shard_map/ppermute | solution.py:387
  56.4 11.4 %collective-permute-start.16 = (f32[256,256]{1,0:T(8,128)S(1)}, f32[256,256]{1,0:T(8,128)S(1)}, u32[]{:S(2)}, u32[]{:S(2)}) collective-permute-start(f32[256,256]{1,0:T(8,128)S(1)} %add.24.own_p), channel_id=1, source_target_pairs={{0,2},{1,3},{2,0},{3,1},{4,6},{5,7},{6,4},{7,5},{8,10},{9,11},{10,... | collective-permute-start | bytes 786440 | tf_op jit(solution)/shard_map/ppermute | solution.py:387
  62.8 5.0 %collective-permute-start.15 = (f32[224,256]{1,0:T(8,128)S(1)}, f32[224,256]{1,0:T(8,128)S(1)}, u32[]{:S(2)}, u32[]{:S(2)}) collective-permute-start(f32[224,256]{1,0:T(8,128)S(1)} %collective-permute-done.14.near), channel_id=1, source_target_pairs={{0,1},{1,0},{2,3},{3,2},{4,5},{5,4},{6,7},{7,6},{8,9},{9,8},{10,11... | collective-permute-start | bytes 688136 | tf_op jit(solution)/shard_map/ppermute | solution.py:387
  76.2 12.9 %collective-permute-start.17 = (f32[224,256]{1,0:T(8,128)S(1)}, f32[224,256]{1,0:T(8,128)S(1)}, u32[]{:S(2)}, u32[]{:S(2)}) collective-permute-start(f32[224,256]{1,0:T(8,128)S(1)} %get-tuple-element.26), channel_id=1, source_target_pairs={{0,4},{4,0},{8,12},{12,8},{16,20},{20,16},{24,28},{28,24},{1,5},{5... | collective-permute-start | bytes 688136 | tf_op jit(solution)/shard_map/ppermute | solution.py:387
  82.7 10.6 %collective-permute-start.19 = (f32[256,256]{1,0:T(8,128)S(1)}, f32[256,256]{1,0:T(8,128)S(1)}, u32[]{:S(2)}, u32[]{:S(2)}) collective-permute-start(f32[256,256]{1,0:T(8,128)S(1)} %add.25.own_p), channel_id=1, source_target_pairs={{0,4},{4,0},{8,12},{12,8},{16,20},{20,16},{24,28},{28,24},{1,5},{5... | collective-permute-start | bytes 786440 | tf_op jit(solution)/shard_map/ppermute | solution.py:387
  89.1 4.2 %collective-permute-start.18 = (f32[224,256]{1,0:T(8,128)S(1)}, f32[224,256]{1,0:T(8,128)S(1)}, u32[]{:S(2)}, u32[]{:S(2)}) collective-permute-start(f32[224,256]{1,0:T(8,128)S(1)} %collective-permute-done.17.near), channel_id=1, source_target_pairs={{0,1},{1,0},{2,3},{3,2},{4,5},{5,4},{6,7},{7,6},{8,9},{9,8},{10,11... | collective-permute-start | bytes 688136 | tf_op jit(solution)/shard_map/ppermute | solution.py:387
  102.0 8.5 %collective-permute-start.20 = (f32[224,256]{1,0:T(8,128)S(1)}, f32[224,256]{1,0:T(8,128)S(1)}, u32[]{:S(2)}, u32[]{:S(2)}) collective-permute-start(f32[224,256]{1,0:T(8,128)S(1)} %get-tuple-element.29), channel_id=1, source_target_pairs={{0,8},{4,12},{8,0},{12,4},{16,24},{20,28},{24,16},{28,20},{1,9},{5... | collective-permute-start | bytes 688136 | tf_op jit(solution)/shard_map/ppermute | solution.py:387
  103.1 10.8 %collective-permute-start.22 = (f32[256,256]{1,0:T(8,128)S(1)}, f32[256,256]{1,0:T(8,128)S(1)}, u32[]{:S(2)}, u32[]{:S(2)}) collective-permute-start(f32[256,256]{1,0:T(8,128)S(1)} %add.26.own_p), channel_id=1, source_target_pairs={{0,8},{4,12},{8,0},{12,4},{16,24},{20,28},{24,16},{28,20},{1,9},{5... | collective-permute-start | bytes 786440 | tf_op jit(solution)/shard_map/ppermute | solution.py:387
  110.5 3.3 %collective-permute-start.21 = (f32[224,256]{1,0:T(8,128)S(1)}, f32[224,256]{1,0:T(8,128)S(1)}, u32[]{:S(2)}, u32[]{:S(2)}) collective-permute-start(f32[224,256]{1,0:T(8,128)S(1)} %collective-permute-done.20.near), channel_id=1, source_target_pairs={{0,1},{1,0},{2,3},{3,2},{4,5},{5,4},{6,7},{7,6},{8,9},{9,8},{10,11... | collective-permute-start | bytes 688136 | tf_op jit(solution)/shard_map/ppermute | solution.py:387
  122.3 17.9 %collective-permute-start.23 = (f32[224,256]{1,0:T(8,128)S(1)}, f32[224,256]{1,0:T(8,128)S(1)}, u32[]{:S(2)}, u32[]{:S(2)}) collective-permute-start(f32[224,256]{1,0:T(8,128)S(1)} %get-tuple-element.32), channel_id=1, source_target_pairs={{0,16},{4,20},{8,24},{12,28},{16,0},{20,4},{24,8},{28,12},{1,17},{... | collective-permute-start | bytes 688136 | tf_op jit(solution)/shard_map/ppermute | solution.py:387
  123.6 21.7 %collective-permute-start.25 = (f32[256,256]{1,0:T(8,128)S(1)}, f32[256,256]{1,0:T(8,128)S(1)}, u32[]{:S(2)}, u32[]{:S(2)}) collective-permute-start(f32[256,256]{1,0:T(8,128)S(1)} %add.27.own_p), channel_id=1, source_target_pairs={{0,16},{4,20},{8,24},{12,28},{16,0},{20,4},{24,8},{28,12},{1,17},{... | collective-permute-start | bytes 786440 | tf_op jit(solution)/shard_map/ppermute | solution.py:387
  140.2 5.0 %collective-permute-start.24 = (f32[224,256]{1,0:T(8,128)S(1)}, f32[224,256]{1,0:T(8,128)S(1)}, u32[]{:S(2)}, u32[]{:S(2)}) collective-permute-start(f32[224,256]{1,0:T(8,128)S(1)} %collective-permute-done.23.near), channel_id=1, source_target_pairs={{0,1},{1,0},{2,3},{3,2},{4,5},{5,4},{6,7},{7,6},{8,9},{9,8},{10,11... | collective-permute-start | bytes 688136 | tf_op jit(solution)/shard_map/ppermute | solution.py:387

commit v4 on v3

--- a/solution.py
+++ b/solution.py
@@ -130,11 +130,9 @@
         high, low = two_parts(jnp.where(mine, 0.0, both))
         low_here = pltpu.roll(low, BLOCK, 1)
         left = jnp.concatenate([jnp.where(mine, low_here, high), high], axis=1).astype(BF16)
-        right = [dot(left, four(x[i]), (1, 0)) for x in rights]
-        for x, y in zip(solved, right):
-            x.append(y)
         row = both
         if i + 1 < count:
+            row = dot(left, four(blocks[i][:, first:]), (1, 0))
             high_here = pltpu.roll(high, BLOCK, 1)
             across = jnp.concatenate([high_here, low_here, high_here], axis=1).astype(BF16)
             below = jnp.concatenate([blocks[j][:, tile] for j in range(i + 1, count)], axis=0)
@@ -144,7 +142,6 @@
                 jnp.concatenate([across, across], axis=0),
                 (1, 1),
             )
-            row = dot(left, four(blocks[i][:, first:]), (1, 0))
             high, low = two_parts(column)
             near = lax.broadcasted_iota(jnp.int32, column.shape, 1) < BLOCK
             column = jnp.concatenate(
@@ -157,8 +154,10 @@
                 if first:
                     new = jnp.concatenate([blocks[j][:, :first], new], axis=1)
                 blocks[j] = new
-            for x, y in zip(rights, right):
-                change = dot(column, four(y), (1, 0))
+        for x, y in zip(rights, solved):
+            y.append(dot(left, four(x[i]), (1, 0)))
+            if i + 1 < count:
+                change = dot(column, four(y[i]), (1, 0))
                 for j in range(i + 1, count):
                     at = BLOCK * (j - i - 1)
                     x[j] = x[j] - change[at : at + BLOCK, :]
@@ -408,7 +407,7 @@
 
     home = [((b % row_count) * col_count + b // row_count, b) for b in range(row_count * col_count)]
     own_w = lax.ppermute(probes, ("row", "col"), home)
-    other_w = lax.ppermute(probes, ("row", "col"), [(at, b ^ 1) for at, b in home])
+    other_w = swap(own_w, "col", 0)
 
     own_p, other_p, total_p = {}, {}, coupling
     for level, (axis, bit) in enumerate(bits, start=1):

time: 154 us -> 143 us (0.929)
  waiting for transfers between devices: 72.3 us -> 66.2 us
  starting transfers between devices: 33.6 us -> 28.6 us
    ppermute x1 -> x0, waiting for transfers between devices: 4.17 us -> none  [step(): lax.ppermute(probes, ('row', 'col'), [(at, b ^ 1) for at, b in home])]
    ppermute x24 -> x25, starting transfers between devices: 30.6 us -> 27.8 us  [swap(): lax.ppermute(x, axis, [(i, i ^ 1 << bit) for i in range(lax.axis_size(axi...]
    ppermute x1 -> x0, starting transfers between devices: 2.31 us -> none  [step(): lax.ppermute(probes, ('row', 'col'), [(at, b ^ 1) for at, b in home])]
    ppermute x24 -> x25, waiting for transfers between devices: 68.1 us -> 66.2 us  [swap(): lax.ppermute(x, axis, [(i, i ^ 1 << bit) for i in range(lax.axis_size(axi...]
where the time goes in v4:
time: 143 us; the launch traced here: 142 us
  waiting for transfers between devices  66.2 us (46%)
  Pallas kernels  45.6 us (32%)
  starting transfers between devices  28.6 us (20%)
    ppermute x25, waiting for transfers between devices, swap(): lax.ppermute(x, axis, [(i, i ^ 1 << bit) for i in range(lax.axis_size(axi...  66.2 us
    pallas_call x4, Pallas kernels, upper_merge(): pl.pallas_call(functools.partial(upper_kernel, level, is_last, bool(extra...  33.7 us
    ppermute x25, starting transfers between devices, swap(): lax.ppermute(x, axis, [(i, i ^ 1 << bit) for i in range(lax.axis_size(axi...  27.8 us
    pallas_call x1, Pallas kernels, first_merge(): pl.pallas_call(first_kernel, out_shape=[jax.ShapeDtypeStruct((rows, size)...  7.9 us
  transfers between devices with their start and end apart: 26, of which 14 were waited for; matrix products, arithmetic and copies ran while one was open for 0% of the time, Pallas kernels for 7%

profile of v4, /device:TPU:0, one launch (start us, length us, event | category | flops | bytes accessed | tf_op | source)
XLA Modules:
  0.0 142.4 jit_solution(797155136118030075)
XLA Ops:
  0.6 4.1 %collective-permute-start.1 = (bf16[256,256]{1,0:T(8,128)(2,1)}, bf16[256,256]{1,0:T(8,128)(2,1)S(1)}, u32[]{:S(2)}, u32[]{:S(2)}) collective-permute-start(bf16[256,256]{1,0:T(8,128)(2,1)} %own.1), channel_id=1, source_target_pairs={{0,16},{4,20},{8,24},{12,28},{16,0},{20,4},{24,8},{28,12},{1,17},{... | collective-permute-start | bytes 393224 | tf_op jit(solution)/shard_map/ppermute | solution.py:386
  4.8 1.6 %collective-permute-start.3 = (bf16[256,256]{1,0:T(8,128)(2,1)}, bf16[256,256]{1,0:T(8,128)(2,1)S(1)}, u32[]{:S(2)}, u32[]{:S(2)}) collective-permute-start(bf16[256,256]{1,0:T(8,128)(2,1)} %own.1), channel_id=1, source_target_pairs={{0,8},{4,12},{8,0},{12,4},{16,24},{20,28},{24,16},{28,20},{1,9},{5... | collective-permute-start | bytes 393224 | tf_op jit(solution)/shard_map/ppermute | solution.py:386
  6.3 5.0 %collective-permute-done.1.refs_2_ = bf16[256,256]{1,0:T(8,128)(2,1)S(1)} collective-permute-done((bf16[256,256]{1,0:T(8,128)(2,1)}, bf16[256,256]{1,0:T(8,128)(2,1)S(1)}, u32[]{:S(2)}, u32[]{:S(2)}) %collective-permute-start.1) | collective-permute-done | bytes 131104 | tf_op jit(solution)/shard_map/ppermute | solution.py:386
  11.4 1.6 %collective-permute-start.2 = (bf16[256,256]{1,0:T(8,128)(2,1)S(1)}, bf16[256,256]{1,0:T(8,128)(2,1)S(1)}, u32[]{:S(2)}, u32[]{:S(2)}) collective-permute-start(bf16[256,256]{1,0:T(8,128)(2,1)S(1)} %collective-permute-done.1.refs_2_), channel_id=1, source_target_pairs={{0,4},{4,0},{8,12},{12,8},{16,20},{20,16},{24,28},{28,24},{1,5},{5... | collective-permute-start | bytes 393224 | tf_op jit(solution)/shard_map/ppermute | solution.py:386
  12.9 0.5 collective-permute-start
  13.4 0.7 collective-permute-start.5
  14.1 1.5 %collective-permute-start.4 = (bf16[256,256]{1,0:T(8,128)(2,1)S(1)}, bf16[256,256]{1,0:T(8,128)(2,1)S(1)}, u32[]{:S(2)}, u32[]{:S(2)}) collective-permute-start(bf16[256,256]{1,0:T(8,128)(2,1)S(1)} %collective-permute-done.3.refs_4_), channel_id=1, source_target_pairs={{0,4},{4,0},{8,12},{12,8},{16,20},{20,16},{24,28},{28,24},{1,5},{5... | collective-permute-start | bytes 393224 | tf_op jit(solution)/shard_map/ppermute | solution.py:386
  15.7 2.1 %collective-permute-done.2.refs_3_ = bf16[256,256]{1,0:T(8,128)(2,1)S(1)} collective-permute-done((bf16[256,256]{1,0:T(8,128)(2,1)S(1)}, bf16[256,256]{1,0:T(8,128)(2,1)S(1)}, u32[]{:S(2)}, u32[]{:S(2)}) %collective-permute-start.2) | collective-permute-done | bytes 131104 | tf_op jit(solution)/shard_map/ppermute | solution.py:386
  17.8 0.7 collective-permute-start.6
  18.5 0.1 pad_add_fusion.place
  18.5 0.7 copy-done
  19.2 2.8 %load_front.1 = (bf16[4,256,2048]{2,1,0:T(8,128)(2,1)S(1)}, bf16[256,256]{1,0:T(8,128)(2,1)S(1)}) custom-call(s32[2]{0:T(128)S(1)} %pad_add_fusion.place, s32[4,8]{1,0:T(4,128)S(1)} %copy-done, bf16[1024,2048]{1,0:T(8,128)(2,1)} %front.1, bf16[256,256]{1,0:T(8,128)(2,1)} %own.1), custom_call_target="tpu_custom_call" | custom-call | tf_op jit(solution)/shard_map/load_front/pallas_call | solution.py:344
  22.0 0.0 copy-start.2
  22.0 0.0 copy-start.1
  22.0 0.0 collective-permute-done.refs_1_
  22.1 0.7 collective-permute-done.6.refs_7_
  22.7 1.2 samples.1
  24.0 0.1 collective-permute-start.7
  24.0 1.9 %collective-permute-done.7 = f32[2,256,256]{2,1,0:T(8,128)S(1)} collective-permute-done((f32[2,256,256]{2,1,0:T(8,128)S(1)}, f32[2,256,256]{2,1,0:T(8,128)S(1)}, u32[]{:S(2)}, u32[]{:S(2)}) %collective-permute-start.7) | collective-permute-done | bytes 524320 | tf_op jit(solution)/shard_map/ppermute | solution.py:386
  25.9 0.1 slice_add_fusion
  26.0 1.3 collective-permute-start.8
  27.4 0.8 collective-permute-start.11
  28.2 2.3 %collective-permute-start.9 = (f32[256,256]{1,0:T(8,128)S(1)}, f32[256,256]{1,0:T(8,128)S(1)}, u32[]{:S(2)}, u32[]{:S(2)}) collective-permute-start(f32[256,256]{1,0:T(8,128)S(1)} %get-tuple-element.35.own_a), channel_id=1, source_target_pairs={{0,1},{1,0},{2,3},{3,2},{4,5},{5,4},{6,7},{7,6},{8,9},{9,8},{10,11... | collective-permute-start | bytes 786440 | tf_op jit(solution)/shard_map/ppermute | solution.py:386
  30.6 4.1 %collective-permute-done.8 = f32[1,256,256]{2,1,0:T(8,128)S(1)} collective-permute-done((f32[1,256,256]{2,1,0:T(8,128)S(1)}, f32[1,256,256]{2,1,0:T(8,128)S(1)}, u32[]{:S(2)}, u32[]{:S(2)}) %collective-permute-start.8) | collective-permute-done | bytes 262176 | tf_op jit(solution)/shard_map/ppermute | solution.py:386
  34.7 0.5 collective-permute-start.12
  35.2 0.1 collective-permute-start.13
  35.3 1.1 collective-permute-done.12.other_w
  36.4 7.9 %first_merge.1 = (f32[256,256]{1,0:T(8,128)}, f32[2,224,256]{2,1,0:T(8,128)S(1)}, f32[224,256]{1,0:T(8,128)S(1)}) custom-call(s32[1]{0:T(128)} %bitcast.side, f32[256,256]{1,0:T(8,128)S(1)} %get-tuple-element.35.own_a, f32[256,256]{1,0:T(8,128)S(1)} %bitcast.7, f32[256,256]{1,0:T(8,128)S(1)} %collective-permute-done.9.other_a, ...), custom_call_target="tpu_custom_call" | custom-call | tf_op jit(solution)/shard_map/first_merge/pallas_call | solution.py:273
  44.3 2.6 %collective-permute-start.14 = (f32[224,256]{1,0:T(8,128)S(1)}, f32[224,256]{1,0:T(8,128)S(1)}, u32[]{:S(2)}, u32[]{:S(2)}) collective-permute-start(f32[224,256]{1,0:T(8,128)S(1)} %get-tuple-element.24), channel_id=1, source_target_pairs={{0,2},{1,3},{2,0},{3,1},{4,6},{5,7},{6,4},{7,5},{8,10},{9,11},{10,... | collective-permute-start | bytes 688136 | tf_op jit(solution)/shard_map/ppermute | solution.py:386
  46.9 0.1 collective-permute-start.16
  47.0 6.3 %collective-permute-done.14.near = f32[224,256]{1,0:T(8,128)S(1)} collective-permute-done((f32[224,256]{1,0:T(8,128)S(1)}, f32[224,256]{1,0:T(8,128)S(1)}, u32[]{:S(2)}, u32[]{:S(2)}) %collective-permute-start.14) | collective-permute-done | bytes 229408 | tf_op jit(solution)/shard_map/ppermute | solution.py:386
  53.3 5.1 %collective-permute-done.16.other_p = f32[256,256]{1,0:T(8,128)S(1)} collective-permute-done((f32[256,256]{1,0:T(8,128)S(1)}, f32[256,256]{1,0:T(8,128)S(1)}, u32[]{:S(2)}, u32[]{:S(2)}) %collective-permute-start.16) | collective-permute-done | bytes 262176 | tf_op jit(solution)/shard_map/ppermute | solution.py:386
  58.4 8.3 %shard_map.59 = (f32[4,256,256]{2,1,0:T(8,128)}, f32[2,224,256]{2,1,0:T(8,128)S(1)}, f32[224,256]{1,0:T(8,128)S(1)}) custom-call(s32[1]{0:T(128)} %bitcast.side, f32[2,224,256]{2,1,0:T(8,128)S(1)} %get-tuple-element.23.own, f32[256,256]{1,0:T(8,128)S(1)} %add.24.own_p, f32[224,256]{1,0:T(8,128)S(1)} %collective-permute-done.14.near, ...), custom_call_target="tpu_custom_call" | custom-call | tf_op jit(solution)/shard_map/pallas_call | solution.py:289
  66.7 4.8 %collective-permute-start.17 = (f32[224,256]{1,0:T(8,128)S(1)}, f32[224,256]{1,0:T(8,128)S(1)}, u32[]{:S(2)}, u32[]{:S(2)}) collective-permute-start(f32[224,256]{1,0:T(8,128)S(1)} %get-tuple-element.26), channel_id=1, source_target_pairs={{0,4},{4,0},{8,12},{12,8},{16,20},{20,16},{24,28},{28,24},{1,5},{5... | collective-permute-start | bytes 688136 | tf_op jit(solution)/shard_map/ppermute | solution.py:386
  71.6 0.1 collective-permute-start.19
  71.7 6.3 %collective-permute-done.17.near = f32[224,256]{1,0:T(8,128)S(1)} collective-permute-done((f32[224,256]{1,0:T(8,128)S(1)}, f32[224,256]{1,0:T(8,128)S(1)}, u32[]{:S(2)}, u32[]{:S(2)}) %collective-permute-start.17) | collective-permute-done | bytes 229408 | tf_op jit(solution)/shard_map/ppermute | solution.py:386
  78.0 4.2 %collective-permute-done.19.other_p = f32[256,256]{1,0:T(8,128)S(1)} collective-permute-done((f32[256,256]{1,0:T(8,128)S(1)}, f32[256,256]{1,0:T(8,128)S(1)}, u32[]{:S(2)}, u32[]{:S(2)}) %collective-permute-start.19) | collective-permute-done | bytes 262176 | tf_op jit(solution)/shard_map/ppermute | solution.py:386
  82.2 8.5 %shard_map.60 = (f32[4,256,256]{2,1,0:T(8,128)}, f32[2,224,256]{2,1,0:T(8,128)S(1)}, f32[224,256]{1,0:T(8,128)S(1)}) custom-call(s32[1]{0:T(128)} %bitcast.side, f32[2,224,256]{2,1,0:T(8,128)S(1)} %get-tuple-element.25.own, f32[256,256]{1,0:T(8,128)S(1)} %add.25.own_p, f32[224,256]{1,0:T(8,128)S(1)} %collective-permute-done.17.near, ...), custom_call_target="tpu_custom_call", output_to_operand_aliasing={{0}: (6, {})} | custom-call | tf_op jit(solution)/shard_map/pallas_call | solution.py:289
  90.8 0.1 collective-permute-start.20
  90.9 2.1 %collective-permute-start.22 = (f32[256,256]{1,0:T(8,128)S(1)}, f32[256,256]{1,0:T(8,128)S(1)}, u32[]{:S(2)}, u32[]{:S(2)}) collective-permute-start(f32[256,256]{1,0:T(8,128)S(1)} %add.26.own_p), channel_id=1, source_target_pairs={{0,8},{4,12},{8,0},{12,4},{16,24},{20,28},{24,16},{28,20},{1,9},{5... | collective-permute-start | bytes 786440 | tf_op jit(solution)/shard_map/ppermute | solution.py:386
  93.0 6.3 %collective-permute-done.20.near = f32[224,256]{1,0:T(8,128)S(1)} collective-permute-done((f32[224,256]{1,0:T(8,128)S(1)}, f32[224,256]{1,0:T(8,128)S(1)}, u32[]{:S(2)}, u32[]{:S(2)}) %collective-permute-start.20) | collective-permute-done | bytes 229408 | tf_op jit(solution)/shard_map/ppermute | solution.py:386
  99.3 3.4 %collective-permute-done.22.other_p = f32[256,256]{1,0:T(8,128)S(1)} collective-permute-done((f32[256,256]{1,0:T(8,128)S(1)}, f32[256,256]{1,0:T(8,128)S(1)}, u32[]{:S(2)}, u32[]{:S(2)}) %collective-permute-start.22) | collective-permute-done | bytes 262176 | tf_op jit(solution)/shard_map/ppermute | solution.py:386
  102.7 8.3 %shard_map.61 = (f32[4,256,256]{2,1,0:T(8,128)}, f32[2,224,256]{2,1,0:T(8,128)S(1)}, f32[224,256]{1,0:T(8,128)S(1)}) custom-call(s32[1]{0:T(128)} %bitcast.side, f32[2,224,256]{2,1,0:T(8,128)S(1)} %get-tuple-element.28.own, f32[256,256]{1,0:T(8,128)S(1)} %add.26.own_p, f32[224,256]{1,0:T(8,128)S(1)} %collective-permute-done.20.near, ...), custom_call_target="tpu_custom_call", output_to_operand_aliasing={{0}: (6, {})} | custom-call | tf_op jit(solution)/shard_map/pallas_call | solution.py:289
  111.0 1.0 collective-permute-start.23
  112.0 2.0 %collective-permute-start.25 = (f32[256,256]{1,0:T(8,128)S(1)}, f32[256,256]{1,0:T(8,128)S(1)}, u32[]{:S(2)}, u32[]{:S(2)}) collective-permute-start(f32[256,256]{1,0:T(8,128)S(1)} %add.27.own_p), channel_id=1, source_target_pairs={{0,16},{4,20},{8,24},{12,28},{16,0},{20,4},{24,8},{28,12},{1,17},{... | collective-permute-start | bytes 786440 | tf_op jit(solution)/shard_map/ppermute | solution.py:386
  114.1 14.0 %collective-permute-done.23.near = f32[224,256]{1,0:T(8,128)S(1)} collective-permute-done((f32[224,256]{1,0:T(8,128)S(1)}, f32[224,256]{1,0:T(8,128)S(1)}, u32[]{:S(2)}, u32[]{:S(2)}) %collective-permute-start.23) | collective-permute-done | bytes 229408 | tf_op jit(solution)/shard_map/ppermute | solution.py:386
  128.1 5.5 %collective-permute-done.25.other_p = f32[256,256]{1,0:T(8,128)S(1)} collective-permute-done((f32[256,256]{1,0:T(8,128)S(1)}, f32[256,256]{1,0:T(8,128)S(1)}, u32[]{:S(2)}, u32[]{:S(2)}) %collective-permute-start.25) | collective-permute-done | bytes 262176 | tf_op jit(solution)/shard_map/ppermute | solution.py:386
  133.6 8.6 %shard_map.62 = f32[4,256,256]{2,1,0:T(8,128)} custom-call(s32[1]{0:T(128)} %bitcast.side, f32[2,224,256]{2,1,0:T(8,128)S(1)} %get-tuple-element.31.own, f32[256,256]{1,0:T(8,128)S(1)} %add.27.own_p, f32[224,256]{1,0:T(8,128)S(1)} %collective-permute-done.23.near, f32[224,256]{1,0:T(8,128)S(1)} %collective-permute-done.24.far, ...), custom_call_target="tpu_custom_call", output_to_operand_aliasing={{}: (6, {})} | custom-call | tf_op jit(solution)/shard_map/pallas_call | solution.py:289
  (23 shorter events, 0.2 us)
Async XLA Ops:
  0.6 10.8 %collective-permute-start.1 = (bf16[256,256]{1,0:T(8,128)(2,1)}, bf16[256,256]{1,0:T(8,128)(2,1)S(1)}, u32[]{:S(2)}, u32[]{:S(2)}) collective-permute-start(bf16[256,256]{1,0:T(8,128)(2,1)} %own.1), channel_id=1, source_target_pairs={{0,16},{4,20},{8,24},{12,28},{16,0},{20,4},{24,8},{28,12},{1,17},{... | collective-permute-start | bytes 393224 | tf_op jit(solution)/shard_map/ppermute | solution.py:386
  4.8 9.4 %collective-permute-start.3 = (bf16[256,256]{1,0:T(8,128)(2,1)}, bf16[256,256]{1,0:T(8,128)(2,1)S(1)}, u32[]{:S(2)}, u32[]{:S(2)}) collective-permute-start(bf16[256,256]{1,0:T(8,128)(2,1)} %own.1), channel_id=1, source_target_pairs={{0,8},{4,12},{8,0},{12,4},{16,24},{20,28},{24,16},{28,20},{1,9},{5... | collective-permute-start | bytes 393224 | tf_op jit(solution)/shard_map/ppermute | solution.py:386
  11.4 6.4 %collective-permute-start.2 = (bf16[256,256]{1,0:T(8,128)(2,1)S(1)}, bf16[256,256]{1,0:T(8,128)(2,1)S(1)}, u32[]{:S(2)}, u32[]{:S(2)}) collective-permute-start(bf16[256,256]{1,0:T(8,128)(2,1)S(1)} %collective-permute-done.1.refs_2_), channel_id=1, source_target_pairs={{0,4},{4,0},{8,12},{12,8},{16,20},{20,16},{24,28},{28,24},{1,5},{5... | collective-permute-start | bytes 393224 | tf_op jit(solution)/shard_map/ppermute | solution.py:386
  12.9 9.1 %collective-permute-start = (bf16[256,256]{1,0:T(8,128)(2,1)}, bf16[256,256]{1,0:T(8,128)(2,1)S(1)}, u32[]{:S(2)}, u32[]{:S(2)}) collective-permute-start(bf16[256,256]{1,0:T(8,128)(2,1)} %own.1), channel_id=1, source_target_pairs={{0,4},{4,0},{8,12},{12,8},{16,20},{20,16},{24,28},{28,24},{1,5},{5... | collective-permute-start | bytes 393224 | tf_op jit(solution)/shard_map/ppermute | solution.py:386
  13.4 8.6 %collective-permute-start.5 = (bf16[256,256]{1,0:T(8,128)(2,1)S(1)}, bf16[256,256]{1,0:T(8,128)(2,1)S(1)}, u32[]{:S(2)}, u32[]{:S(2)}) collective-permute-start(bf16[256,256]{1,0:T(8,128)(2,1)S(1)} %collective-permute-done.1.refs_2_), channel_id=1, source_target_pairs={{0,8},{4,12},{8,0},{12,4},{16,24},{20,28},{24,16},{28,20},{1,9},{5... | collective-permute-start | bytes 393224 | tf_op jit(solution)/shard_map/ppermute | solution.py:386
  14.1 7.9 %collective-permute-start.4 = (bf16[256,256]{1,0:T(8,128)(2,1)S(1)}, bf16[256,256]{1,0:T(8,128)(2,1)S(1)}, u32[]{:S(2)}, u32[]{:S(2)}) collective-permute-start(bf16[256,256]{1,0:T(8,128)(2,1)S(1)} %collective-permute-done.3.refs_4_), channel_id=1, source_target_pairs={{0,4},{4,0},{8,12},{12,8},{16,20},{20,16},{24,28},{28,24},{1,5},{5... | collective-permute-start | bytes 393224 | tf_op jit(solution)/shard_map/ppermute | solution.py:386
  17.8 5.0 %collective-permute-start.6 = (bf16[256,256]{1,0:T(8,128)(2,1)S(1)}, bf16[256,256]{1,0:T(8,128)(2,1)S(1)}, u32[]{:S(2)}, u32[]{:S(2)}) collective-permute-start(bf16[256,256]{1,0:T(8,128)(2,1)S(1)} %collective-permute-done.2.refs_3_), channel_id=1, source_target_pairs={{0,8},{4,12},{8,0},{12,4},{16,24},{20,28},{24,16},{28,20},{1,9},{5... | collective-permute-start | bytes 393224 | tf_op jit(solution)/shard_map/ppermute | solution.py:386
  18.5 0.7 copy-start
  22.0 5.4 %copy-start.2 = (bf16[256,256]{1,0:T(8,128)(2,1)S(1)}, bf16[256,256]{1,0:T(8,128)(2,1)}, u32[]{:S(2)}) copy-start(bf16[256,256]{1,0:T(8,128)(2,1)} %own.1) | copy-start | bytes 393220
  22.0 13.2 %copy-start.1 = (f32[256,256]{1,0:T(8,128)S(1)}, f32[256,256]{1,0:T(8,128)}, u32[]{:S(2)}) copy-start(f32[256,256]{1,0:T(8,128)} %param.7) | copy-start | bytes 786436
  24.0 2.0 %collective-permute-start.7 = (f32[2,256,256]{2,1,0:T(8,128)S(1)}, f32[2,256,256]{2,1,0:T(8,128)S(1)}, u32[]{:S(2)}, u32[]{:S(2)}) collective-permute-start(f32[2,256,256]{2,1,0:T(8,128)S(1)} %get-tuple-element.21), channel_id=1, source_target_pairs={{0,1},{1,0},{2,3},{3,2},{4,5},{5,4},{6,7},{7,6},{8,9},{9,8},{10,11... | collective-permute-start | bytes 1572872 | tf_op jit(solution)/shard_map/ppermute | solution.py:386
  26.0 8.7 %collective-permute-start.8 = (f32[1,256,256]{2,1,0:T(8,128)S(1)}, f32[1,256,256]{2,1,0:T(8,128)S(1)}, u32[]{:S(2)}, u32[]{:S(2)}) collective-permute-start(f32[1,256,256]{2,1,0:T(8,128)S(1)} %get-tuple-element.34), channel_id=1, source_target_pairs={{0,2},{1,3},{2,0},{3,1},{4,6},{5,7},{6,4},{7,5},{8,10},{9,11},{10,... | collective-permute-start | bytes 786440 | tf_op jit(solution)/shard_map/ppermute | solution.py:386
  27.4 7.3 %collective-permute-start.11 = (bf16[256,256]{1,0:T(8,128)(2,1)S(1)}, bf16[256,256]{1,0:T(8,128)(2,1)S(1)}, u32[]{:S(2)}, u32[]{:S(2)}) collective-permute-start(bf16[256,256]{1,0:T(8,128)(2,1)S(1)} %copy-done.2), channel_id=1, source_target_pairs={{0,0},{4,1},{8,2},{12,3},{16,4},{20,5},{24,6},{28,7},{1,8},{5,9},{... | collective-permute-start | bytes 393224 | tf_op jit(solution)/shard_map/ppermute | solution.py:409
  28.2 8.2 %collective-permute-start.9 = (f32[256,256]{1,0:T(8,128)S(1)}, f32[256,256]{1,0:T(8,128)S(1)}, u32[]{:S(2)}, u32[]{:S(2)}) collective-permute-start(f32[256,256]{1,0:T(8,128)S(1)} %get-tuple-element.35.own_a), channel_id=1, source_target_pairs={{0,1},{1,0},{2,3},{3,2},{4,5},{5,4},{6,7},{7,6},{8,9},{9,8},{10,11... | collective-permute-start | bytes 786440 | tf_op jit(solution)/shard_map/ppermute | solution.py:386
  34.7 1.7 %collective-permute-start.10 = (f32[256,256]{1,0:T(8,128)S(1)}, f32[256,256]{1,0:T(8,128)S(1)}, u32[]{:S(2)}, u32[]{:S(2)}) collective-permute-start(f32[256,256]{1,0:T(8,128)S(1)} %bitcast.6), channel_id=1, source_target_pairs={{0,1},{1,0},{2,3},{3,2},{4,5},{5,4},{6,7},{7,6},{8,9},{9,8},{10,11... | collective-permute-start | bytes 786440 | tf_op jit(solution)/shard_map/ppermute | solution.py:386
  34.7 1.7 %collective-permute-start.12 = (bf16[256,256]{1,0:T(8,128)(2,1)S(1)}, bf16[256,256]{1,0:T(8,128)(2,1)S(1)}, u32[]{:S(2)}, u32[]{:S(2)}) collective-permute-start(bf16[256,256]{1,0:T(8,128)(2,1)S(1)} %collective-permute-done.11.own_w), channel_id=1, source_target_pairs={{0,1},{1,0},{2,3},{3,2},{4,5},{5,4},{6,7},{7,6},{8,9},{9,8},{10,11... | collective-permute-start | bytes 393224 | tf_op jit(solution)/shard_map/ppermute | solution.py:386
  35.2 11.7 %collective-permute-start.13 = (f32[256,256]{1,0:T(8,128)S(1)}, f32[256,256]{1,0:T(8,128)S(1)}, u32[]{:S(2)}, u32[]{:S(2)}) collective-permute-start(f32[256,256]{1,0:T(8,128)S(1)} %copy-done.1), channel_id=1, source_target_pairs={{0,1},{1,0},{2,3},{3,2},{4,5},{5,4},{6,7},{7,6},{8,9},{9,8},{10,11... | collective-permute-start | bytes 786440 | tf_op jit(solution)/shard_map/ppermute | solution.py:386
  44.3 9.0 %collective-permute-start.14 = (f32[224,256]{1,0:T(8,128)S(1)}, f32[224,256]{1,0:T(8,128)S(1)}, u32[]{:S(2)}, u32[]{:S(2)}) collective-permute-start(f32[224,256]{1,0:T(8,128)S(1)} %get-tuple-element.24), channel_id=1, source_target_pairs={{0,2},{1,3},{2,0},{3,1},{4,6},{5,7},{6,4},{7,5},{8,10},{9,11},{10,... | collective-permute-start | bytes 688136 | tf_op jit(solution)/shard_map/ppermute | solution.py:386
  46.9 11.5 %collective-permute-start.16 = (f32[256,256]{1,0:T(8,128)S(1)}, f32[256,256]{1,0:T(8,128)S(1)}, u32[]{:S(2)}, u32[]{:S(2)}) collective-permute-start(f32[256,256]{1,0:T(8,128)S(1)} %add.24.own_p), channel_id=1, source_target_pairs={{0,2},{1,3},{2,0},{3,1},{4,6},{5,7},{6,4},{7,5},{8,10},{9,11},{10,... | collective-permute-start | bytes 786440 | tf_op jit(solution)/shard_map/ppermute | solution.py:386
  53.3 5.1 %collective-permute-start.15 = (f32[224,256]{1,0:T(8,128)S(1)}, f32[224,256]{1,0:T(8,128)S(1)}, u32[]{:S(2)}, u32[]{:S(2)}) collective-permute-start(f32[224,256]{1,0:T(8,128)S(1)} %collective-permute-done.14.near), channel_id=1, source_target_pairs={{0,1},{1,0},{2,3},{3,2},{4,5},{5,4},{6,7},{7,6},{8,9},{9,8},{10,11... | collective-permute-start | bytes 688136 | tf_op jit(solution)/shard_map/ppermute | solution.py:386
  66.7 11.3 %collective-permute-start.17 = (f32[224,256]{1,0:T(8,128)S(1)}, f32[224,256]{1,0:T(8,128)S(1)}, u32[]{:S(2)}, u32[]{:S(2)}) collective-permute-start(f32[224,256]{1,0:T(8,128)S(1)} %get-tuple-element.26), channel_id=1, source_target_pairs={{0,4},{4,0},{8,12},{12,8},{16,20},{20,16},{24,28},{28,24},{1,5},{5... | collective-permute-start | bytes 688136 | tf_op jit(solution)/shard_map/ppermute | solution.py:386
  71.6 10.6 %collective-permute-start.19 = (f32[256,256]{1,0:T(8,128)S(1)}, f32[256,256]{1,0:T(8,128)S(1)}, u32[]{:S(2)}, u32[]{:S(2)}) collective-permute-start(f32[256,256]{1,0:T(8,128)S(1)} %add.25.own_p), channel_id=1, source_target_pairs={{0,4},{4,0},{8,12},{12,8},{16,20},{20,16},{24,28},{28,24},{1,5},{5... | collective-permute-start | bytes 786440 | tf_op jit(solution)/shard_map/ppermute | solution.py:386
  78.0 4.2 %collective-permute-start.18 = (f32[224,256]{1,0:T(8,128)S(1)}, f32[224,256]{1,0:T(8,128)S(1)}, u32[]{:S(2)}, u32[]{:S(2)}) collective-permute-start(f32[224,256]{1,0:T(8,128)S(1)} %collective-permute-done.17.near), channel_id=1, source_target_pairs={{0,1},{1,0},{2,3},{3,2},{4,5},{5,4},{6,7},{7,6},{8,9},{9,8},{10,11... | collective-permute-start | bytes 688136 | tf_op jit(solution)/shard_map/ppermute | solution.py:386
  90.8 8.5 %collective-permute-start.20 = (f32[224,256]{1,0:T(8,128)S(1)}, f32[224,256]{1,0:T(8,128)S(1)}, u32[]{:S(2)}, u32[]{:S(2)}) collective-permute-start(f32[224,256]{1,0:T(8,128)S(1)} %get-tuple-element.29), channel_id=1, source_target_pairs={{0,8},{4,12},{8,0},{12,4},{16,24},{20,28},{24,16},{28,20},{1,9},{5... | collective-permute-start | bytes 688136 | tf_op jit(solution)/shard_map/ppermute | solution.py:386
  90.9 11.8 %collective-permute-start.22 = (f32[256,256]{1,0:T(8,128)S(1)}, f32[256,256]{1,0:T(8,128)S(1)}, u32[]{:S(2)}, u32[]{:S(2)}) collective-permute-start(f32[256,256]{1,0:T(8,128)S(1)} %add.26.own_p), channel_id=1, source_target_pairs={{0,8},{4,12},{8,0},{12,4},{16,24},{20,28},{24,16},{28,20},{1,9},{5... | collective-permute-start | bytes 786440 | tf_op jit(solution)/shard_map/ppermute | solution.py:386
  99.3 3.4 %collective-permute-start.21 = (f32[224,256]{1,0:T(8,128)S(1)}, f32[224,256]{1,0:T(8,128)S(1)}, u32[]{:S(2)}, u32[]{:S(2)}) collective-permute-start(f32[224,256]{1,0:T(8,128)S(1)} %collective-permute-done.20.near), channel_id=1, source_target_pairs={{0,1},{1,0},{2,3},{3,2},{4,5},{5,4},{6,7},{7,6},{8,9},{9,8},{10,11... | collective-permute-start | bytes 688136 | tf_op jit(solution)/shard_map/ppermute | solution.py:386
  111.0 17.1 %collective-permute-start.23 = (f32[224,256]{1,0:T(8,128)S(1)}, f32[224,256]{1,0:T(8,128)S(1)}, u32[]{:S(2)}, u32[]{:S(2)}) collective-permute-start(f32[224,256]{1,0:T(8,128)S(1)} %get-tuple-element.32), channel_id=1, source_target_pairs={{0,16},{4,20},{8,24},{12,28},{16,0},{20,4},{24,8},{28,12},{1,17},{... | collective-permute-start | bytes 688136 | tf_op jit(solution)/shard_map/ppermute | solution.py:386
  112.0 21.6 %collective-permute-start.25 = (f32[256,256]{1,0:T(8,128)S(1)}, f32[256,256]{1,0:T(8,128)S(1)}, u32[]{:S(2)}, u32[]{:S(2)}) collective-permute-start(f32[256,256]{1,0:T(8,128)S(1)} %add.27.own_p), channel_id=1, source_target_pairs={{0,16},{4,20},{8,24},{12,28},{16,0},{20,4},{24,8},{28,12},{1,17},{... | collective-permute-start | bytes 786440 | tf_op jit(solution)/shard_map/ppermute | solution.py:386
  128.1 5.5 %collective-permute-start.24 = (f32[224,256]{1,0:T(8,128)S(1)}, f32[224,256]{1,0:T(8,128)S(1)}, u32[]{:S(2)}, u32[]{:S(2)}) collective-permute-start(f32[224,256]{1,0:T(8,128)S(1)} %collective-permute-done.23.near), channel_id=1, source_target_pairs={{0,1},{1,0},{2,3},{3,2},{4,5},{5,4},{6,7},{7,6},{8,9},{9,8},{10,11... | collective-permute-start | bytes 688136 | tf_op jit(solution)/shard_map/ppermute | solution.py:386

commit v5 on v4

--- a/solution.py
+++ b/solution.py
@@ -200,7 +200,11 @@
     state[0, half:] = top[:share]
     state[1, half : half + half - share] = top[share:]
     state[1, half + half - share :] = jnp.concatenate(upper[2:], axis=1)
-    send[...] = state[side[0]]
+    rows = send.shape[0]
+    if rows == state.shape[1]:
+        send[...] = state[side[0]]
+    else:
+        send[...] = state[side[0], pl.ds(pl.multiple_of(side[1] * rows, SUB), rows)]
 
 
 def load_state(first, second):
@@ -229,8 +233,18 @@
     q_out[...] = q
 
 
-def upper_kernel(level, is_last, has_buffer, side, own, own_p, near, far, other_p, *refs):
-    refs = list(refs)
+def gather_half(side, pieces):
+    if len(pieces) == 1:
+        return pieces[0][...]
+    mine, theirs = pieces[0][...], pieces[1][...]
+    is_first = side[1] == 0
+    return jnp.concatenate(
+        [jnp.where(is_first, mine, theirs), jnp.where(is_first, theirs, mine)], axis=0
+    )
+
+
+def upper_kernel(level, is_last, has_buffer, pieces, side, own, own_p, other_p, *refs):
+    near, far, refs = list(refs[:pieces]), list(refs[pieces : 2 * pieces]), list(refs[2 * pieces :])
     if has_buffer:
         refs.pop(0)
     q_all = refs.pop(0)
@@ -238,7 +252,7 @@
     q_here, done = refs
     is_first = side[0] == 0
     own_s, own_w = load_state(own[0], own[1])
-    near, far = near[...], far[...]
+    near, far = gather_half(side, near), gather_half(side, far)
     other_s, other_w = load_state(jnp.where(is_first, near, far), jnp.where(is_first, far, near))
     q, upper, w = merge_math(
         (own_s, split(own_w), split(own_p[...])),
@@ -263,16 +277,16 @@
     return [pltpu.with_memory_space_constraint(x, pltpu.VMEM) for x in arrays]
 
 
-def state_shapes(size):
+def state_shapes(size, pieces):
     rows = size // 2 + 3 * size // 8
-    return [pltpu.VMEM((2, rows, size), F32), pltpu.VMEM((rows, size), F32)]
-
-
-def first_merge(side, arrays):
+    return [pltpu.VMEM((2, rows, size), F32), pltpu.VMEM((rows // pieces, size), F32)]
+
+
+def first_merge(side, arrays, pieces):
     rows, size = arrays[0].shape
     return pl.pallas_call(
         first_kernel,
-        out_shape=[jax.ShapeDtypeStruct((rows, size), F32)] + state_shapes(size),
+        out_shape=[jax.ShapeDtypeStruct((rows, size), F32)] + state_shapes(size, pieces),
         in_specs=[SMEM] + [VMEM] * len(arrays),
         out_specs=[VMEM] * 3,
         compiler_params=pltpu.CompilerParams(vmem_limit_bytes=SCRATCH_BYTES),
@@ -280,14 +294,14 @@
     )(side, *near_core(arrays))
 
 
-def upper_merge(level, levels, side, arrays, buffer):
+def upper_merge(level, levels, side, arrays, buffer, pieces):
     size = arrays[1].shape[1]
     is_last = level == levels
     extra = [] if buffer is None else [buffer]
     out_shape = [jax.ShapeDtypeStruct((levels - 1, size, size), F32)]
-    out_shape += [] if is_last else state_shapes(size)
+    out_shape += [] if is_last else state_shapes(size, pieces)
     return pl.pallas_call(
-        functools.partial(upper_kernel, level, is_last, bool(extra)),
+        functools.partial(upper_kernel, level, is_last, bool(extra), (len(arrays) - 3) // 2),
         out_shape=out_shape,
         in_specs=[SMEM] + [VMEM] * len(arrays) + [ANY] * len(extra),
         out_specs=[ANY] + [VMEM] * (len(out_shape) - 1),
@@ -392,7 +406,7 @@
     col_levels, row_levels = col_count.bit_length() - 1, row_count.bit_length() - 1
     levels = col_levels + row_levels
     place = jnp.stack([row_index, col_index]).astype(jnp.int32)
-    side = (col_index & 1).astype(jnp.int32)[None]
+    side = jnp.stack([col_index & 1, col_index >> 1 & 1]).astype(jnp.int32)
     bits = [("col", b) for b in range(col_levels)] + [("row", b) for b in range(row_levels)]
 
     chunks = {0: probes}
@@ -429,15 +443,27 @@
     other_a = swap(own_a, "col", 0)
     other_b = swap(own_b, "col", 0)
 
+    def pieces(level):
+        return 2 if level == levels and col_levels > 1 and row_levels > 0 else 1
+
     leaf_basis, state, send = first_merge(
-        side, (own_a, own_b, other_a, other_b, own_w, other_w)
+        side, (own_a, own_b, other_a, other_b, own_w, other_w), pieces(2)
     )
     buffer = None
     for level, (axis, bit) in list(enumerate(bits, start=1))[1:]:
-        near = swap(send, axis, bit)
-        far = swap(near, "col", 0)
+        near = [swap(send, axis, bit)]
+        if pieces(level) > 1:
+            near.append(swap(near[0], "col", 1))
+        far = []
+        for x in near:
+            far.append(swap(x, "col", 0))
         buffer, *rest = upper_merge(
-            level, levels, side, (state, own_p[level], near, far, other_p[level]), buffer
+            level,
+            levels,
+            side,
+            (state, own_p[level], other_p[level], *near, *far),
+            buffer,
+            pieces(level + 1),
         )
         if rest:
             state, send = rest

time: 143 us -> 142 us (level)
  waiting for transfers between devices: 66.2 us -> 61.8 us
  Pallas kernels: 45.6 us -> 48.3 us
    ppermute x25 -> x27, waiting for transfers between devices: 66.2 us -> 61.8 us  [swap(): lax.ppermute(x, axis, [(i, i ^ 1 << bit) for i in range(lax.axis_size(axi...]
    pallas_call x4, Pallas kernels: 33.7 us -> 35.9 us  [upper_merge(): pl.pallas_call(functools.partial(upper_kernel, level, is_last, bool(extra...]
    ppermute x25 -> x27, starting transfers between devices: 27.8 us -> 29 us  [swap(): lax.ppermute(x, axis, [(i, i ^ 1 << bit) for i in range(lax.axis_size(axi...]
  transfers between devices with their start and end apart: 26 -> 28, of which waited for: 14 -> 15; matrix products, arithmetic and copies ran while one was open for 0% -> 0% of each run, Pallas kernels for 7% -> 8%
where the time goes in v5:
time: 142 us
  waiting for transfers between devices  61.8 us (44%)
  Pallas kernels  48.3 us (34%)
  starting transfers between devices  29.9 us (21%)
    ppermute x27, waiting for transfers between devices, swap(): lax.ppermute(x, axis, [(i, i ^ 1 << bit) for i in range(lax.axis_size(axi...  61.8 us
    pallas_call x4, Pallas kernels, upper_merge(): pl.pallas_call(functools.partial(upper_kernel, level, is_last, bool(extra...  35.9 us
    ppermute x27, starting transfers between devices, swap(): lax.ppermute(x, axis, [(i, i ^ 1 << bit) for i in range(lax.axis_size(axi...  29 us
    pallas_call x1, Pallas kernels, first_merge(): pl.pallas_call(first_kernel, out_shape=[jax.ShapeDtypeStruct((rows, size)...  8.44 us
  transfers between devices with their start and end apart: 28, of which 15 were waited for; matrix products, arithmetic and copies ran while one was open for 0% of the time, Pallas kernels for 8%

profile of v5, /device:TPU:0, one launch (start us, length us, event | category | flops | bytes accessed | tf_op | source)
XLA Modules:
  0.0 142.0 jit_solution(17497404356031175603)
XLA Ops:
  0.6 4.1 %collective-permute-start.1 = (bf16[256,256]{1,0:T(8,128)(2,1)}, bf16[256,256]{1,0:T(8,128)(2,1)S(1)}, u32[]{:S(2)}, u32[]{:S(2)}) collective-permute-start(bf16[256,256]{1,0:T(8,128)(2,1)} %own.1), channel_id=1, source_target_pairs={{0,16},{4,20},{8,24},{12,28},{16,0},{20,4},{24,8},{28,12},{1,17},{... | collective-permute-start | bytes 393224 | tf_op jit(solution)/shard_map/ppermute | solution.py:400
  4.8 1.6 %collective-permute-start.3 = (bf16[256,256]{1,0:T(8,128)(2,1)}, bf16[256,256]{1,0:T(8,128)(2,1)S(1)}, u32[]{:S(2)}, u32[]{:S(2)}) collective-permute-start(bf16[256,256]{1,0:T(8,128)(2,1)} %own.1), channel_id=1, source_target_pairs={{0,8},{4,12},{8,0},{12,4},{16,24},{20,28},{24,16},{28,20},{1,9},{5... | collective-permute-start | bytes 393224 | tf_op jit(solution)/shard_map/ppermute | solution.py:400
  6.3 5.0 %collective-permute-done.1.refs_2_ = bf16[256,256]{1,0:T(8,128)(2,1)S(1)} collective-permute-done((bf16[256,256]{1,0:T(8,128)(2,1)}, bf16[256,256]{1,0:T(8,128)(2,1)S(1)}, u32[]{:S(2)}, u32[]{:S(2)}) %collective-permute-start.1) | collective-permute-done | bytes 131104 | tf_op jit(solution)/shard_map/ppermute | solution.py:400
  11.4 1.6 %collective-permute-start.2 = (bf16[256,256]{1,0:T(8,128)(2,1)S(1)}, bf16[256,256]{1,0:T(8,128)(2,1)S(1)}, u32[]{:S(2)}, u32[]{:S(2)}) collective-permute-start(bf16[256,256]{1,0:T(8,128)(2,1)S(1)} %collective-permute-done.1.refs_2_), channel_id=1, source_target_pairs={{0,4},{4,0},{8,12},{12,8},{16,20},{20,16},{24,28},{28,24},{1,5},{5... | collective-permute-start | bytes 393224 | tf_op jit(solution)/shard_map/ppermute | solution.py:400
  12.9 0.5 collective-permute-start
  13.4 0.7 collective-permute-start.5
  14.1 1.5 %collective-permute-start.4 = (bf16[256,256]{1,0:T(8,128)(2,1)S(1)}, bf16[256,256]{1,0:T(8,128)(2,1)S(1)}, u32[]{:S(2)}, u32[]{:S(2)}) collective-permute-start(bf16[256,256]{1,0:T(8,128)(2,1)S(1)} %collective-permute-done.3.refs_4_), channel_id=1, source_target_pairs={{0,4},{4,0},{8,12},{12,8},{16,20},{20,16},{24,28},{28,24},{1,5},{5... | collective-permute-start | bytes 393224 | tf_op jit(solution)/shard_map/ppermute | solution.py:400
  15.7 2.1 %collective-permute-done.2.refs_3_ = bf16[256,256]{1,0:T(8,128)(2,1)S(1)} collective-permute-done((bf16[256,256]{1,0:T(8,128)(2,1)S(1)}, bf16[256,256]{1,0:T(8,128)(2,1)S(1)}, u32[]{:S(2)}, u32[]{:S(2)}) %collective-permute-start.2) | collective-permute-done | bytes 131104 | tf_op jit(solution)/shard_map/ppermute | solution.py:400
  17.8 0.7 collective-permute-start.6
  18.5 0.1 pad_add_fusion.1.place
  18.5 0.7 copy-done
  19.2 2.8 %load_front.1 = (bf16[4,256,2048]{2,1,0:T(8,128)(2,1)S(1)}, bf16[256,256]{1,0:T(8,128)(2,1)S(1)}) custom-call(s32[2]{0:T(128)S(1)} %pad_add_fusion.1.place, s32[4,8]{1,0:T(4,128)S(1)} %copy-done, bf16[1024,2048]{1,0:T(8,128)(2,1)} %front.1, bf16[256,256]{1,0:T(8,128)(2,1)} %own.1), custom_call_target="tpu_custom_call" | custom-call | tf_op jit(solution)/shard_map/load_front/pallas_call | solution.py:358
  22.1 0.7 collective-permute-done.6.refs_7_
  22.7 1.2 samples.1
  24.0 0.1 collective-permute-start.7
  24.0 1.9 %collective-permute-done.7 = f32[2,256,256]{2,1,0:T(8,128)S(1)} collective-permute-done((f32[2,256,256]{2,1,0:T(8,128)S(1)}, f32[2,256,256]{2,1,0:T(8,128)S(1)}, u32[]{:S(2)}, u32[]{:S(2)}) %collective-permute-start.7) | collective-permute-done | bytes 524320 | tf_op jit(solution)/shard_map/ppermute | solution.py:400
  25.9 0.1 slice_add_fusion
  26.0 1.3 collective-permute-start.8
  27.4 0.8 collective-permute-start.11
  28.2 2.3 %collective-permute-start.9 = (f32[256,256]{1,0:T(8,128)S(1)}, f32[256,256]{1,0:T(8,128)S(1)}, u32[]{:S(2)}, u32[]{:S(2)}) collective-permute-start(f32[256,256]{1,0:T(8,128)S(1)} %get-tuple-element.35.own_a), channel_id=1, source_target_pairs={{0,1},{1,0},{2,3},{3,2},{4,5},{5,4},{6,7},{7,6},{8,9},{9,8},{10,11... | collective-permute-start | bytes 786440 | tf_op jit(solution)/shard_map/ppermute | solution.py:400
  30.6 4.1 %collective-permute-done.8 = f32[1,256,256]{2,1,0:T(8,128)S(1)} collective-permute-done((f32[1,256,256]{2,1,0:T(8,128)S(1)}, f32[1,256,256]{2,1,0:T(8,128)S(1)}, u32[]{:S(2)}, u32[]{:S(2)}) %collective-permute-start.8) | collective-permute-done | bytes 262176 | tf_op jit(solution)/shard_map/ppermute | solution.py:400
  34.7 0.5 collective-permute-start.12
  35.2 0.1 collective-permute-start.13
  35.3 0.1 pad_add_fusion.side
  35.4 1.1 collective-permute-done.12.other_w
  36.4 8.4 %first_merge.1 = (f32[256,256]{1,0:T(8,128)}, f32[2,224,256]{2,1,0:T(8,128)S(1)}, f32[224,256]{1,0:T(8,128)S(1)}) custom-call(s32[2]{0:T(128)S(1)} %pad_add_fusion.side, f32[256,256]{1,0:T(8,128)S(1)} %get-tuple-element.35.own_a, f32[256,256]{1,0:T(8,128)S(1)} %bitcast.8, f32[256,256]{1,0:T(8,128)S(1)} %collective-permute-done.9.other_a, ...), custom_call_target="tpu_custom_call" | custom-call | tf_op jit(solution)/shard_map/first_merge/pallas_call | solution.py:287
  44.9 2.6 %collective-permute-start.15 = (f32[224,256]{1,0:T(8,128)S(1)}, f32[224,256]{1,0:T(8,128)S(1)}, u32[]{:S(2)}, u32[]{:S(2)}) collective-permute-start(f32[224,256]{1,0:T(8,128)S(1)} %get-tuple-element.24), channel_id=1, source_target_pairs={{0,2},{1,3},{2,0},{3,1},{4,6},{5,7},{6,4},{7,5},{8,10},{9,11},{10,... | collective-permute-start | bytes 688136 | tf_op jit(solution)/shard_map/ppermute | solution.py:400
  47.5 0.1 collective-permute-start.14
  47.6 6.3 %collective-permute-done.15.refs_0_ = f32[224,256]{1,0:T(8,128)S(1)} collective-permute-done((f32[224,256]{1,0:T(8,128)S(1)}, f32[224,256]{1,0:T(8,128)S(1)}, u32[]{:S(2)}, u32[]{:S(2)}) %collective-permute-start.15) | collective-permute-done | bytes 229408 | tf_op jit(solution)/shard_map/ppermute | solution.py:400
  53.9 5.1 %collective-permute-done.14.other_p = f32[256,256]{1,0:T(8,128)S(1)} collective-permute-done((f32[256,256]{1,0:T(8,128)S(1)}, f32[256,256]{1,0:T(8,128)S(1)}, u32[]{:S(2)}, u32[]{:S(2)}) %collective-permute-start.14) | collective-permute-done | bytes 262176 | tf_op jit(solution)/shard_map/ppermute | solution.py:400
  59.0 8.9 %shard_map.59 = (f32[4,256,256]{2,1,0:T(8,128)}, f32[2,224,256]{2,1,0:T(8,128)S(1)}, f32[224,256]{1,0:T(8,128)S(1)}) custom-call(s32[2]{0:T(128)S(1)} %pad_add_fusion.side, f32[2,224,256]{2,1,0:T(8,128)S(1)} %get-tuple-element.23.own, f32[256,256]{1,0:T(8,128)S(1)} %add.24.own_p, f32[256,256]{1,0:T(8,128)S(1)} %collective-permute-done.14.other_p, ...), custom_call_target="tpu_custom_call" | custom-call | tf_op jit(solution)/shard_map/pallas_call | solution.py:303
  67.8 4.8 %collective-permute-start.18 = (f32[224,256]{1,0:T(8,128)S(1)}, f32[224,256]{1,0:T(8,128)S(1)}, u32[]{:S(2)}, u32[]{:S(2)}) collective-permute-start(f32[224,256]{1,0:T(8,128)S(1)} %get-tuple-element.26), channel_id=1, source_target_pairs={{0,4},{4,0},{8,12},{12,8},{16,20},{20,16},{24,28},{28,24},{1,5},{5... | collective-permute-start | bytes 688136 | tf_op jit(solution)/shard_map/ppermute | solution.py:400
  72.7 0.1 collective-permute-start.17
  72.8 6.3 %collective-permute-done.18.refs_0_ = f32[224,256]{1,0:T(8,128)S(1)} collective-permute-done((f32[224,256]{1,0:T(8,128)S(1)}, f32[224,256]{1,0:T(8,128)S(1)}, u32[]{:S(2)}, u32[]{:S(2)}) %collective-permute-start.18) | collective-permute-done | bytes 229408 | tf_op jit(solution)/shard_map/ppermute | solution.py:400
  79.1 4.2 %collective-permute-done.17.other_p = f32[256,256]{1,0:T(8,128)S(1)} collective-permute-done((f32[256,256]{1,0:T(8,128)S(1)}, f32[256,256]{1,0:T(8,128)S(1)}, u32[]{:S(2)}, u32[]{:S(2)}) %collective-permute-start.17) | collective-permute-done | bytes 262176 | tf_op jit(solution)/shard_map/ppermute | solution.py:400
  83.3 9.1 %shard_map.60 = (f32[4,256,256]{2,1,0:T(8,128)}, f32[2,224,256]{2,1,0:T(8,128)S(1)}, f32[224,256]{1,0:T(8,128)S(1)}) custom-call(s32[2]{0:T(128)S(1)} %pad_add_fusion.side, f32[2,224,256]{2,1,0:T(8,128)S(1)} %get-tuple-element.25.own, f32[256,256]{1,0:T(8,128)S(1)} %add.25.own_p, ...), custom_call_target="tpu_custom_call", output_to_operand_aliasing={{0}: (6, {})} | custom-call | tf_op jit(solution)/shard_map/pallas_call | solution.py:303
  92.4 0.1 collective-permute-start.21
  92.5 2.1 %collective-permute-start.20 = (f32[256,256]{1,0:T(8,128)S(1)}, f32[256,256]{1,0:T(8,128)S(1)}, u32[]{:S(2)}, u32[]{:S(2)}) collective-permute-start(f32[256,256]{1,0:T(8,128)S(1)} %add.26.own_p), channel_id=1, source_target_pairs={{0,8},{4,12},{8,0},{12,4},{16,24},{20,28},{24,16},{28,20},{1,9},{5... | collective-permute-start | bytes 786440 | tf_op jit(solution)/shard_map/ppermute | solution.py:400
  94.6 6.3 %collective-permute-done.21.refs_0_ = f32[224,256]{1,0:T(8,128)S(1)} collective-permute-done((f32[224,256]{1,0:T(8,128)S(1)}, f32[224,256]{1,0:T(8,128)S(1)}, u32[]{:S(2)}, u32[]{:S(2)}) %collective-permute-start.21) | collective-permute-done | bytes 229408 | tf_op jit(solution)/shard_map/ppermute | solution.py:400
  100.9 3.4 %collective-permute-done.20.other_p = f32[256,256]{1,0:T(8,128)S(1)} collective-permute-done((f32[256,256]{1,0:T(8,128)S(1)}, f32[256,256]{1,0:T(8,128)S(1)}, u32[]{:S(2)}, u32[]{:S(2)}) %collective-permute-start.20) | collective-permute-done | bytes 262176 | tf_op jit(solution)/shard_map/ppermute | solution.py:400
  104.3 8.8 %shard_map.61 = (f32[4,256,256]{2,1,0:T(8,128)}, f32[2,224,256]{2,1,0:T(8,128)S(1)}, f32[112,256]{1,0:T(8,128)S(1)}) custom-call(s32[2]{0:T(128)S(1)} %pad_add_fusion.side, f32[2,224,256]{2,1,0:T(8,128)S(1)} %get-tuple-element.28.own, f32[256,256]{1,0:T(8,128)S(1)} %add.26.own_p, ...), custom_call_target="tpu_custom_call", output_to_operand_aliasing={{0}: (6, {})} | custom-call | tf_op jit(solution)/shard_map/pallas_call | solution.py:303
  113.2 1.0 collective-permute-start.24
  114.2 2.0 %collective-permute-start.23 = (f32[256,256]{1,0:T(8,128)S(1)}, f32[256,256]{1,0:T(8,128)S(1)}, u32[]{:S(2)}, u32[]{:S(2)}) collective-permute-start(f32[256,256]{1,0:T(8,128)S(1)} %add.27.own_p), channel_id=1, source_target_pairs={{0,16},{4,20},{8,24},{12,28},{16,0},{20,4},{24,8},{28,12},{1,17},{... | collective-permute-start | bytes 786440 | tf_op jit(solution)/shard_map/ppermute | solution.py:400
  116.2 10.3 %collective-permute-done.24.refs_0_ = f32[112,256]{1,0:T(8,128)S(1)} collective-permute-done((f32[112,256]{1,0:T(8,128)S(1)}, f32[112,256]{1,0:T(8,128)S(1)}, u32[]{:S(2)}, u32[]{:S(2)}) %collective-permute-start.24) | collective-permute-done | bytes 114720 | tf_op jit(solution)/shard_map/ppermute | solution.py:400
  126.6 1.2 collective-permute-start.25
  127.8 3.5 %collective-permute-done.25.refs_1_ = f32[112,256]{1,0:T(8,128)S(1)} collective-permute-done((f32[112,256]{1,0:T(8,128)S(1)}, f32[112,256]{1,0:T(8,128)S(1)}, u32[]{:S(2)}, u32[]{:S(2)}) %collective-permute-start.25) | collective-permute-done | bytes 114720 | tf_op jit(solution)/shard_map/ppermute | solution.py:400
  131.4 1.3 collective-permute-done.27.refs_3_
  132.7 9.1 %shard_map.62 = f32[4,256,256]{2,1,0:T(8,128)} custom-call(s32[2]{0:T(128)S(1)} %pad_add_fusion.side, f32[2,224,256]{2,1,0:T(8,128)S(1)} %get-tuple-element.31.own, f32[256,256]{1,0:T(8,128)S(1)} %add.27.own_p, f32[256,256]{1,0:T(8,128)S(1)} %collective-permute-done.23.other_p, ...), custom_call_target="tpu_custom_call", output_to_operand_aliasing={{}: (8, {})} | custom-call | tf_op jit(solution)/shard_map/pallas_call | solution.py:303
  (28 shorter events, 0.2 us)
Async XLA Ops:
  0.6 10.8 %collective-permute-start.1 = (bf16[256,256]{1,0:T(8,128)(2,1)}, bf16[256,256]{1,0:T(8,128)(2,1)S(1)}, u32[]{:S(2)}, u32[]{:S(2)}) collective-permute-start(bf16[256,256]{1,0:T(8,128)(2,1)} %own.1), channel_id=1, source_target_pairs={{0,16},{4,20},{8,24},{12,28},{16,0},{20,4},{24,8},{28,12},{1,17},{... | collective-permute-start | bytes 393224 | tf_op jit(solution)/shard_map/ppermute | solution.py:400
  4.8 9.4 %collective-permute-start.3 = (bf16[256,256]{1,0:T(8,128)(2,1)}, bf16[256,256]{1,0:T(8,128)(2,1)S(1)}, u32[]{:S(2)}, u32[]{:S(2)}) collective-permute-start(bf16[256,256]{1,0:T(8,128)(2,1)} %own.1), channel_id=1, source_target_pairs={{0,8},{4,12},{8,0},{12,4},{16,24},{20,28},{24,16},{28,20},{1,9},{5... | collective-permute-start | bytes 393224 | tf_op jit(solution)/shard_map/ppermute | solution.py:400
  11.4 6.4 %collective-permute-start.2 = (bf16[256,256]{1,0:T(8,128)(2,1)S(1)}, bf16[256,256]{1,0:T(8,128)(2,1)S(1)}, u32[]{:S(2)}, u32[]{:S(2)}) collective-permute-start(bf16[256,256]{1,0:T(8,128)(2,1)S(1)} %collective-permute-done.1.refs_2_), channel_id=1, source_target_pairs={{0,4},{4,0},{8,12},{12,8},{16,20},{20,16},{24,28},{28,24},{1,5},{5... | collective-permute-start | bytes 393224 | tf_op jit(solution)/shard_map/ppermute | solution.py:400
  12.9 9.1 %collective-permute-start = (bf16[256,256]{1,0:T(8,128)(2,1)}, bf16[256,256]{1,0:T(8,128)(2,1)S(1)}, u32[]{:S(2)}, u32[]{:S(2)}) collective-permute-start(bf16[256,256]{1,0:T(8,128)(2,1)} %own.1), channel_id=1, source_target_pairs={{0,4},{4,0},{8,12},{12,8},{16,20},{20,16},{24,28},{28,24},{1,5},{5... | collective-permute-start | bytes 393224 | tf_op jit(solution)/shard_map/ppermute | solution.py:400
  13.4 8.6 %collective-permute-start.5 = (bf16[256,256]{1,0:T(8,128)(2,1)S(1)}, bf16[256,256]{1,0:T(8,128)(2,1)S(1)}, u32[]{:S(2)}, u32[]{:S(2)}) collective-permute-start(bf16[256,256]{1,0:T(8,128)(2,1)S(1)} %collective-permute-done.1.refs_2_), channel_id=1, source_target_pairs={{0,8},{4,12},{8,0},{12,4},{16,24},{20,28},{24,16},{28,20},{1,9},{5... | collective-permute-start | bytes 393224 | tf_op jit(solution)/shard_map/ppermute | solution.py:400
  14.1 7.9 %collective-permute-start.4 = (bf16[256,256]{1,0:T(8,128)(2,1)S(1)}, bf16[256,256]{1,0:T(8,128)(2,1)S(1)}, u32[]{:S(2)}, u32[]{:S(2)}) collective-permute-start(bf16[256,256]{1,0:T(8,128)(2,1)S(1)} %collective-permute-done.3.refs_4_), channel_id=1, source_target_pairs={{0,4},{4,0},{8,12},{12,8},{16,20},{20,16},{24,28},{28,24},{1,5},{5... | collective-permute-start | bytes 393224 | tf_op jit(solution)/shard_map/ppermute | solution.py:400
  17.8 5.0 %collective-permute-start.6 = (bf16[256,256]{1,0:T(8,128)(2,1)S(1)}, bf16[256,256]{1,0:T(8,128)(2,1)S(1)}, u32[]{:S(2)}, u32[]{:S(2)}) collective-permute-start(bf16[256,256]{1,0:T(8,128)(2,1)S(1)} %collective-permute-done.2.refs_3_), channel_id=1, source_target_pairs={{0,8},{4,12},{8,0},{12,4},{16,24},{20,28},{24,16},{28,20},{1,9},{5... | collective-permute-start | bytes 393224 | tf_op jit(solution)/shard_map/ppermute | solution.py:400
  18.5 0.7 copy-start
  22.0 5.4 %copy-start.2 = (bf16[256,256]{1,0:T(8,128)(2,1)S(1)}, bf16[256,256]{1,0:T(8,128)(2,1)}, u32[]{:S(2)}) copy-start(bf16[256,256]{1,0:T(8,128)(2,1)} %own.1) | copy-start | bytes 393220
  22.0 13.2 %copy-start.1 = (f32[256,256]{1,0:T(8,128)S(1)}, f32[256,256]{1,0:T(8,128)}, u32[]{:S(2)}) copy-start(f32[256,256]{1,0:T(8,128)} %param.7) | copy-start | bytes 786436
  24.0 2.0 %collective-permute-start.7 = (f32[2,256,256]{2,1,0:T(8,128)S(1)}, f32[2,256,256]{2,1,0:T(8,128)S(1)}, u32[]{:S(2)}, u32[]{:S(2)}) collective-permute-start(f32[2,256,256]{2,1,0:T(8,128)S(1)} %get-tuple-element.21), channel_id=1, source_target_pairs={{0,1},{1,0},{2,3},{3,2},{4,5},{5,4},{6,7},{7,6},{8,9},{9,8},{10,11... | collective-permute-start | bytes 1572872 | tf_op jit(solution)/shard_map/ppermute | solution.py:400
  26.0 8.7 %collective-permute-start.8 = (f32[1,256,256]{2,1,0:T(8,128)S(1)}, f32[1,256,256]{2,1,0:T(8,128)S(1)}, u32[]{:S(2)}, u32[]{:S(2)}) collective-permute-start(f32[1,256,256]{2,1,0:T(8,128)S(1)} %get-tuple-element.34), channel_id=1, source_target_pairs={{0,2},{1,3},{2,0},{3,1},{4,6},{5,7},{6,4},{7,5},{8,10},{9,11},{10,... | collective-permute-start | bytes 786440 | tf_op jit(solution)/shard_map/ppermute | solution.py:400
  27.4 7.3 %collective-permute-start.11 = (bf16[256,256]{1,0:T(8,128)(2,1)S(1)}, bf16[256,256]{1,0:T(8,128)(2,1)S(1)}, u32[]{:S(2)}, u32[]{:S(2)}) collective-permute-start(bf16[256,256]{1,0:T(8,128)(2,1)S(1)} %copy-done.2), channel_id=1, source_target_pairs={{0,0},{4,1},{8,2},{12,3},{16,4},{20,5},{24,6},{28,7},{1,8},{5,9},{... | collective-permute-start | bytes 393224 | tf_op jit(solution)/shard_map/ppermute | solution.py:423
  28.2 8.2 %collective-permute-start.9 = (f32[256,256]{1,0:T(8,128)S(1)}, f32[256,256]{1,0:T(8,128)S(1)}, u32[]{:S(2)}, u32[]{:S(2)}) collective-permute-start(f32[256,256]{1,0:T(8,128)S(1)} %get-tuple-element.35.own_a), channel_id=1, source_target_pairs={{0,1},{1,0},{2,3},{3,2},{4,5},{5,4},{6,7},{7,6},{8,9},{9,8},{10,11... | collective-permute-start | bytes 786440 | tf_op jit(solution)/shard_map/ppermute | solution.py:400
  34.7 1.7 %collective-permute-start.10 = (f32[256,256]{1,0:T(8,128)S(1)}, f32[256,256]{1,0:T(8,128)S(1)}, u32[]{:S(2)}, u32[]{:S(2)}) collective-permute-start(f32[256,256]{1,0:T(8,128)S(1)} %bitcast.7), channel_id=1, source_target_pairs={{0,1},{1,0},{2,3},{3,2},{4,5},{5,4},{6,7},{7,6},{8,9},{9,8},{10,11... | collective-permute-start | bytes 786440 | tf_op jit(solution)/shard_map/ppermute | solution.py:400
  34.7 1.7 %collective-permute-start.12 = (bf16[256,256]{1,0:T(8,128)(2,1)S(1)}, bf16[256,256]{1,0:T(8,128)(2,1)S(1)}, u32[]{:S(2)}, u32[]{:S(2)}) collective-permute-start(bf16[256,256]{1,0:T(8,128)(2,1)S(1)} %collective-permute-done.11.own_w), channel_id=1, source_target_pairs={{0,1},{1,0},{2,3},{3,2},{4,5},{5,4},{6,7},{7,6},{8,9},{9,8},{10,11... | collective-permute-start | bytes 393224 | tf_op jit(solution)/shard_map/ppermute | solution.py:400
  35.2 12.2 %collective-permute-start.13 = (f32[256,256]{1,0:T(8,128)S(1)}, f32[256,256]{1,0:T(8,128)S(1)}, u32[]{:S(2)}, u32[]{:S(2)}) collective-permute-start(f32[256,256]{1,0:T(8,128)S(1)} %copy-done.1), channel_id=1, source_target_pairs={{0,1},{1,0},{2,3},{3,2},{4,5},{5,4},{6,7},{7,6},{8,9},{9,8},{10,11... | collective-permute-start | bytes 786440 | tf_op jit(solution)/shard_map/ppermute | solution.py:400
  44.9 9.0 %collective-permute-start.15 = (f32[224,256]{1,0:T(8,128)S(1)}, f32[224,256]{1,0:T(8,128)S(1)}, u32[]{:S(2)}, u32[]{:S(2)}) collective-permute-start(f32[224,256]{1,0:T(8,128)S(1)} %get-tuple-element.24), channel_id=1, source_target_pairs={{0,2},{1,3},{2,0},{3,1},{4,6},{5,7},{6,4},{7,5},{8,10},{9,11},{10,... | collective-permute-start | bytes 688136 | tf_op jit(solution)/shard_map/ppermute | solution.py:400
  47.5 11.5 %collective-permute-start.14 = (f32[256,256]{1,0:T(8,128)S(1)}, f32[256,256]{1,0:T(8,128)S(1)}, u32[]{:S(2)}, u32[]{:S(2)}) collective-permute-start(f32[256,256]{1,0:T(8,128)S(1)} %add.24.own_p), channel_id=1, source_target_pairs={{0,2},{1,3},{2,0},{3,1},{4,6},{5,7},{6,4},{7,5},{8,10},{9,11},{10,... | collective-permute-start | bytes 786440 | tf_op jit(solution)/shard_map/ppermute | solution.py:400
  53.9 5.1 %collective-permute-start.16 = (f32[224,256]{1,0:T(8,128)S(1)}, f32[224,256]{1,0:T(8,128)S(1)}, u32[]{:S(2)}, u32[]{:S(2)}) collective-permute-start(f32[224,256]{1,0:T(8,128)S(1)} %collective-permute-done.15.refs_0_), channel_id=1, source_target_pairs={{0,1},{1,0},{2,3},{3,2},{4,5},{5,4},{6,7},{7,6},{8,9},{9,8},{10,11... | collective-permute-start | bytes 688136 | tf_op jit(solution)/shard_map/ppermute | solution.py:400
  67.8 11.3 %collective-permute-start.18 = (f32[224,256]{1,0:T(8,128)S(1)}, f32[224,256]{1,0:T(8,128)S(1)}, u32[]{:S(2)}, u32[]{:S(2)}) collective-permute-start(f32[224,256]{1,0:T(8,128)S(1)} %get-tuple-element.26), channel_id=1, source_target_pairs={{0,4},{4,0},{8,12},{12,8},{16,20},{20,16},{24,28},{28,24},{1,5},{5... | collective-permute-start | bytes 688136 | tf_op jit(solution)/shard_map/ppermute | solution.py:400
  72.7 10.6 %collective-permute-start.17 = (f32[256,256]{1,0:T(8,128)S(1)}, f32[256,256]{1,0:T(8,128)S(1)}, u32[]{:S(2)}, u32[]{:S(2)}) collective-permute-start(f32[256,256]{1,0:T(8,128)S(1)} %add.25.own_p), channel_id=1, source_target_pairs={{0,4},{4,0},{8,12},{12,8},{16,20},{20,16},{24,28},{28,24},{1,5},{5... | collective-permute-start | bytes 786440 | tf_op jit(solution)/shard_map/ppermute | solution.py:400
  79.1 4.2 %collective-permute-start.19 = (f32[224,256]{1,0:T(8,128)S(1)}, f32[224,256]{1,0:T(8,128)S(1)}, u32[]{:S(2)}, u32[]{:S(2)}) collective-permute-start(f32[224,256]{1,0:T(8,128)S(1)} %collective-permute-done.18.refs_0_), channel_id=1, source_target_pairs={{0,1},{1,0},{2,3},{3,2},{4,5},{5,4},{6,7},{7,6},{8,9},{9,8},{10,11... | collective-permute-start | bytes 688136 | tf_op jit(solution)/shard_map/ppermute | solution.py:400
  92.4 8.5 %collective-permute-start.21 = (f32[224,256]{1,0:T(8,128)S(1)}, f32[224,256]{1,0:T(8,128)S(1)}, u32[]{:S(2)}, u32[]{:S(2)}) collective-permute-start(f32[224,256]{1,0:T(8,128)S(1)} %get-tuple-element.29), channel_id=1, source_target_pairs={{0,8},{4,12},{8,0},{12,4},{16,24},{20,28},{24,16},{28,20},{1,9},{5... | collective-permute-start | bytes 688136 | tf_op jit(solution)/shard_map/ppermute | solution.py:400
  92.5 11.8 %collective-permute-start.20 = (f32[256,256]{1,0:T(8,128)S(1)}, f32[256,256]{1,0:T(8,128)S(1)}, u32[]{:S(2)}, u32[]{:S(2)}) collective-permute-start(f32[256,256]{1,0:T(8,128)S(1)} %add.26.own_p), channel_id=1, source_target_pairs={{0,8},{4,12},{8,0},{12,4},{16,24},{20,28},{24,16},{28,20},{1,9},{5... | collective-permute-start | bytes 786440 | tf_op jit(solution)/shard_map/ppermute | solution.py:400
  100.9 3.4 %collective-permute-start.22 = (f32[224,256]{1,0:T(8,128)S(1)}, f32[224,256]{1,0:T(8,128)S(1)}, u32[]{:S(2)}, u32[]{:S(2)}) collective-permute-start(f32[224,256]{1,0:T(8,128)S(1)} %collective-permute-done.21.refs_0_), channel_id=1, source_target_pairs={{0,1},{1,0},{2,3},{3,2},{4,5},{5,4},{6,7},{7,6},{8,9},{9,8},{10,11... | collective-permute-start | bytes 688136 | tf_op jit(solution)/shard_map/ppermute | solution.py:400
  113.2 13.4 %collective-permute-start.24 = (f32[112,256]{1,0:T(8,128)S(1)}, f32[112,256]{1,0:T(8,128)S(1)}, u32[]{:S(2)}, u32[]{:S(2)}) collective-permute-start(f32[112,256]{1,0:T(8,128)S(1)} %get-tuple-element.32), channel_id=1, source_target_pairs={{0,16},{4,20},{8,24},{12,28},{16,0},{20,4},{24,8},{28,12},{1,17},{... | collective-permute-start | bytes 344072 | tf_op jit(solution)/shard_map/ppermute | solution.py:400
  114.2 17.1 %collective-permute-start.23 = (f32[256,256]{1,0:T(8,128)S(1)}, f32[256,256]{1,0:T(8,128)S(1)}, u32[]{:S(2)}, u32[]{:S(2)}) collective-permute-start(f32[256,256]{1,0:T(8,128)S(1)} %add.27.own_p), channel_id=1, source_target_pairs={{0,16},{4,20},{8,24},{12,28},{16,0},{20,4},{24,8},{28,12},{1,17},{... | collective-permute-start | bytes 786440 | tf_op jit(solution)/shard_map/ppermute | solution.py:400
  126.6 4.8 %collective-permute-start.25 = (f32[112,256]{1,0:T(8,128)S(1)}, f32[112,256]{1,0:T(8,128)S(1)}, u32[]{:S(2)}, u32[]{:S(2)}) collective-permute-start(f32[112,256]{1,0:T(8,128)S(1)} %collective-permute-done.24.refs_0_), channel_id=1, source_target_pairs={{0,2},{1,3},{2,0},{3,1},{4,6},{5,7},{6,4},{7,5},{8,10},{9,11},{10,... | collective-permute-start | bytes 344072 | tf_op jit(solution)/shard_map/ppermute | solution.py:400
  127.8 3.6 %collective-permute-start.26 = (f32[112,256]{1,0:T(8,128)S(1)}, f32[112,256]{1,0:T(8,128)S(1)}, u32[]{:S(2)}, u32[]{:S(2)}) collective-permute-start(f32[112,256]{1,0:T(8,128)S(1)} %collective-permute-done.24.refs_0_), channel_id=1, source_target_pairs={{0,1},{1,0},{2,3},{3,2},{4,5},{5,4},{6,7},{7,6},{8,9},{9,8},{10,11... | collective-permute-start | bytes 344072 | tf_op jit(solution)/shard_map/ppermute | solution.py:400
  131.4 1.3 collective-permute-start.27

commit v6 on v5

--- a/solution.py
+++ b/solution.py
@@ -220,8 +220,13 @@
     return jnp.concatenate([top, bottom], axis=0), w
 
 
+def chip_side():
+    col = lax.axis_index("col")
+    return col & 1, col >> 1 & 1
+
+
 def first_kernel(
-    side, own_a, own_b, other_a, other_b, own_w, other_w, q_out, state, send
+    own_a, own_b, other_a, other_b, own_w, other_w, q_out, state, send
 ):
     q, upper, w = merge_math(
         (own_a[...] + own_b[...], (own_w[...],), None),
@@ -229,7 +234,7 @@
         1,
         True,
     )
-    store_state(side, upper, w, state, send)
+    store_state(chip_side(), upper, w, state, send)
     q_out[...] = q
 
 
@@ -243,7 +248,8 @@
     )
 
 
-def upper_kernel(level, is_last, has_buffer, pieces, side, own, own_p, other_p, *refs):
+def upper_kernel(level, is_last, has_buffer, pieces, own, own_p, other_p, *refs):
+    side = chip_side()
     near, far, refs = list(refs[:pieces]), list(refs[pieces : 2 * pieces]), list(refs[2 * pieces :])
     if has_buffer:
         refs.pop(0)
@@ -282,19 +288,19 @@
     return [pltpu.VMEM((2, rows, size), F32), pltpu.VMEM((rows // pieces, size), F32)]
 
 
-def first_merge(side, arrays, pieces):
+def first_merge(arrays, pieces):
     rows, size = arrays[0].shape
     return pl.pallas_call(
         first_kernel,
         out_shape=[jax.ShapeDtypeStruct((rows, size), F32)] + state_shapes(size, pieces),
-        in_specs=[SMEM] + [VMEM] * len(arrays),
+        in_specs=[VMEM] * len(arrays),
         out_specs=[VMEM] * 3,
         compiler_params=pltpu.CompilerParams(vmem_limit_bytes=SCRATCH_BYTES),
         name="first_merge",
-    )(side, *near_core(arrays))
-
-
-def upper_merge(level, levels, side, arrays, buffer, pieces):
+    )(*near_core(arrays))
+
+
+def upper_merge(level, levels, arrays, buffer, pieces):
     size = arrays[1].shape[1]
     is_last = level == levels
     extra = [] if buffer is None else [buffer]
@@ -303,12 +309,12 @@
     return pl.pallas_call(
         functools.partial(upper_kernel, level, is_last, bool(extra), (len(arrays) - 3) // 2),
         out_shape=out_shape,
-        in_specs=[SMEM] + [VMEM] * len(arrays) + [ANY] * len(extra),
+        in_specs=[VMEM] * len(arrays) + [ANY] * len(extra),
         out_specs=[ANY] + [VMEM] * (len(out_shape) - 1),
         scratch_shapes=[pltpu.VMEM((size, size), F32), pltpu.SemaphoreType.DMA(())],
-        input_output_aliases={1 + len(arrays): 0} if extra else {},
+        input_output_aliases={len(arrays): 0} if extra else {},
         compiler_params=pltpu.CompilerParams(vmem_limit_bytes=SCRATCH_BYTES),
-    )(side, *near_core(arrays), *extra)
+    )(*near_core(arrays), *extra)
 
 
 def load_kernel(keys, place, mask, front, own, rows, own_here, arrived):
@@ -406,7 +412,6 @@
     col_levels, row_levels = col_count.bit_length() - 1, row_count.bit_length() - 1
     levels = col_levels + row_levels
     place = jnp.stack([row_index, col_index]).astype(jnp.int32)
-    side = jnp.stack([col_index & 1, col_index >> 1 & 1]).astype(jnp.int32)
     bits = [("col", b) for b in range(col_levels)] + [("row", b) for b in range(row_levels)]
 
     chunks = {0: probes}
@@ -447,7 +452,7 @@
         return 2 if level == levels and col_levels > 1 and row_levels > 0 else 1
 
     leaf_basis, state, send = first_merge(
-        side, (own_a, own_b, other_a, other_b, own_w, other_w), pieces(2)
+        (own_a, own_b, other_a, other_b, own_w, other_w), pieces(2)
     )
     buffer = None
     for level, (axis, bit) in list(enumerate(bits, start=1))[1:]:
@@ -460,7 +465,6 @@
         buffer, *rest = upper_merge(
             level,
             levels,
-            side,
             (state, own_p[level], other_p[level], *near, *far),
             buffer,
             pieces(level + 1),

time: 142 us -> 139 us (0.979)
  Pallas kernels: 48.3 us -> 45.6 us
    pallas_call x4, Pallas kernels: 35.9 us -> 33.7 us  [upper_merge(): pl.pallas_call(functools.partial(upper_kernel, level, is_last, bool(extra...]
where the time goes in v6:
time: 139 us
  waiting for transfers between devices  61.9 us (45%)
  Pallas kernels  45.6 us (33%)
  starting transfers between devices  29.9 us (22%)
    ppermute x27, waiting for transfers between devices, swap(): lax.ppermute(x, axis, [(i, i ^ 1 << bit) for i in range(lax.axis_size(axi...  61.9 us
    pallas_call x4, Pallas kernels, upper_merge(): pl.pallas_call(functools.partial(upper_kernel, level, is_last, bool(extra...  33.7 us
    ppermute x27, starting transfers between devices, swap(): lax.ppermute(x, axis, [(i, i ^ 1 << bit) for i in range(lax.axis_size(axi...  29.1 us
    pallas_call x1, Pallas kernels, first_merge(): pl.pallas_call(first_kernel, out_shape=[jax.ShapeDtypeStruct((rows, size)...  7.89 us
  transfers between devices with their start and end apart: 28, of which 15 were waited for; matrix products, arithmetic and copies ran while one was open for 0% of the time, Pallas kernels for 8%

profile of v6, /device:TPU:0, one launch (start us, length us, event | category | flops | bytes accessed | tf_op | source)
XLA Modules:
  0.0 139.3 jit_solution(1914568887897264972)
XLA Ops:
  0.6 4.1 %collective-permute-start.1 = (bf16[256,256]{1,0:T(8,128)(2,1)}, bf16[256,256]{1,0:T(8,128)(2,1)S(1)}, u32[]{:S(2)}, u32[]{:S(2)}) collective-permute-start(bf16[256,256]{1,0:T(8,128)(2,1)} %own.1), channel_id=1, source_target_pairs={{0,16},{4,20},{8,24},{12,28},{16,0},{20,4},{24,8},{28,12},{1,17},{... | collective-permute-start | bytes 393224 | tf_op jit(solution)/shard_map/ppermute | solution.py:406
  4.8 1.6 %collective-permute-start.3 = (bf16[256,256]{1,0:T(8,128)(2,1)}, bf16[256,256]{1,0:T(8,128)(2,1)S(1)}, u32[]{:S(2)}, u32[]{:S(2)}) collective-permute-start(bf16[256,256]{1,0:T(8,128)(2,1)} %own.1), channel_id=1, source_target_pairs={{0,8},{4,12},{8,0},{12,4},{16,24},{20,28},{24,16},{28,20},{1,9},{5... | collective-permute-start | bytes 393224 | tf_op jit(solution)/shard_map/ppermute | solution.py:406
  6.3 5.0 %collective-permute-done.1.refs_2_ = bf16[256,256]{1,0:T(8,128)(2,1)S(1)} collective-permute-done((bf16[256,256]{1,0:T(8,128)(2,1)}, bf16[256,256]{1,0:T(8,128)(2,1)S(1)}, u32[]{:S(2)}, u32[]{:S(2)}) %collective-permute-start.1) | collective-permute-done | bytes 131104 | tf_op jit(solution)/shard_map/ppermute | solution.py:406
  11.4 1.6 %collective-permute-start.2 = (bf16[256,256]{1,0:T(8,128)(2,1)S(1)}, bf16[256,256]{1,0:T(8,128)(2,1)S(1)}, u32[]{:S(2)}, u32[]{:S(2)}) collective-permute-start(bf16[256,256]{1,0:T(8,128)(2,1)S(1)} %collective-permute-done.1.refs_2_), channel_id=1, source_target_pairs={{0,4},{4,0},{8,12},{12,8},{16,20},{20,16},{24,28},{28,24},{1,5},{5... | collective-permute-start | bytes 393224 | tf_op jit(solution)/shard_map/ppermute | solution.py:406
  12.9 0.5 collective-permute-start
  13.4 0.7 collective-permute-start.5
  14.1 1.5 %collective-permute-start.4 = (bf16[256,256]{1,0:T(8,128)(2,1)S(1)}, bf16[256,256]{1,0:T(8,128)(2,1)S(1)}, u32[]{:S(2)}, u32[]{:S(2)}) collective-permute-start(bf16[256,256]{1,0:T(8,128)(2,1)S(1)} %collective-permute-done.3.refs_4_), channel_id=1, source_target_pairs={{0,4},{4,0},{8,12},{12,8},{16,20},{20,16},{24,28},{28,24},{1,5},{5... | collective-permute-start | bytes 393224 | tf_op jit(solution)/shard_map/ppermute | solution.py:406
  15.7 2.1 %collective-permute-done.2.refs_3_ = bf16[256,256]{1,0:T(8,128)(2,1)S(1)} collective-permute-done((bf16[256,256]{1,0:T(8,128)(2,1)S(1)}, bf16[256,256]{1,0:T(8,128)(2,1)S(1)}, u32[]{:S(2)}, u32[]{:S(2)}) %collective-permute-start.2) | collective-permute-done | bytes 131104 | tf_op jit(solution)/shard_map/ppermute | solution.py:406
  17.8 0.7 collective-permute-start.6
  18.5 0.1 pad_add_fusion.place
  18.5 0.7 copy-done
  19.2 2.8 %load_front.1 = (bf16[4,256,2048]{2,1,0:T(8,128)(2,1)S(1)}, bf16[256,256]{1,0:T(8,128)(2,1)S(1)}) custom-call(s32[2]{0:T(128)S(1)} %pad_add_fusion.place, s32[4,8]{1,0:T(4,128)S(1)} %copy-done, bf16[1024,2048]{1,0:T(8,128)(2,1)} %front.1, bf16[256,256]{1,0:T(8,128)(2,1)} %own.1), custom_call_target="tpu_custom_call" | custom-call | tf_op jit(solution)/shard_map/load_front/pallas_call | solution.py:364
  22.0 0.0 copy-start.2
  22.1 0.7 collective-permute-done.6.refs_7_
  22.7 1.2 samples.1
  24.0 0.1 collective-permute-start.7
  24.0 1.9 %collective-permute-done.7 = f32[2,256,256]{2,1,0:T(8,128)S(1)} collective-permute-done((f32[2,256,256]{2,1,0:T(8,128)S(1)}, f32[2,256,256]{2,1,0:T(8,128)S(1)}, u32[]{:S(2)}, u32[]{:S(2)}) %collective-permute-start.7) | collective-permute-done | bytes 524320 | tf_op jit(solution)/shard_map/ppermute | solution.py:406
  25.9 0.1 slice_add_fusion
  26.0 1.3 collective-permute-start.8
  27.4 0.8 collective-permute-start.11
  28.2 2.3 %collective-permute-start.9 = (f32[256,256]{1,0:T(8,128)S(1)}, f32[256,256]{1,0:T(8,128)S(1)}, u32[]{:S(2)}, u32[]{:S(2)}) collective-permute-start(f32[256,256]{1,0:T(8,128)S(1)} %get-tuple-element.35.own_a), channel_id=1, source_target_pairs={{0,1},{1,0},{2,3},{3,2},{4,5},{5,4},{6,7},{7,6},{8,9},{9,8},{10,11... | collective-permute-start | bytes 786440 | tf_op jit(solution)/shard_map/ppermute | solution.py:406
  30.6 4.1 %collective-permute-done.8 = f32[1,256,256]{2,1,0:T(8,128)S(1)} collective-permute-done((f32[1,256,256]{2,1,0:T(8,128)S(1)}, f32[1,256,256]{2,1,0:T(8,128)S(1)}, u32[]{:S(2)}, u32[]{:S(2)}) %collective-permute-start.8) | collective-permute-done | bytes 262176 | tf_op jit(solution)/shard_map/ppermute | solution.py:406
  34.7 0.5 collective-permute-start.12
  35.2 0.1 collective-permute-start.13
  35.3 1.1 collective-permute-done.12.other_w
  36.4 7.9 %first_merge.1 = (f32[256,256]{1,0:T(8,128)}, f32[2,224,256]{2,1,0:T(8,128)S(1)}, f32[224,256]{1,0:T(8,128)S(1)}) custom-call(f32[256,256]{1,0:T(8,128)S(1)} %get-tuple-element.35.own_a, f32[256,256]{1,0:T(8,128)S(1)} %bitcast.6, f32[256,256]{1,0:T(8,128)S(1)} %collective-permute-done.9.other_a, f32[256,256]{1,0:T(8,128)S(1)} %collective-permute-done.10.other_b, ...), custom_call_target="tpu_custom_call" | custom-call | tf_op jit(solution)/shard_map/first_merge/pallas_call | solution.py:293
  44.3 2.6 %collective-permute-start.15 = (f32[224,256]{1,0:T(8,128)S(1)}, f32[224,256]{1,0:T(8,128)S(1)}, u32[]{:S(2)}, u32[]{:S(2)}) collective-permute-start(f32[224,256]{1,0:T(8,128)S(1)} %get-tuple-element.24), channel_id=1, source_target_pairs={{0,2},{1,3},{2,0},{3,1},{4,6},{5,7},{6,4},{7,5},{8,10},{9,11},{10,... | collective-permute-start | bytes 688136 | tf_op jit(solution)/shard_map/ppermute | solution.py:406
  46.9 0.1 collective-permute-start.14
  47.0 6.3 %collective-permute-done.15.refs_0_ = f32[224,256]{1,0:T(8,128)S(1)} collective-permute-done((f32[224,256]{1,0:T(8,128)S(1)}, f32[224,256]{1,0:T(8,128)S(1)}, u32[]{:S(2)}, u32[]{:S(2)}) %collective-permute-start.15) | collective-permute-done | bytes 229408 | tf_op jit(solution)/shard_map/ppermute | solution.py:406
  53.3 5.1 %collective-permute-done.14.other_p = f32[256,256]{1,0:T(8,128)S(1)} collective-permute-done((f32[256,256]{1,0:T(8,128)S(1)}, f32[256,256]{1,0:T(8,128)S(1)}, u32[]{:S(2)}, u32[]{:S(2)}) %collective-permute-start.14) | collective-permute-done | bytes 262176 | tf_op jit(solution)/shard_map/ppermute | solution.py:406
  58.4 8.3 %shard_map.59 = (f32[4,256,256]{2,1,0:T(8,128)}, f32[2,224,256]{2,1,0:T(8,128)S(1)}, f32[224,256]{1,0:T(8,128)S(1)}) custom-call(f32[2,224,256]{2,1,0:T(8,128)S(1)} %get-tuple-element.23.own, f32[256,256]{1,0:T(8,128)S(1)} %add.24.own_p, f32[256,256]{1,0:T(8,128)S(1)} %collective-permute-done.14.other_p, f32[224,256]{1,0:T(8,128)S(1)} %collective-permute-done.15.refs_0_, ...), custom_call_target="tpu_custom_call" | custom-call | tf_op jit(solution)/shard_map/pallas_call | solution.py:309
  66.7 4.8 %collective-permute-start.18 = (f32[224,256]{1,0:T(8,128)S(1)}, f32[224,256]{1,0:T(8,128)S(1)}, u32[]{:S(2)}, u32[]{:S(2)}) collective-permute-start(f32[224,256]{1,0:T(8,128)S(1)} %get-tuple-element.26), channel_id=1, source_target_pairs={{0,4},{4,0},{8,12},{12,8},{16,20},{20,16},{24,28},{28,24},{1,5},{5... | collective-permute-start | bytes 688136 | tf_op jit(solution)/shard_map/ppermute | solution.py:406
  71.6 0.1 collective-permute-start.17
  71.7 6.3 %collective-permute-done.18.refs_0_ = f32[224,256]{1,0:T(8,128)S(1)} collective-permute-done((f32[224,256]{1,0:T(8,128)S(1)}, f32[224,256]{1,0:T(8,128)S(1)}, u32[]{:S(2)}, u32[]{:S(2)}) %collective-permute-start.18) | collective-permute-done | bytes 229408 | tf_op jit(solution)/shard_map/ppermute | solution.py:406
  78.0 4.2 %collective-permute-done.17.other_p = f32[256,256]{1,0:T(8,128)S(1)} collective-permute-done((f32[256,256]{1,0:T(8,128)S(1)}, f32[256,256]{1,0:T(8,128)S(1)}, u32[]{:S(2)}, u32[]{:S(2)}) %collective-permute-start.17) | collective-permute-done | bytes 262176 | tf_op jit(solution)/shard_map/ppermute | solution.py:406
  82.3 8.5 %shard_map.60 = (f32[4,256,256]{2,1,0:T(8,128)}, f32[2,224,256]{2,1,0:T(8,128)S(1)}, f32[224,256]{1,0:T(8,128)S(1)}) custom-call(f32[2,224,256]{2,1,0:T(8,128)S(1)} %get-tuple-element.25.own, f32[256,256]{1,0:T(8,128)S(1)} %add.25.own_p, f32[256,256]{1,0:T(8,128)S(1)} %collective-permute-done.17.other_p, ...), custom_call_target="tpu_custom_call", output_to_operand_aliasing={{0}: (5, {})} | custom-call | tf_op jit(solution)/shard_map/pallas_call | solution.py:309
  90.8 0.1 collective-permute-start.21
  90.9 2.1 %collective-permute-start.20 = (f32[256,256]{1,0:T(8,128)S(1)}, f32[256,256]{1,0:T(8,128)S(1)}, u32[]{:S(2)}, u32[]{:S(2)}) collective-permute-start(f32[256,256]{1,0:T(8,128)S(1)} %add.26.own_p), channel_id=1, source_target_pairs={{0,8},{4,12},{8,0},{12,4},{16,24},{20,28},{24,16},{28,20},{1,9},{5... | collective-permute-start | bytes 786440 | tf_op jit(solution)/shard_map/ppermute | solution.py:406
  93.0 6.3 %collective-permute-done.21.refs_0_ = f32[224,256]{1,0:T(8,128)S(1)} collective-permute-done((f32[224,256]{1,0:T(8,128)S(1)}, f32[224,256]{1,0:T(8,128)S(1)}, u32[]{:S(2)}, u32[]{:S(2)}) %collective-permute-start.21) | collective-permute-done | bytes 229408 | tf_op jit(solution)/shard_map/ppermute | solution.py:406
  99.3 3.4 %collective-permute-done.20.other_p = f32[256,256]{1,0:T(8,128)S(1)} collective-permute-done((f32[256,256]{1,0:T(8,128)S(1)}, f32[256,256]{1,0:T(8,128)S(1)}, u32[]{:S(2)}, u32[]{:S(2)}) %collective-permute-start.20) | collective-permute-done | bytes 262176 | tf_op jit(solution)/shard_map/ppermute | solution.py:406
  102.7 8.3 %shard_map.61 = (f32[4,256,256]{2,1,0:T(8,128)}, f32[2,224,256]{2,1,0:T(8,128)S(1)}, f32[112,256]{1,0:T(8,128)S(1)}) custom-call(f32[2,224,256]{2,1,0:T(8,128)S(1)} %get-tuple-element.28.own, f32[256,256]{1,0:T(8,128)S(1)} %add.26.own_p, f32[256,256]{1,0:T(8,128)S(1)} %collective-permute-done.20.other_p, ...), custom_call_target="tpu_custom_call", output_to_operand_aliasing={{0}: (5, {})} | custom-call | tf_op jit(solution)/shard_map/pallas_call | solution.py:309
  111.0 1.0 collective-permute-start.24
  112.1 2.0 %collective-permute-start.23 = (f32[256,256]{1,0:T(8,128)S(1)}, f32[256,256]{1,0:T(8,128)S(1)}, u32[]{:S(2)}, u32[]{:S(2)}) collective-permute-start(f32[256,256]{1,0:T(8,128)S(1)} %add.27.own_p), channel_id=1, source_target_pairs={{0,16},{4,20},{8,24},{12,28},{16,0},{20,4},{24,8},{28,12},{1,17},{... | collective-permute-start | bytes 786440 | tf_op jit(solution)/shard_map/ppermute | solution.py:406
  114.1 10.3 %collective-permute-done.24.refs_0_ = f32[112,256]{1,0:T(8,128)S(1)} collective-permute-done((f32[112,256]{1,0:T(8,128)S(1)}, f32[112,256]{1,0:T(8,128)S(1)}, u32[]{:S(2)}, u32[]{:S(2)}) %collective-permute-start.24) | collective-permute-done | bytes 114720 | tf_op jit(solution)/shard_map/ppermute | solution.py:406
  124.4 1.3 collective-permute-start.25
  125.7 3.5 %collective-permute-done.25.refs_1_ = f32[112,256]{1,0:T(8,128)S(1)} collective-permute-done((f32[112,256]{1,0:T(8,128)S(1)}, f32[112,256]{1,0:T(8,128)S(1)}, u32[]{:S(2)}, u32[]{:S(2)}) %collective-permute-start.25) | collective-permute-done | bytes 114720 | tf_op jit(solution)/shard_map/ppermute | solution.py:406
  129.2 1.3 collective-permute-done.27.refs_3_
  130.5 8.6 %shard_map.62 = f32[4,256,256]{2,1,0:T(8,128)} custom-call(f32[2,224,256]{2,1,0:T(8,128)S(1)} %get-tuple-element.31.own, f32[256,256]{1,0:T(8,128)S(1)} %add.27.own_p, f32[256,256]{1,0:T(8,128)S(1)} %collective-permute-done.23.other_p, f32[112,256]{1,0:T(8,128)S(1)} %collective-permute-done.24.refs_0_, ...), custom_call_target="tpu_custom_call", output_to_operand_aliasing={{}: (7, {})} | custom-call | tf_op jit(solution)/shard_map/pallas_call | solution.py:309
  (27 shorter events, 0.2 us)
Async XLA Ops:
  0.6 10.8 %collective-permute-start.1 = (bf16[256,256]{1,0:T(8,128)(2,1)}, bf16[256,256]{1,0:T(8,128)(2,1)S(1)}, u32[]{:S(2)}, u32[]{:S(2)}) collective-permute-start(bf16[256,256]{1,0:T(8,128)(2,1)} %own.1), channel_id=1, source_target_pairs={{0,16},{4,20},{8,24},{12,28},{16,0},{20,4},{24,8},{28,12},{1,17},{... | collective-permute-start | bytes 393224 | tf_op jit(solution)/shard_map/ppermute | solution.py:406
  4.8 9.4 %collective-permute-start.3 = (bf16[256,256]{1,0:T(8,128)(2,1)}, bf16[256,256]{1,0:T(8,128)(2,1)S(1)}, u32[]{:S(2)}, u32[]{:S(2)}) collective-permute-start(bf16[256,256]{1,0:T(8,128)(2,1)} %own.1), channel_id=1, source_target_pairs={{0,8},{4,12},{8,0},{12,4},{16,24},{20,28},{24,16},{28,20},{1,9},{5... | collective-permute-start | bytes 393224 | tf_op jit(solution)/shard_map/ppermute | solution.py:406
  11.4 6.4 %collective-permute-start.2 = (bf16[256,256]{1,0:T(8,128)(2,1)S(1)}, bf16[256,256]{1,0:T(8,128)(2,1)S(1)}, u32[]{:S(2)}, u32[]{:S(2)}) collective-permute-start(bf16[256,256]{1,0:T(8,128)(2,1)S(1)} %collective-permute-done.1.refs_2_), channel_id=1, source_target_pairs={{0,4},{4,0},{8,12},{12,8},{16,20},{20,16},{24,28},{28,24},{1,5},{5... | collective-permute-start | bytes 393224 | tf_op jit(solution)/shard_map/ppermute | solution.py:406
  12.9 9.1 %collective-permute-start = (bf16[256,256]{1,0:T(8,128)(2,1)}, bf16[256,256]{1,0:T(8,128)(2,1)S(1)}, u32[]{:S(2)}, u32[]{:S(2)}) collective-permute-start(bf16[256,256]{1,0:T(8,128)(2,1)} %own.1), channel_id=1, source_target_pairs={{0,4},{4,0},{8,12},{12,8},{16,20},{20,16},{24,28},{28,24},{1,5},{5... | collective-permute-start | bytes 393224 | tf_op jit(solution)/shard_map/ppermute | solution.py:406
  13.4 8.6 %collective-permute-start.5 = (bf16[256,256]{1,0:T(8,128)(2,1)S(1)}, bf16[256,256]{1,0:T(8,128)(2,1)S(1)}, u32[]{:S(2)}, u32[]{:S(2)}) collective-permute-start(bf16[256,256]{1,0:T(8,128)(2,1)S(1)} %collective-permute-done.1.refs_2_), channel_id=1, source_target_pairs={{0,8},{4,12},{8,0},{12,4},{16,24},{20,28},{24,16},{28,20},{1,9},{5... | collective-permute-start | bytes 393224 | tf_op jit(solution)/shard_map/ppermute | solution.py:406
  14.1 7.9 %collective-permute-start.4 = (bf16[256,256]{1,0:T(8,128)(2,1)S(1)}, bf16[256,256]{1,0:T(8,128)(2,1)S(1)}, u32[]{:S(2)}, u32[]{:S(2)}) collective-permute-start(bf16[256,256]{1,0:T(8,128)(2,1)S(1)} %collective-permute-done.3.refs_4_), channel_id=1, source_target_pairs={{0,4},{4,0},{8,12},{12,8},{16,20},{20,16},{24,28},{28,24},{1,5},{5... | collective-permute-start | bytes 393224 | tf_op jit(solution)/shard_map/ppermute | solution.py:406
  17.8 5.0 %collective-permute-start.6 = (bf16[256,256]{1,0:T(8,128)(2,1)S(1)}, bf16[256,256]{1,0:T(8,128)(2,1)S(1)}, u32[]{:S(2)}, u32[]{:S(2)}) collective-permute-start(bf16[256,256]{1,0:T(8,128)(2,1)S(1)} %collective-permute-done.2.refs_3_), channel_id=1, source_target_pairs={{0,8},{4,12},{8,0},{12,4},{16,24},{20,28},{24,16},{28,20},{1,9},{5... | collective-permute-start | bytes 393224 | tf_op jit(solution)/shard_map/ppermute | solution.py:406
  18.5 0.7 copy-start
  22.0 5.4 %copy-start.2 = (bf16[256,256]{1,0:T(8,128)(2,1)S(1)}, bf16[256,256]{1,0:T(8,128)(2,1)}, u32[]{:S(2)}) copy-start(bf16[256,256]{1,0:T(8,128)(2,1)} %own.1) | copy-start | bytes 393220
  22.0 13.2 %copy-start.1 = (f32[256,256]{1,0:T(8,128)S(1)}, f32[256,256]{1,0:T(8,128)}, u32[]{:S(2)}) copy-start(f32[256,256]{1,0:T(8,128)} %param.7) | copy-start | bytes 786436
  24.0 2.0 %collective-permute-start.7 = (f32[2,256,256]{2,1,0:T(8,128)S(1)}, f32[2,256,256]{2,1,0:T(8,128)S(1)}, u32[]{:S(2)}, u32[]{:S(2)}) collective-permute-start(f32[2,256,256]{2,1,0:T(8,128)S(1)} %get-tuple-element.21), channel_id=1, source_target_pairs={{0,1},{1,0},{2,3},{3,2},{4,5},{5,4},{6,7},{7,6},{8,9},{9,8},{10,11... | collective-permute-start | bytes 1572872 | tf_op jit(solution)/shard_map/ppermute | solution.py:406
  26.0 8.7 %collective-permute-start.8 = (f32[1,256,256]{2,1,0:T(8,128)S(1)}, f32[1,256,256]{2,1,0:T(8,128)S(1)}, u32[]{:S(2)}, u32[]{:S(2)}) collective-permute-start(f32[1,256,256]{2,1,0:T(8,128)S(1)} %get-tuple-element.34), channel_id=1, source_target_pairs={{0,2},{1,3},{2,0},{3,1},{4,6},{5,7},{6,4},{7,5},{8,10},{9,11},{10,... | collective-permute-start | bytes 786440 | tf_op jit(solution)/shard_map/ppermute | solution.py:406
  27.4 7.3 %collective-permute-start.11 = (bf16[256,256]{1,0:T(8,128)(2,1)S(1)}, bf16[256,256]{1,0:T(8,128)(2,1)S(1)}, u32[]{:S(2)}, u32[]{:S(2)}) collective-permute-start(bf16[256,256]{1,0:T(8,128)(2,1)S(1)} %copy-done.2), channel_id=1, source_target_pairs={{0,0},{4,1},{8,2},{12,3},{16,4},{20,5},{24,6},{28,7},{1,8},{5,9},{... | collective-permute-start | bytes 393224 | tf_op jit(solution)/shard_map/ppermute | solution.py:428
  28.2 8.2 %collective-permute-start.9 = (f32[256,256]{1,0:T(8,128)S(1)}, f32[256,256]{1,0:T(8,128)S(1)}, u32[]{:S(2)}, u32[]{:S(2)}) collective-permute-start(f32[256,256]{1,0:T(8,128)S(1)} %get-tuple-element.35.own_a), channel_id=1, source_target_pairs={{0,1},{1,0},{2,3},{3,2},{4,5},{5,4},{6,7},{7,6},{8,9},{9,8},{10,11... | collective-permute-start | bytes 786440 | tf_op jit(solution)/shard_map/ppermute | solution.py:406
  34.7 1.7 %collective-permute-start.10 = (f32[256,256]{1,0:T(8,128)S(1)}, f32[256,256]{1,0:T(8,128)S(1)}, u32[]{:S(2)}, u32[]{:S(2)}) collective-permute-start(f32[256,256]{1,0:T(8,128)S(1)} %bitcast.5), channel_id=1, source_target_pairs={{0,1},{1,0},{2,3},{3,2},{4,5},{5,4},{6,7},{7,6},{8,9},{9,8},{10,11... | collective-permute-start | bytes 786440 | tf_op jit(solution)/shard_map/ppermute | solution.py:406
  34.7 1.7 %collective-permute-start.12 = (bf16[256,256]{1,0:T(8,128)(2,1)S(1)}, bf16[256,256]{1,0:T(8,128)(2,1)S(1)}, u32[]{:S(2)}, u32[]{:S(2)}) collective-permute-start(bf16[256,256]{1,0:T(8,128)(2,1)S(1)} %collective-permute-done.11.own_w), channel_id=1, source_target_pairs={{0,1},{1,0},{2,3},{3,2},{4,5},{5,4},{6,7},{7,6},{8,9},{9,8},{10,11... | collective-permute-start | bytes 393224 | tf_op jit(solution)/shard_map/ppermute | solution.py:406
  35.2 11.7 %collective-permute-start.13 = (f32[256,256]{1,0:T(8,128)S(1)}, f32[256,256]{1,0:T(8,128)S(1)}, u32[]{:S(2)}, u32[]{:S(2)}) collective-permute-start(f32[256,256]{1,0:T(8,128)S(1)} %copy-done.1), channel_id=1, source_target_pairs={{0,1},{1,0},{2,3},{3,2},{4,5},{5,4},{6,7},{7,6},{8,9},{9,8},{10,11... | collective-permute-start | bytes 786440 | tf_op jit(solution)/shard_map/ppermute | solution.py:406
  44.3 9.0 %collective-permute-start.15 = (f32[224,256]{1,0:T(8,128)S(1)}, f32[224,256]{1,0:T(8,128)S(1)}, u32[]{:S(2)}, u32[]{:S(2)}) collective-permute-start(f32[224,256]{1,0:T(8,128)S(1)} %get-tuple-element.24), channel_id=1, source_target_pairs={{0,2},{1,3},{2,0},{3,1},{4,6},{5,7},{6,4},{7,5},{8,10},{9,11},{10,... | collective-permute-start | bytes 688136 | tf_op jit(solution)/shard_map/ppermute | solution.py:406
  46.9 11.5 %collective-permute-start.14 = (f32[256,256]{1,0:T(8,128)S(1)}, f32[256,256]{1,0:T(8,128)S(1)}, u32[]{:S(2)}, u32[]{:S(2)}) collective-permute-start(f32[256,256]{1,0:T(8,128)S(1)} %add.24.own_p), channel_id=1, source_target_pairs={{0,2},{1,3},{2,0},{3,1},{4,6},{5,7},{6,4},{7,5},{8,10},{9,11},{10,... | collective-permute-start | bytes 786440 | tf_op jit(solution)/shard_map/ppermute | solution.py:406
  53.3 5.1 %collective-permute-start.16 = (f32[224,256]{1,0:T(8,128)S(1)}, f32[224,256]{1,0:T(8,128)S(1)}, u32[]{:S(2)}, u32[]{:S(2)}) collective-permute-start(f32[224,256]{1,0:T(8,128)S(1)} %collective-permute-done.15.refs_0_), channel_id=1, source_target_pairs={{0,1},{1,0},{2,3},{3,2},{4,5},{5,4},{6,7},{7,6},{8,9},{9,8},{10,11... | collective-permute-start | bytes 688136 | tf_op jit(solution)/shard_map/ppermute | solution.py:406
  66.7 11.3 %collective-permute-start.18 = (f32[224,256]{1,0:T(8,128)S(1)}, f32[224,256]{1,0:T(8,128)S(1)}, u32[]{:S(2)}, u32[]{:S(2)}) collective-permute-start(f32[224,256]{1,0:T(8,128)S(1)} %get-tuple-element.26), channel_id=1, source_target_pairs={{0,4},{4,0},{8,12},{12,8},{16,20},{20,16},{24,28},{28,24},{1,5},{5... | collective-permute-start | bytes 688136 | tf_op jit(solution)/shard_map/ppermute | solution.py:406
  71.6 10.7 %collective-permute-start.17 = (f32[256,256]{1,0:T(8,128)S(1)}, f32[256,256]{1,0:T(8,128)S(1)}, u32[]{:S(2)}, u32[]{:S(2)}) collective-permute-start(f32[256,256]{1,0:T(8,128)S(1)} %add.25.own_p), channel_id=1, source_target_pairs={{0,4},{4,0},{8,12},{12,8},{16,20},{20,16},{24,28},{28,24},{1,5},{5... | collective-permute-start | bytes 786440 | tf_op jit(solution)/shard_map/ppermute | solution.py:406
  78.0 4.2 %collective-permute-start.19 = (f32[224,256]{1,0:T(8,128)S(1)}, f32[224,256]{1,0:T(8,128)S(1)}, u32[]{:S(2)}, u32[]{:S(2)}) collective-permute-start(f32[224,256]{1,0:T(8,128)S(1)} %collective-permute-done.18.refs_0_), channel_id=1, source_target_pairs={{0,1},{1,0},{2,3},{3,2},{4,5},{5,4},{6,7},{7,6},{8,9},{9,8},{10,11... | collective-permute-start | bytes 688136 | tf_op jit(solution)/shard_map/ppermute | solution.py:406
  90.8 8.5 %collective-permute-start.21 = (f32[224,256]{1,0:T(8,128)S(1)}, f32[224,256]{1,0:T(8,128)S(1)}, u32[]{:S(2)}, u32[]{:S(2)}) collective-permute-start(f32[224,256]{1,0:T(8,128)S(1)} %get-tuple-element.29), channel_id=1, source_target_pairs={{0,8},{4,12},{8,0},{12,4},{16,24},{20,28},{24,16},{28,20},{1,9},{5... | collective-permute-start | bytes 688136 | tf_op jit(solution)/shard_map/ppermute | solution.py:406
  90.9 11.8 %collective-permute-start.20 = (f32[256,256]{1,0:T(8,128)S(1)}, f32[256,256]{1,0:T(8,128)S(1)}, u32[]{:S(2)}, u32[]{:S(2)}) collective-permute-start(f32[256,256]{1,0:T(8,128)S(1)} %add.26.own_p), channel_id=1, source_target_pairs={{0,8},{4,12},{8,0},{12,4},{16,24},{20,28},{24,16},{28,20},{1,9},{5... | collective-permute-start | bytes 786440 | tf_op jit(solution)/shard_map/ppermute | solution.py:406
  99.3 3.4 %collective-permute-start.22 = (f32[224,256]{1,0:T(8,128)S(1)}, f32[224,256]{1,0:T(8,128)S(1)}, u32[]{:S(2)}, u32[]{:S(2)}) collective-permute-start(f32[224,256]{1,0:T(8,128)S(1)} %collective-permute-done.21.refs_0_), channel_id=1, source_target_pairs={{0,1},{1,0},{2,3},{3,2},{4,5},{5,4},{6,7},{7,6},{8,9},{9,8},{10,11... | collective-permute-start | bytes 688136 | tf_op jit(solution)/shard_map/ppermute | solution.py:406
  111.0 13.4 %collective-permute-start.24 = (f32[112,256]{1,0:T(8,128)S(1)}, f32[112,256]{1,0:T(8,128)S(1)}, u32[]{:S(2)}, u32[]{:S(2)}) collective-permute-start(f32[112,256]{1,0:T(8,128)S(1)} %get-tuple-element.32), channel_id=1, source_target_pairs={{0,16},{4,20},{8,24},{12,28},{16,0},{20,4},{24,8},{28,12},{1,17},{... | collective-permute-start | bytes 344072 | tf_op jit(solution)/shard_map/ppermute | solution.py:406
  112.1 17.1 %collective-permute-start.23 = (f32[256,256]{1,0:T(8,128)S(1)}, f32[256,256]{1,0:T(8,128)S(1)}, u32[]{:S(2)}, u32[]{:S(2)}) collective-permute-start(f32[256,256]{1,0:T(8,128)S(1)} %add.27.own_p), channel_id=1, source_target_pairs={{0,16},{4,20},{8,24},{12,28},{16,0},{20,4},{24,8},{28,12},{1,17},{... | collective-permute-start | bytes 786440 | tf_op jit(solution)/shard_map/ppermute | solution.py:406
  124.4 4.8 %collective-permute-start.25 = (f32[112,256]{1,0:T(8,128)S(1)}, f32[112,256]{1,0:T(8,128)S(1)}, u32[]{:S(2)}, u32[]{:S(2)}) collective-permute-start(f32[112,256]{1,0:T(8,128)S(1)} %collective-permute-done.24.refs_0_), channel_id=1, source_target_pairs={{0,2},{1,3},{2,0},{3,1},{4,6},{5,7},{6,4},{7,5},{8,10},{9,11},{10,... | collective-permute-start | bytes 344072 | tf_op jit(solution)/shard_map/ppermute | solution.py:406
  125.7 3.5 %collective-permute-start.26 = (f32[112,256]{1,0:T(8,128)S(1)}, f32[112,256]{1,0:T(8,128)S(1)}, u32[]{:S(2)}, u32[]{:S(2)}) collective-permute-start(f32[112,256]{1,0:T(8,128)S(1)} %collective-permute-done.24.refs_0_), channel_id=1, source_target_pairs={{0,1},{1,0},{2,3},{3,2},{4,5},{5,4},{6,7},{7,6},{8,9},{9,8},{10,11... | collective-permute-start | bytes 344072 | tf_op jit(solution)/shard_map/ppermute | solution.py:406
  129.2 1.3 collective-permute-start.27

commit v7 on v6

--- a/solution.py
+++ b/solution.py
@@ -248,14 +248,18 @@
     )
 
 
-def upper_kernel(level, is_last, has_buffer, pieces, own, own_p, other_p, *refs):
+def upper_kernel(level, is_last, has_earlier, has_buffer, pieces, own, own_p, other_p, *refs):
     side = chip_side()
     near, far, refs = list(refs[:pieces]), list(refs[pieces : 2 * pieces]), list(refs[2 * pieces :])
+    earlier = refs.pop(0) if has_earlier else None
     if has_buffer:
         refs.pop(0)
-    q_all = refs.pop(0)
-    outs = [] if is_last else [refs.pop(0), refs.pop(0)]
-    q_here, done = refs
+    q_all = refs.pop(0) if has_earlier or is_last else None
+    q_here, *outs = refs[:-1]
+    done = refs[-1]
+    if has_earlier:
+        early = pltpu.make_async_copy(earlier, q_all.at[level - 3], done.at[0])
+        early.start()
     is_first = side[0] == 0
     own_s, own_w = load_state(own[0], own[1])
     near, far = gather_half(side, near), gather_half(side, far)
@@ -267,11 +271,14 @@
         not is_last,
     )
     q_here[...] = q
-    copy = pltpu.make_async_copy(q_here, q_all.at[level - 2], done)
-    copy.start()
-    if not is_last:
+    if is_last:
+        late = pltpu.make_async_copy(q_here, q_all.at[level - 2], done.at[1])
+        late.start()
+        late.wait()
+    else:
         store_state(side, upper, w, *outs)
-    copy.wait()
+    if has_earlier:
+        early.wait()
 
 
 VMEM = pl.BlockSpec(memory_space=pltpu.VMEM)
@@ -300,21 +307,34 @@
     )(*near_core(arrays))
 
 
-def upper_merge(level, levels, arrays, buffer, pieces):
+def upper_merge(level, levels, arrays, earlier, buffer, pieces):
     size = arrays[1].shape[1]
     is_last = level == levels
+    held = list(arrays) + ([] if earlier is None else [earlier])
     extra = [] if buffer is None else [buffer]
-    out_shape = [jax.ShapeDtypeStruct((levels - 1, size, size), F32)]
-    out_shape += [] if is_last else state_shapes(size, pieces)
-    return pl.pallas_call(
-        functools.partial(upper_kernel, level, is_last, bool(extra), (len(arrays) - 3) // 2),
+    out_shape, out_specs = [], []
+    if is_last or earlier is not None:
+        out_shape.append(jax.ShapeDtypeStruct((levels - 1, size, size), F32))
+        out_specs.append(ANY)
+    here = pltpu.VMEM((size, size), F32)
+    if not is_last:
+        more = [here] + state_shapes(size, pieces)
+        out_shape += more
+        out_specs += [VMEM] * len(more)
+    results = pl.pallas_call(
+        functools.partial(
+            upper_kernel, level, is_last, earlier is not None, bool(extra), (len(arrays) - 3) // 2
+        ),
         out_shape=out_shape,
-        in_specs=[VMEM] * len(arrays) + [ANY] * len(extra),
-        out_specs=[ANY] + [VMEM] * (len(out_shape) - 1),
-        scratch_shapes=[pltpu.VMEM((size, size), F32), pltpu.SemaphoreType.DMA(())],
-        input_output_aliases={len(arrays): 0} if extra else {},
+        in_specs=[VMEM] * len(held) + [ANY] * len(extra),
+        out_specs=out_specs,
+        scratch_shapes=([here] if is_last else []) + [pltpu.SemaphoreType.DMA((2,))],
+        input_output_aliases={len(held): 0} if extra else {},
         compiler_params=pltpu.CompilerParams(vmem_limit_bytes=SCRATCH_BYTES),
-    )(*near_core(arrays), *extra)
+    )(*near_core(held), *extra)
+    if is_last:
+        return results[0], None, None, None
+    return (None, *results) if earlier is None else tuple(results)
 
 
 def load_kernel(keys, place, mask, front, own, rows, own_here, arrived):
@@ -454,7 +474,7 @@
     leaf_basis, state, send = first_merge(
         (own_a, own_b, other_a, other_b, own_w, other_w), pieces(2)
     )
-    buffer = None
+    buffer = earlier = None
     for level, (axis, bit) in list(enumerate(bits, start=1))[1:]:
         near = [swap(send, axis, bit)]
         if pieces(level) > 1:
@@ -462,15 +482,14 @@
         far = []
         for x in near:
             far.append(swap(x, "col", 0))
-        buffer, *rest = upper_merge(
+        buffer, earlier, state, send = upper_merge(
             level,
             levels,
             (state, own_p[level], other_p[level], *near, *far),
+            earlier,
             buffer,
             pieces(level + 1),
         )
-        if rest:
-            state, send = rest
     return (leaf_basis, buffer)
 
 

time: 139 us -> 137 us (0.986)
  Pallas kernels: 45.6 us -> 43.5 us
    pallas_call x4, Pallas kernels: 33.7 us -> 31.6 us  [upper_merge(): pl.pallas_call(functools.partial(upper_kernel, level, is_last, earlier is...]
where the time goes in v7:
time: 137 us
  waiting for transfers between devices  61.8 us (45%)
  Pallas kernels  43.5 us (32%)
  starting transfers between devices  29.9 us (22%)
    ppermute x27, waiting for transfers between devices, swap(): lax.ppermute(x, axis, [(i, i ^ 1 << bit) for i in range(lax.axis_size(axi...  61.8 us
    pallas_call x4, Pallas kernels, upper_merge(): pl.pallas_call(functools.partial(upper_kernel, level, is_last, earlier is...  31.6 us
    ppermute x27, starting transfers between devices, swap(): lax.ppermute(x, axis, [(i, i ^ 1 << bit) for i in range(lax.axis_size(axi...  29.1 us
    pallas_call x1, Pallas kernels, first_merge(): pl.pallas_call(first_kernel, out_shape=[jax.ShapeDtypeStruct((rows, size)...  7.89 us
    pallas_call x1, Pallas kernels, load_front(): pl.pallas_call(functools.partial(load_kernel, keys), out_shape=[form((slo...  2.76 us
  transfers between devices with their start and end apart: 28, of which 15 were waited for; matrix products, arithmetic and copies ran while one was open for 0% of the time, Pallas kernels for 8%

profile of v7, /device:TPU:0, one launch (start us, length us, event | category | flops | bytes accessed | tf_op | source)
XLA Modules:
  0.0 137.2 jit_solution(9688937633200845136)
XLA Ops:
  0.6 4.1 %collective-permute-start.1 = (bf16[256,256]{1,0:T(8,128)(2,1)}, bf16[256,256]{1,0:T(8,128)(2,1)S(1)}, u32[]{:S(2)}, u32[]{:S(2)}) collective-permute-start(bf16[256,256]{1,0:T(8,128)(2,1)} %own.1), channel_id=1, source_target_pairs={{0,16},{4,20},{8,24},{12,28},{16,0},{20,4},{24,8},{28,12},{1,17},{... | collective-permute-start | bytes 393224 | tf_op jit(solution)/shard_map/ppermute | solution.py:426
  4.8 1.6 %collective-permute-start.3 = (bf16[256,256]{1,0:T(8,128)(2,1)}, bf16[256,256]{1,0:T(8,128)(2,1)S(1)}, u32[]{:S(2)}, u32[]{:S(2)}) collective-permute-start(bf16[256,256]{1,0:T(8,128)(2,1)} %own.1), channel_id=1, source_target_pairs={{0,8},{4,12},{8,0},{12,4},{16,24},{20,28},{24,16},{28,20},{1,9},{5... | collective-permute-start | bytes 393224 | tf_op jit(solution)/shard_map/ppermute | solution.py:426
  6.3 5.0 %collective-permute-done.1.refs_2_ = bf16[256,256]{1,0:T(8,128)(2,1)S(1)} collective-permute-done((bf16[256,256]{1,0:T(8,128)(2,1)}, bf16[256,256]{1,0:T(8,128)(2,1)S(1)}, u32[]{:S(2)}, u32[]{:S(2)}) %collective-permute-start.1) | collective-permute-done | bytes 131104 | tf_op jit(solution)/shard_map/ppermute | solution.py:426
  11.4 1.6 %collective-permute-start.2 = (bf16[256,256]{1,0:T(8,128)(2,1)S(1)}, bf16[256,256]{1,0:T(8,128)(2,1)S(1)}, u32[]{:S(2)}, u32[]{:S(2)}) collective-permute-start(bf16[256,256]{1,0:T(8,128)(2,1)S(1)} %collective-permute-done.1.refs_2_), channel_id=1, source_target_pairs={{0,4},{4,0},{8,12},{12,8},{16,20},{20,16},{24,28},{28,24},{1,5},{5... | collective-permute-start | bytes 393224 | tf_op jit(solution)/shard_map/ppermute | solution.py:426
  12.9 0.5 collective-permute-start
  13.4 0.7 collective-permute-start.5
  14.1 1.5 %collective-permute-start.4 = (bf16[256,256]{1,0:T(8,128)(2,1)S(1)}, bf16[256,256]{1,0:T(8,128)(2,1)S(1)}, u32[]{:S(2)}, u32[]{:S(2)}) collective-permute-start(bf16[256,256]{1,0:T(8,128)(2,1)S(1)} %collective-permute-done.3.refs_4_), channel_id=1, source_target_pairs={{0,4},{4,0},{8,12},{12,8},{16,20},{20,16},{24,28},{28,24},{1,5},{5... | collective-permute-start | bytes 393224 | tf_op jit(solution)/shard_map/ppermute | solution.py:426
  15.7 2.1 %collective-permute-done.2.refs_3_ = bf16[256,256]{1,0:T(8,128)(2,1)S(1)} collective-permute-done((bf16[256,256]{1,0:T(8,128)(2,1)S(1)}, bf16[256,256]{1,0:T(8,128)(2,1)S(1)}, u32[]{:S(2)}, u32[]{:S(2)}) %collective-permute-start.2) | collective-permute-done | bytes 131104 | tf_op jit(solution)/shard_map/ppermute | solution.py:426
  17.8 0.7 collective-permute-start.6
  18.5 0.1 pad_add_fusion.place
  18.5 0.7 copy-done
  19.2 2.8 %load_front.1 = (bf16[4,256,2048]{2,1,0:T(8,128)(2,1)S(1)}, bf16[256,256]{1,0:T(8,128)(2,1)S(1)}) custom-call(s32[2]{0:T(128)S(1)} %pad_add_fusion.place, s32[4,8]{1,0:T(4,128)S(1)} %copy-done, bf16[1024,2048]{1,0:T(8,128)(2,1)} %front.1, bf16[256,256]{1,0:T(8,128)(2,1)} %own.1), custom_call_target="tpu_custom_call" | custom-call | tf_op jit(solution)/shard_map/load_front/pallas_call | solution.py:384
  22.0 0.0 copy-start.2
  22.1 0.7 collective-permute-done.6.refs_7_
  22.7 1.2 samples.1
  24.0 0.1 collective-permute-start.7
  24.0 1.9 %collective-permute-done.7 = f32[2,256,256]{2,1,0:T(8,128)S(1)} collective-permute-done((f32[2,256,256]{2,1,0:T(8,128)S(1)}, f32[2,256,256]{2,1,0:T(8,128)S(1)}, u32[]{:S(2)}, u32[]{:S(2)}) %collective-permute-start.7) | collective-permute-done | bytes 524320 | tf_op jit(solution)/shard_map/ppermute | solution.py:426
  25.9 0.1 slice_add_fusion
  26.0 1.3 collective-permute-start.8
  27.4 0.8 collective-permute-start.11
  28.2 2.3 %collective-permute-start.9 = (f32[256,256]{1,0:T(8,128)S(1)}, f32[256,256]{1,0:T(8,128)S(1)}, u32[]{:S(2)}, u32[]{:S(2)}) collective-permute-start(f32[256,256]{1,0:T(8,128)S(1)} %get-tuple-element.39.own_a), channel_id=1, source_target_pairs={{0,1},{1,0},{2,3},{3,2},{4,5},{5,4},{6,7},{7,6},{8,9},{9,8},{10,11... | collective-permute-start | bytes 786440 | tf_op jit(solution)/shard_map/ppermute | solution.py:426
  30.6 4.1 %collective-permute-done.8 = f32[1,256,256]{2,1,0:T(8,128)S(1)} collective-permute-done((f32[1,256,256]{2,1,0:T(8,128)S(1)}, f32[1,256,256]{2,1,0:T(8,128)S(1)}, u32[]{:S(2)}, u32[]{:S(2)}) %collective-permute-start.8) | collective-permute-done | bytes 262176 | tf_op jit(solution)/shard_map/ppermute | solution.py:426
  34.7 0.5 collective-permute-start.12
  35.2 0.1 collective-permute-start.13
  35.3 1.1 collective-permute-done.12.other_w
  36.4 7.9 %first_merge.1 = (f32[256,256]{1,0:T(8,128)}, f32[2,224,256]{2,1,0:T(8,128)S(1)}, f32[224,256]{1,0:T(8,128)S(1)}) custom-call(f32[256,256]{1,0:T(8,128)S(1)} %get-tuple-element.39.own_a, f32[256,256]{1,0:T(8,128)S(1)} %bitcast.6, f32[256,256]{1,0:T(8,128)S(1)} %collective-permute-done.9.other_a, f32[256,256]{1,0:T(8,128)S(1)} %collective-permute-done.10.other_b, ...), custom_call_target="tpu_custom_call" | custom-call | tf_op jit(solution)/shard_map/first_merge/pallas_call | solution.py:300
  44.3 2.6 %collective-permute-start.15 = (f32[224,256]{1,0:T(8,128)S(1)}, f32[224,256]{1,0:T(8,128)S(1)}, u32[]{:S(2)}, u32[]{:S(2)}) collective-permute-start(f32[224,256]{1,0:T(8,128)S(1)} %get-tuple-element.26), channel_id=1, source_target_pairs={{0,2},{1,3},{2,0},{3,1},{4,6},{5,7},{6,4},{7,5},{8,10},{9,11},{10,... | collective-permute-start | bytes 688136 | tf_op jit(solution)/shard_map/ppermute | solution.py:426
  46.9 0.1 collective-permute-start.14
  47.0 6.3 %collective-permute-done.15.refs_0_ = f32[224,256]{1,0:T(8,128)S(1)} collective-permute-done((f32[224,256]{1,0:T(8,128)S(1)}, f32[224,256]{1,0:T(8,128)S(1)}, u32[]{:S(2)}, u32[]{:S(2)}) %collective-permute-start.15) | collective-permute-done | bytes 229408 | tf_op jit(solution)/shard_map/ppermute | solution.py:426
  53.3 5.1 %collective-permute-done.14.other_p = f32[256,256]{1,0:T(8,128)S(1)} collective-permute-done((f32[256,256]{1,0:T(8,128)S(1)}, f32[256,256]{1,0:T(8,128)S(1)}, u32[]{:S(2)}, u32[]{:S(2)}) %collective-permute-start.14) | collective-permute-done | bytes 262176 | tf_op jit(solution)/shard_map/ppermute | solution.py:426
  58.4 7.6 %shard_map.59 = (f32[256,256]{1,0:T(8,128)S(1)}, f32[2,224,256]{2,1,0:T(8,128)S(1)}, f32[224,256]{1,0:T(8,128)S(1)}) custom-call(f32[2,224,256]{2,1,0:T(8,128)S(1)} %get-tuple-element.25.own, f32[256,256]{1,0:T(8,128)S(1)} %add.24.own_p, f32[256,256]{1,0:T(8,128)S(1)} %collective-permute-done.14.other_p, f32[224,256]{1,0:T(8,128)S(1)} %collective-permute-done.15.refs_0_, ...), custom_call_target="tpu_custom_call" | custom-call | tf_op jit(solution)/shard_map/pallas_call | solution.py:324
  66.0 4.8 %collective-permute-start.18 = (f32[224,256]{1,0:T(8,128)S(1)}, f32[224,256]{1,0:T(8,128)S(1)}, u32[]{:S(2)}, u32[]{:S(2)}) collective-permute-start(f32[224,256]{1,0:T(8,128)S(1)} %get-tuple-element.28), channel_id=1, source_target_pairs={{0,4},{4,0},{8,12},{12,8},{16,20},{20,16},{24,28},{28,24},{1,5},{5... | collective-permute-start | bytes 688136 | tf_op jit(solution)/shard_map/ppermute | solution.py:426
  70.9 0.1 collective-permute-start.17
  71.0 6.3 %collective-permute-done.18.refs_0_ = f32[224,256]{1,0:T(8,128)S(1)} collective-permute-done((f32[224,256]{1,0:T(8,128)S(1)}, f32[224,256]{1,0:T(8,128)S(1)}, u32[]{:S(2)}, u32[]{:S(2)}) %collective-permute-start.18) | collective-permute-done | bytes 229408 | tf_op jit(solution)/shard_map/ppermute | solution.py:426
  77.3 4.2 %collective-permute-done.17.other_p = f32[256,256]{1,0:T(8,128)S(1)} collective-permute-done((f32[256,256]{1,0:T(8,128)S(1)}, f32[256,256]{1,0:T(8,128)S(1)}, u32[]{:S(2)}, u32[]{:S(2)}) %collective-permute-start.17) | collective-permute-done | bytes 262176 | tf_op jit(solution)/shard_map/ppermute | solution.py:426
  81.6 7.8 %shard_map.60 = (f32[4,256,256]{2,1,0:T(8,128)}, f32[256,256]{1,0:T(8,128)S(1)}, f32[2,224,256]{2,1,0:T(8,128)S(1)}, f32[224,256]{1,0:T(8,128)S(1)}) custom-call(f32[2,224,256]{2,1,0:T(8,128)S(1)} %get-tuple-element.27.own, f32[256,256]{1,0:T(8,128)S(1)} %add.25.own_p, f32[256,256]{1,0:T(8,128)S(1)} %collective-permute-done.17.other_p, ...), custom_call_target="tpu_custom_call" | custom-call | tf_op jit(solution)/shard_map/pallas_call | solution.py:324
  89.4 0.1 collective-permute-start.21
  89.5 2.1 %collective-permute-start.20 = (f32[256,256]{1,0:T(8,128)S(1)}, f32[256,256]{1,0:T(8,128)S(1)}, u32[]{:S(2)}, u32[]{:S(2)}) collective-permute-start(f32[256,256]{1,0:T(8,128)S(1)} %add.26.own_p), channel_id=1, source_target_pairs={{0,8},{4,12},{8,0},{12,4},{16,24},{20,28},{24,16},{28,20},{1,9},{5... | collective-permute-start | bytes 786440 | tf_op jit(solution)/shard_map/ppermute | solution.py:426
  91.6 6.3 %collective-permute-done.21.refs_0_ = f32[224,256]{1,0:T(8,128)S(1)} collective-permute-done((f32[224,256]{1,0:T(8,128)S(1)}, f32[224,256]{1,0:T(8,128)S(1)}, u32[]{:S(2)}, u32[]{:S(2)}) %collective-permute-start.21) | collective-permute-done | bytes 229408 | tf_op jit(solution)/shard_map/ppermute | solution.py:426
  98.0 3.4 %collective-permute-done.20.other_p = f32[256,256]{1,0:T(8,128)S(1)} collective-permute-done((f32[256,256]{1,0:T(8,128)S(1)}, f32[256,256]{1,0:T(8,128)S(1)}, u32[]{:S(2)}, u32[]{:S(2)}) %collective-permute-start.20) | collective-permute-done | bytes 262176 | tf_op jit(solution)/shard_map/ppermute | solution.py:426
  101.4 7.6 %shard_map.61 = (f32[4,256,256]{2,1,0:T(8,128)}, f32[256,256]{1,0:T(8,128)S(1)}, f32[2,224,256]{2,1,0:T(8,128)S(1)}, f32[112,256]{1,0:T(8,128)S(1)}) custom-call(f32[2,224,256]{2,1,0:T(8,128)S(1)} %get-tuple-element.30.own, f32[256,256]{1,0:T(8,128)S(1)} %add.26.own_p, ...), custom_call_target="tpu_custom_call", output_to_operand_aliasing={{0}: (6, {})} | custom-call | tf_op jit(solution)/shard_map/pallas_call | solution.py:324
  109.0 1.0 collective-permute-start.24
  110.0 2.0 %collective-permute-start.23 = (f32[256,256]{1,0:T(8,128)S(1)}, f32[256,256]{1,0:T(8,128)S(1)}, u32[]{:S(2)}, u32[]{:S(2)}) collective-permute-start(f32[256,256]{1,0:T(8,128)S(1)} %add.27.own_p), channel_id=1, source_target_pairs={{0,16},{4,20},{8,24},{12,28},{16,0},{20,4},{24,8},{28,12},{1,17},{... | collective-permute-start | bytes 786440 | tf_op jit(solution)/shard_map/ppermute | solution.py:426
  112.1 10.3 %collective-permute-done.24.refs_0_ = f32[112,256]{1,0:T(8,128)S(1)} collective-permute-done((f32[112,256]{1,0:T(8,128)S(1)}, f32[112,256]{1,0:T(8,128)S(1)}, u32[]{:S(2)}, u32[]{:S(2)}) %collective-permute-start.24) | collective-permute-done | bytes 114720 | tf_op jit(solution)/shard_map/ppermute | solution.py:426
  122.3 1.3 collective-permute-start.25
  123.6 3.5 %collective-permute-done.25.refs_1_ = f32[112,256]{1,0:T(8,128)S(1)} collective-permute-done((f32[112,256]{1,0:T(8,128)S(1)}, f32[112,256]{1,0:T(8,128)S(1)}, u32[]{:S(2)}, u32[]{:S(2)}) %collective-permute-start.25) | collective-permute-done | bytes 114720 | tf_op jit(solution)/shard_map/ppermute | solution.py:426
  127.1 1.3 collective-permute-done.27.refs_3_
  128.5 8.6 %shard_map.62 = f32[4,256,256]{2,1,0:T(8,128)} custom-call(f32[2,224,256]{2,1,0:T(8,128)S(1)} %get-tuple-element.34.own, f32[256,256]{1,0:T(8,128)S(1)} %add.27.own_p, f32[256,256]{1,0:T(8,128)S(1)} %collective-permute-done.23.other_p, f32[112,256]{1,0:T(8,128)S(1)} %collective-permute-done.24.refs_0_, ...), custom_call_target="tpu_custom_call", output_to_operand_aliasing={{}: (8, {})} | custom-call | tf_op jit(solution)/shard_map/pallas_call | solution.py:324
  (27 shorter events, 0.2 us)
Async XLA Ops:
  0.6 10.8 %collective-permute-start.1 = (bf16[256,256]{1,0:T(8,128)(2,1)}, bf16[256,256]{1,0:T(8,128)(2,1)S(1)}, u32[]{:S(2)}, u32[]{:S(2)}) collective-permute-start(bf16[256,256]{1,0:T(8,128)(2,1)} %own.1), channel_id=1, source_target_pairs={{0,16},{4,20},{8,24},{12,28},{16,0},{20,4},{24,8},{28,12},{1,17},{... | collective-permute-start | bytes 393224 | tf_op jit(solution)/shard_map/ppermute | solution.py:426
  4.8 9.4 %collective-permute-start.3 = (bf16[256,256]{1,0:T(8,128)(2,1)}, bf16[256,256]{1,0:T(8,128)(2,1)S(1)}, u32[]{:S(2)}, u32[]{:S(2)}) collective-permute-start(bf16[256,256]{1,0:T(8,128)(2,1)} %own.1), channel_id=1, source_target_pairs={{0,8},{4,12},{8,0},{12,4},{16,24},{20,28},{24,16},{28,20},{1,9},{5... | collective-permute-start | bytes 393224 | tf_op jit(solution)/shard_map/ppermute | solution.py:426
  11.4 6.4 %collective-permute-start.2 = (bf16[256,256]{1,0:T(8,128)(2,1)S(1)}, bf16[256,256]{1,0:T(8,128)(2,1)S(1)}, u32[]{:S(2)}, u32[]{:S(2)}) collective-permute-start(bf16[256,256]{1,0:T(8,128)(2,1)S(1)} %collective-permute-done.1.refs_2_), channel_id=1, source_target_pairs={{0,4},{4,0},{8,12},{12,8},{16,20},{20,16},{24,28},{28,24},{1,5},{5... | collective-permute-start | bytes 393224 | tf_op jit(solution)/shard_map/ppermute | solution.py:426
  12.9 9.1 %collective-permute-start = (bf16[256,256]{1,0:T(8,128)(2,1)}, bf16[256,256]{1,0:T(8,128)(2,1)S(1)}, u32[]{:S(2)}, u32[]{:S(2)}) collective-permute-start(bf16[256,256]{1,0:T(8,128)(2,1)} %own.1), channel_id=1, source_target_pairs={{0,4},{4,0},{8,12},{12,8},{16,20},{20,16},{24,28},{28,24},{1,5},{5... | collective-permute-start | bytes 393224 | tf_op jit(solution)/shard_map/ppermute | solution.py:426
  13.4 8.6 %collective-permute-start.5 = (bf16[256,256]{1,0:T(8,128)(2,1)S(1)}, bf16[256,256]{1,0:T(8,128)(2,1)S(1)}, u32[]{:S(2)}, u32[]{:S(2)}) collective-permute-start(bf16[256,256]{1,0:T(8,128)(2,1)S(1)} %collective-permute-done.1.refs_2_), channel_id=1, source_target_pairs={{0,8},{4,12},{8,0},{12,4},{16,24},{20,28},{24,16},{28,20},{1,9},{5... | collective-permute-start | bytes 393224 | tf_op jit(solution)/shard_map/ppermute | solution.py:426
  14.1 7.9 %collective-permute-start.4 = (bf16[256,256]{1,0:T(8,128)(2,1)S(1)}, bf16[256,256]{1,0:T(8,128)(2,1)S(1)}, u32[]{:S(2)}, u32[]{:S(2)}) collective-permute-start(bf16[256,256]{1,0:T(8,128)(2,1)S(1)} %collective-permute-done.3.refs_4_), channel_id=1, source_target_pairs={{0,4},{4,0},{8,12},{12,8},{16,20},{20,16},{24,28},{28,24},{1,5},{5... | collective-permute-start | bytes 393224 | tf_op jit(solution)/shard_map/ppermute | solution.py:426
  17.8 5.0 %collective-permute-start.6 = (bf16[256,256]{1,0:T(8,128)(2,1)S(1)}, bf16[256,256]{1,0:T(8,128)(2,1)S(1)}, u32[]{:S(2)}, u32[]{:S(2)}) collective-permute-start(bf16[256,256]{1,0:T(8,128)(2,1)S(1)} %collective-permute-done.2.refs_3_), channel_id=1, source_target_pairs={{0,8},{4,12},{8,0},{12,4},{16,24},{20,28},{24,16},{28,20},{1,9},{5... | collective-permute-start | bytes 393224 | tf_op jit(solution)/shard_map/ppermute | solution.py:426
  18.5 0.7 copy-start
  22.0 5.4 %copy-start.2 = (bf16[256,256]{1,0:T(8,128)(2,1)S(1)}, bf16[256,256]{1,0:T(8,128)(2,1)}, u32[]{:S(2)}) copy-start(bf16[256,256]{1,0:T(8,128)(2,1)} %own.1) | copy-start | bytes 393220
  22.0 13.2 %copy-start.1 = (f32[256,256]{1,0:T(8,128)S(1)}, f32[256,256]{1,0:T(8,128)}, u32[]{:S(2)}) copy-start(f32[256,256]{1,0:T(8,128)} %param.7) | copy-start | bytes 786436
  24.0 2.0 %collective-permute-start.7 = (f32[2,256,256]{2,1,0:T(8,128)S(1)}, f32[2,256,256]{2,1,0:T(8,128)S(1)}, u32[]{:S(2)}, u32[]{:S(2)}) collective-permute-start(f32[2,256,256]{2,1,0:T(8,128)S(1)} %get-tuple-element.23), channel_id=1, source_target_pairs={{0,1},{1,0},{2,3},{3,2},{4,5},{5,4},{6,7},{7,6},{8,9},{9,8},{10,11... | collective-permute-start | bytes 1572872 | tf_op jit(solution)/shard_map/ppermute | solution.py:426
  26.0 8.7 %collective-permute-start.8 = (f32[1,256,256]{2,1,0:T(8,128)S(1)}, f32[1,256,256]{2,1,0:T(8,128)S(1)}, u32[]{:S(2)}, u32[]{:S(2)}) collective-permute-start(f32[1,256,256]{2,1,0:T(8,128)S(1)} %get-tuple-element.38), channel_id=1, source_target_pairs={{0,2},{1,3},{2,0},{3,1},{4,6},{5,7},{6,4},{7,5},{8,10},{9,11},{10,... | collective-permute-start | bytes 786440 | tf_op jit(solution)/shard_map/ppermute | solution.py:426
  27.4 7.3 %collective-permute-start.11 = (bf16[256,256]{1,0:T(8,128)(2,1)S(1)}, bf16[256,256]{1,0:T(8,128)(2,1)S(1)}, u32[]{:S(2)}, u32[]{:S(2)}) collective-permute-start(bf16[256,256]{1,0:T(8,128)(2,1)S(1)} %copy-done.2), channel_id=1, source_target_pairs={{0,0},{4,1},{8,2},{12,3},{16,4},{20,5},{24,6},{28,7},{1,8},{5,9},{... | collective-permute-start | bytes 393224 | tf_op jit(solution)/shard_map/ppermute | solution.py:448
  28.2 8.2 %collective-permute-start.9 = (f32[256,256]{1,0:T(8,128)S(1)}, f32[256,256]{1,0:T(8,128)S(1)}, u32[]{:S(2)}, u32[]{:S(2)}) collective-permute-start(f32[256,256]{1,0:T(8,128)S(1)} %get-tuple-element.39.own_a), channel_id=1, source_target_pairs={{0,1},{1,0},{2,3},{3,2},{4,5},{5,4},{6,7},{7,6},{8,9},{9,8},{10,11... | collective-permute-start | bytes 786440 | tf_op jit(solution)/shard_map/ppermute | solution.py:426
  34.7 1.7 %collective-permute-start.10 = (f32[256,256]{1,0:T(8,128)S(1)}, f32[256,256]{1,0:T(8,128)S(1)}, u32[]{:S(2)}, u32[]{:S(2)}) collective-permute-start(f32[256,256]{1,0:T(8,128)S(1)} %bitcast.5), channel_id=1, source_target_pairs={{0,1},{1,0},{2,3},{3,2},{4,5},{5,4},{6,7},{7,6},{8,9},{9,8},{10,11... | collective-permute-start | bytes 786440 | tf_op jit(solution)/shard_map/ppermute | solution.py:426
  34.7 1.7 %collective-permute-start.12 = (bf16[256,256]{1,0:T(8,128)(2,1)S(1)}, bf16[256,256]{1,0:T(8,128)(2,1)S(1)}, u32[]{:S(2)}, u32[]{:S(2)}) collective-permute-start(bf16[256,256]{1,0:T(8,128)(2,1)S(1)} %collective-permute-done.11.own_w), channel_id=1, source_target_pairs={{0,1},{1,0},{2,3},{3,2},{4,5},{5,4},{6,7},{7,6},{8,9},{9,8},{10,11... | collective-permute-start | bytes 393224 | tf_op jit(solution)/shard_map/ppermute | solution.py:426
  35.2 11.7 %collective-permute-start.13 = (f32[256,256]{1,0:T(8,128)S(1)}, f32[256,256]{1,0:T(8,128)S(1)}, u32[]{:S(2)}, u32[]{:S(2)}) collective-permute-start(f32[256,256]{1,0:T(8,128)S(1)} %copy-done.1), channel_id=1, source_target_pairs={{0,1},{1,0},{2,3},{3,2},{4,5},{5,4},{6,7},{7,6},{8,9},{9,8},{10,11... | collective-permute-start | bytes 786440 | tf_op jit(solution)/shard_map/ppermute | solution.py:426
  44.3 9.0 %collective-permute-start.15 = (f32[224,256]{1,0:T(8,128)S(1)}, f32[224,256]{1,0:T(8,128)S(1)}, u32[]{:S(2)}, u32[]{:S(2)}) collective-permute-start(f32[224,256]{1,0:T(8,128)S(1)} %get-tuple-element.26), channel_id=1, source_target_pairs={{0,2},{1,3},{2,0},{3,1},{4,6},{5,7},{6,4},{7,5},{8,10},{9,11},{10,... | collective-permute-start | bytes 688136 | tf_op jit(solution)/shard_map/ppermute | solution.py:426
  46.9 11.5 %collective-permute-start.14 = (f32[256,256]{1,0:T(8,128)S(1)}, f32[256,256]{1,0:T(8,128)S(1)}, u32[]{:S(2)}, u32[]{:S(2)}) collective-permute-start(f32[256,256]{1,0:T(8,128)S(1)} %add.24.own_p), channel_id=1, source_target_pairs={{0,2},{1,3},{2,0},{3,1},{4,6},{5,7},{6,4},{7,5},{8,10},{9,11},{10,... | collective-permute-start | bytes 786440 | tf_op jit(solution)/shard_map/ppermute | solution.py:426
  53.3 5.1 %collective-permute-start.16 = (f32[224,256]{1,0:T(8,128)S(1)}, f32[224,256]{1,0:T(8,128)S(1)}, u32[]{:S(2)}, u32[]{:S(2)}) collective-permute-start(f32[224,256]{1,0:T(8,128)S(1)} %collective-permute-done.15.refs_0_), channel_id=1, source_target_pairs={{0,1},{1,0},{2,3},{3,2},{4,5},{5,4},{6,7},{7,6},{8,9},{9,8},{10,11... | collective-permute-start | bytes 688136 | tf_op jit(solution)/shard_map/ppermute | solution.py:426
  66.0 11.3 %collective-permute-start.18 = (f32[224,256]{1,0:T(8,128)S(1)}, f32[224,256]{1,0:T(8,128)S(1)}, u32[]{:S(2)}, u32[]{:S(2)}) collective-permute-start(f32[224,256]{1,0:T(8,128)S(1)} %get-tuple-element.28), channel_id=1, source_target_pairs={{0,4},{4,0},{8,12},{12,8},{16,20},{20,16},{24,28},{28,24},{1,5},{5... | collective-permute-start | bytes 688136 | tf_op jit(solution)/shard_map/ppermute | solution.py:426
  70.9 10.7 %collective-permute-start.17 = (f32[256,256]{1,0:T(8,128)S(1)}, f32[256,256]{1,0:T(8,128)S(1)}, u32[]{:S(2)}, u32[]{:S(2)}) collective-permute-start(f32[256,256]{1,0:T(8,128)S(1)} %add.25.own_p), channel_id=1, source_target_pairs={{0,4},{4,0},{8,12},{12,8},{16,20},{20,16},{24,28},{28,24},{1,5},{5... | collective-permute-start | bytes 786440 | tf_op jit(solution)/shard_map/ppermute | solution.py:426
  77.3 4.2 %collective-permute-start.19 = (f32[224,256]{1,0:T(8,128)S(1)}, f32[224,256]{1,0:T(8,128)S(1)}, u32[]{:S(2)}, u32[]{:S(2)}) collective-permute-start(f32[224,256]{1,0:T(8,128)S(1)} %collective-permute-done.18.refs_0_), channel_id=1, source_target_pairs={{0,1},{1,0},{2,3},{3,2},{4,5},{5,4},{6,7},{7,6},{8,9},{9,8},{10,11... | collective-permute-start | bytes 688136 | tf_op jit(solution)/shard_map/ppermute | solution.py:426
  89.4 8.5 %collective-permute-start.21 = (f32[224,256]{1,0:T(8,128)S(1)}, f32[224,256]{1,0:T(8,128)S(1)}, u32[]{:S(2)}, u32[]{:S(2)}) collective-permute-start(f32[224,256]{1,0:T(8,128)S(1)} %get-tuple-element.31), channel_id=1, source_target_pairs={{0,8},{4,12},{8,0},{12,4},{16,24},{20,28},{24,16},{28,20},{1,9},{5... | collective-permute-start | bytes 688136 | tf_op jit(solution)/shard_map/ppermute | solution.py:426
  89.5 11.8 %collective-permute-start.20 = (f32[256,256]{1,0:T(8,128)S(1)}, f32[256,256]{1,0:T(8,128)S(1)}, u32[]{:S(2)}, u32[]{:S(2)}) collective-permute-start(f32[256,256]{1,0:T(8,128)S(1)} %add.26.own_p), channel_id=1, source_target_pairs={{0,8},{4,12},{8,0},{12,4},{16,24},{20,28},{24,16},{28,20},{1,9},{5... | collective-permute-start | bytes 786440 | tf_op jit(solution)/shard_map/ppermute | solution.py:426
  97.9 3.4 %collective-permute-start.22 = (f32[224,256]{1,0:T(8,128)S(1)}, f32[224,256]{1,0:T(8,128)S(1)}, u32[]{:S(2)}, u32[]{:S(2)}) collective-permute-start(f32[224,256]{1,0:T(8,128)S(1)} %collective-permute-done.21.refs_0_), channel_id=1, source_target_pairs={{0,1},{1,0},{2,3},{3,2},{4,5},{5,4},{6,7},{7,6},{8,9},{9,8},{10,11... | collective-permute-start | bytes 688136 | tf_op jit(solution)/shard_map/ppermute | solution.py:426
  109.0 13.4 %collective-permute-start.24 = (f32[112,256]{1,0:T(8,128)S(1)}, f32[112,256]{1,0:T(8,128)S(1)}, u32[]{:S(2)}, u32[]{:S(2)}) collective-permute-start(f32[112,256]{1,0:T(8,128)S(1)} %get-tuple-element.35), channel_id=1, source_target_pairs={{0,16},{4,20},{8,24},{12,28},{16,0},{20,4},{24,8},{28,12},{1,17},{... | collective-permute-start | bytes 344072 | tf_op jit(solution)/shard_map/ppermute | solution.py:426
  110.0 17.1 %collective-permute-start.23 = (f32[256,256]{1,0:T(8,128)S(1)}, f32[256,256]{1,0:T(8,128)S(1)}, u32[]{:S(2)}, u32[]{:S(2)}) collective-permute-start(f32[256,256]{1,0:T(8,128)S(1)} %add.27.own_p), channel_id=1, source_target_pairs={{0,16},{4,20},{8,24},{12,28},{16,0},{20,4},{24,8},{28,12},{1,17},{... | collective-permute-start | bytes 786440 | tf_op jit(solution)/shard_map/ppermute | solution.py:426
  122.3 4.8 %collective-permute-start.25 = (f32[112,256]{1,0:T(8,128)S(1)}, f32[112,256]{1,0:T(8,128)S(1)}, u32[]{:S(2)}, u32[]{:S(2)}) collective-permute-start(f32[112,256]{1,0:T(8,128)S(1)} %collective-permute-done.24.refs_0_), channel_id=1, source_target_pairs={{0,2},{1,3},{2,0},{3,1},{4,6},{5,7},{6,4},{7,5},{8,10},{9,11},{10,... | collective-permute-start | bytes 344072 | tf_op jit(solution)/shard_map/ppermute | solution.py:426
  123.6 3.5 %collective-permute-start.26 = (f32[112,256]{1,0:T(8,128)S(1)}, f32[112,256]{1,0:T(8,128)S(1)}, u32[]{:S(2)}, u32[]{:S(2)}) collective-permute-start(f32[112,256]{1,0:T(8,128)S(1)} %collective-permute-done.24.refs_0_), channel_id=1, source_target_pairs={{0,1},{1,0},{2,3},{3,2},{4,5},{5,4},{6,7},{7,6},{8,9},{9,8},{10,11... | collective-permute-start | bytes 344072 | tf_op jit(solution)/shard_map/ppermute | solution.py:426
  127.1 1.3 collective-permute-start.27
